TPU v7x, 32 devices: a whole 2x2x4 slice. The times are simulated.
32 devices in a mesh: grp: 2 (over y), queue: 4 (over z), tp: 2 (over x), seq: 2 (over core).
Axes of the slice: x: 2, y: 2, z: 4, core: 2. Of those that a mesh axis runs over, the one named last changes fastest.
Arguments:
- query_input: bfloat16 [8, 512, 1280], P(('grp', 'queue'), 'seq', 'tp'), parts along dimension 0, may hold values from -256 to 256
- key_input: bfloat16 [8, 512, 1280], P(('grp', 'queue'), 'seq', 'tp'), parts along dimension 0, may hold values from -256 to 256
- value_input: bfloat16 [8, 512, 1280], P(('grp', 'queue'), 'seq', 'tp'), parts along dimension 0, may hold values from -6 to 6
- query_gain: float32 [1280], P('tp'), may hold values from 0.1 to 1.9
- key_gain: float32 [1280], P('tp'), may hold values from 0.1 to 1.9
- gate_table: float32 [64, 1280], P(None, 'tp'), may hold values from -5 to 5
- levels: int32 [8], P(('grp', 'queue')), parts along dimension 0, may hold values from 0 to 63
Outputs:
- rolled: bfloat16 [8, 512, 1280], P(('grp', 'queue'), 'seq', 'tp'), parts along dimension 0
There are 2 independent parts, one for each index of `grp`. A program takes and returns all parts, laid end to end along the dimension named above; an argument that names none is the same for every part. Nothing has to cross between parts.
All inputs are finite; a program needn't handle non-finite values.
Results may differ from a plain program's by a relative error of at most 0.0015.
The roundings to bfloat16 on the way count: a program that leaves them out, or rounds other values in their place, can miss the bound.
Values may be sent and summed in bfloat16 or wider, within the bound.
No kernel may reach another device: no remote copies, remote signals or barrier semaphores. Data moves between devices by JAX's collectives and lax.ppermute only.
A program may use at most 64 MiB of HBM per device.

v0:
```python
import math

import jax
import jax.numpy as jnp
from jax import lax
from jax.sharding import PartitionSpec as P

DH = 128


epsilon = 1e-06


def shifted(value, axis, steps):
    count = lax.axis_size(axis)
    leading, last = (max(0, -steps), min(count, count - steps))
    return lax.ppermute(value, axis, [(source, source + steps) for source in range(leading, last)])


def from_behind(x, axis, by):
    peers = lax.axis_size(axis)
    return lax.ppermute(x, axis, [(i, (i + by) % peers) for i in range(peers)])


def neighbour_halves(paired):
    beside = []
    for offset in (1, -1):
        beside.append(shifted(paired, "queue", offset))
    return jnp.stack([beside[0], paired, beside[1]], axis=1)


def usable_keys(block_rows):
    position = lax.axis_index("queue")
    queue_size = lax.axis_size("queue")
    block_number = lax.broadcasted_iota(jnp.int32, (3 * block_rows,), 0) // block_rows
    return ((block_number != 0) | (position > 0)) & (
        (block_number != 2) | (position < queue_size - 1)
    )


def body(query_input, key_input, value_input, query_gain, key_gain, gate_table, levels):
    query_wide = query_input[0].astype(jnp.float32)
    key_wide = key_input[0].astype(jnp.float32)
    local_width = query_wide.shape[1]
    full_width = local_width * lax.axis_size("tp")
    query_square, key_square = lax.psum(
        (jnp.sum(query_wide * query_wide, axis=1), jnp.sum(key_wide * key_wide, axis=1)), "tp"
    )
    query_normed = (
        query_wide * lax.rsqrt(query_square / full_width + epsilon)[:, None] * query_gain
    ).astype(jnp.bfloat16)
    key_normed = (
        key_wide * lax.rsqrt(key_square / full_width + epsilon)[:, None] * key_gain
    ).astype(jnp.bfloat16)
    paired = jnp.stack([key_normed, value_input[0]])
    inverse_root = 1.0 / math.sqrt(DH)
    head_count = local_width // DH
    halves = neighbour_halves(paired)
    blocks = lax.all_gather(halves, "seq", axis=2, tiled=True)
    group_rows = blocks.shape[2]
    key_rows = blocks[0].reshape(3 * group_rows, local_width)
    value_rows = blocks[1].reshape(3 * group_rows, local_width)
    usable = usable_keys(group_rows)
    outputs = []
    for head_index in range(head_count):
        start = head_index * DH
        head_query = query_normed[:, start : start + DH]
        head_key = key_rows[:, start : start + DH]
        head_value = value_rows[:, start : start + DH]
        scores = (
            jnp.einsum("qd,kd->qk", head_query, head_key, preferred_element_type=jnp.float32)
            * inverse_root
        )
        scores = jnp.where(usable[None, :], scores, -1e30)
        row_max = jnp.max(scores, axis=-1, keepdims=True)
        weights = jnp.exp(scores - row_max)
        weight_sum = jnp.sum(weights, axis=-1, keepdims=True)
        summed = jnp.dot(
            weights.astype(jnp.bfloat16), head_value, preferred_element_type=jnp.float32
        )
        outputs.append(summed / weight_sum)
    attended = jnp.concatenate(outputs, axis=1)
    level_index = levels[0]
    gate_row = lax.dynamic_slice_in_dim(gate_table, level_index, 1, 0)
    gated = (gate_row * attended).astype(jnp.bfloat16)
    return from_behind(gated[None], "queue", -1)


def solution(mesh):
    in_specs = (
        P(("grp", "queue"), "seq", "tp"),
        P(("grp", "queue"), "seq", "tp"),
        P(("grp", "queue"), "seq", "tp"),
        P("tp"),
        P("tp"),
        P(None, "tp"),
        P(("grp", "queue")),
    )
    out_specs = P(("grp", "queue"), "seq", "tp")
    return jax.shard_map(body, mesh=mesh, in_specs=in_specs, out_specs=out_specs, check_vma=False)
```

profile of v0, /device:TPU:0, one launch (start us, length us, event | category | flops | bytes accessed | tf_op | source)
XLA Modules:
  0.0 81.2 jit_solution(9755903564621727770)
XLA Ops:
  6.5 0.0 copy-start
  6.5 0.0 all-gather.2.cloned.1.call-start
  6.5 1.2 %fusion.35 = f32[256]{0:T(256)S(1)} fusion(bf16[1,256,640]{2,1,0:T(8,128)(2,1)} %param.8), kind=kLoop, calls=%fused_computation.50 | loop fusion | flops 491264 | bytes 328704 | tf_op jit(solution)/shard_map/reduce_sum | solution.py:47
  7.7 1.1 %fusion.38 = f32[256]{0:T(256)S(1)} fusion(bf16[1,256,640]{2,1,0:T(8,128)(2,1)} %param.7), kind=kLoop, calls=%fused_computation.53 | loop fusion | flops 491264 | bytes 328704 | tf_op jit(solution)/shard_map/reduce_sum | solution.py:47
  8.8 5.9 %all-reduce = (f32[256]{0:T(256)S(1)}, f32[256]{0:T(256)S(1)}) all-reduce(f32[256]{0:T(256)S(1)} %fusion.35, f32[256]{0:T(256)S(1)} %fusion.38), channel_id=1, replica_groups=mesh['grp'=2,'queue'=4,'tp'=2,'seq'=2] {'tp'}, use_global_device_ids=true, to_apply=%region_3.0 | all-reduce | flops 512 | bytes 4096 | tf_op jit(solution)/shard_map/psum | solution.py:46
  14.7 1.1 %fusion.37 = bf16[1,256,640]{2,1,0:T(8,128)(2,1)S(1)} fusion(bf16[1,256,640]{2,1,0:T(8,128)(2,1)} %param.8, f32[640]{0:T(1024)} %param.11, f32[256]{0:T(256)S(1)} %add_rsqrt_fusion), kind=kLoop, calls=%fused_computation.52 | loop fusion | flops 655360 | bytes 658944 | tf_op jit(solution)/shard_map/convert_element_type | solution.py:54
  15.8 1.1 %fusion.64 = (bf16[2,1,256,640]{3,2,0,1:T(8,128)(2,1)S(1)}, bf16[2,256,640]{2,1,0:T(8,128)(2,1)S(1)}) fusion(bf16[1,256,640]{2,1,0:T(8,128)(2,1)} %param.9, bf16[1,256,640]{2,1,0:T(8,128)(2,1)S(1)} %fusion.37), kind=kLoop, calls=%fused_computation.88 | loop fusion | flops 327680 | bytes 1966080 | tf_op jit(solution)/shard_map/stack | solution.py:29
  16.9 4.1 %collective-permute-start = (bf16[2,256,640]{2,1,0:T(8,128)(2,1)S(1)}, bf16[2,256,640]{2,1,0:T(8,128)(2,1)S(1)}, u32[]{:S(2)}, u32[]{:S(2)}) collective-permute-start(bf16[2,256,640]{2,1,0:T(8,128)(2,1)S(1)} %get-tuple-element.10), channel_id=1, source_target_pairs={{0,4},{4,8},{8,12},{1,5},{5,9},{9,13},{2,6},{6,10},{10,14},{3,7},{... | collective-permute-start | bytes 1966088 | tf_op jit(solution)/shard_map/ppermute | solution.py:17
  21.0 1.3 %collective-permute-start.1 = (bf16[2,256,640]{2,1,0:T(8,128)(2,1)S(1)}, bf16[2,256,640]{2,1,0:T(8,128)(2,1)S(1)}, u32[]{:S(2)}, u32[]{:S(2)}) collective-permute-start(bf16[2,256,640]{2,1,0:T(8,128)(2,1)S(1)} %get-tuple-element.10), channel_id=1, source_target_pairs={{4,0},{8,4},{12,8},{5,1},{9,5},{13,9},{6,2},{10,6},{14,10},{7,3},{... | collective-permute-start | bytes 1966088 | tf_op jit(solution)/shard_map/ppermute | solution.py:17
  22.3 11.5 %collective-permute-done = bf16[2,256,640]{2,1,0:T(8,128)(2,1)S(1)} collective-permute-done((bf16[2,256,640]{2,1,0:T(8,128)(2,1)S(1)}, bf16[2,256,640]{2,1,0:T(8,128)(2,1)S(1)}, u32[]{:S(2)}, u32[]{:S(2)}) %collective-permute-start) | collective-permute-done | bytes 655392 | tf_op jit(solution)/shard_map/ppermute | solution.py:17
  33.7 4.2 %collective-permute-done.1 = bf16[2,256,640]{2,1,0:T(8,128)(2,1)S(1)} collective-permute-done((bf16[2,256,640]{2,1,0:T(8,128)(2,1)S(1)}, bf16[2,256,640]{2,1,0:T(8,128)(2,1)S(1)}, u32[]{:S(2)}, u32[]{:S(2)}) %collective-permute-start.1) | collective-permute-done | bytes 655392 | tf_op jit(solution)/shard_map/ppermute | solution.py:17
  37.9 1.5 %pad_maximum_fusion = bf16[2,3,256,640]{3,2,0,1:T(8,128)(2,1)} fusion(bf16[2,1,256,640]{3,2,0,1:T(8,128)(2,1)S(1)} %bitcast.45, bf16[2,1,256,640]{3,2,0,1:T(8,128)(2,1)S(1)} %get-tuple-element.9, bf16[2,1,256,640]{3,2,0,1:T(8,128)(2,1)S(1)} %bitcast.44), kind=kLoop, calls=%fused_computation.10 | loop fusion | flops 1966080 | bytes 3932160 | tf_op jit(solution)/shard_map/stack | solution.py:29
  39.4 0.0 copy-start.1
  39.4 0.0 copy-start.2
  39.4 0.0 all-gather.2.cloned.1.call-update
  40.2 0.0 copy-done
  40.2 0.2 copy-done.1
  40.4 0.0 copy-done.2
  40.4 0.1 fusion.40
  40.6 12.5 %all-gather.2.cloned.1.call-done = bf16[2,3,512,640]{3,2,0,1:T(8,128)(2,1)} async-done(((bf16[2,3,256,640]{3,2,0,1:T(8,128)(2,1)}), bf16[2,3,512,640]{3,2,0,1:T(8,128)(2,1)}) %all-gather.2.cloned.1.call-update) | async-done | bytes 3932176 | tf_op jit(solution)/shard_map/all_gather | solution.py:59
  53.1 2.5 %fusion.65 = (bf16[1,3,512,640]{3,2,0,1:T(8,128)(2,1)S(1)}, bf16[1,3,512,640]{3,2,0,1:T(8,128)(2,1)S(1)}) fusion(bf16[2,3,512,640]{3,2,0,1:T(8,128)(2,1)} %all-gather.2.cloned.1.call-done), kind=kLoop, calls=%fused_computation.89 | loop fusion | bytes 7864320 | tf_op jit(solution)/shard_map/slice | solution.py:62
  55.6 0.5 fusion.66
  56.0 0.5 fusion.67
  56.5 0.5 fusion.68
  57.0 0.5 fusion.69
  57.4 0.5 fusion.70
  57.9 0.4 fusion.5
  58.3 0.5 fusion.24
  58.8 0.4 fusion.7
  59.1 0.5 fusion.22
  59.6 0.4 fusion.9
  60.0 0.5 fusion.20
  60.5 0.4 fusion.11
  60.8 0.5 fusion.18
  61.3 0.4 fusion.13
  61.7 0.5 fusion.16
  62.2 0.2 multiply_convert_fusion
  62.4 3.6 %collective-permute-start.2 = (bf16[1,256,640]{1,2,0:T(8,128)(2,1)S(1)}, bf16[1,256,640]{1,2,0:T(8,128)(2,1)S(1)}, u32[]{:S(2)}, u32[]{:S(2)}) collective-permute-start(bf16[1,256,640]{1,2,0:T(8,128)(2,1)S(1)} %multiply_convert_fusion), channel_id=1, source_target_pairs={{0,12},{4,0},{8,4},{12,8},{1,13},{5,1},{9,5},{13,9},{2,14},{6,2},{... | collective-permute-start | bytes 983048 | tf_op jit(solution)/shard_map/ppermute | solution.py:22
  66.0 7.4 %collective-permute-done.2 = bf16[1,256,640]{1,2,0:T(8,128)(2,1)S(1)} collective-permute-done((bf16[1,256,640]{1,2,0:T(8,128)(2,1)S(1)}, bf16[1,256,640]{1,2,0:T(8,128)(2,1)S(1)}, u32[]{:S(2)}, u32[]{:S(2)}) %collective-permute-start.2) | collective-permute-done | bytes 327712 | tf_op jit(solution)/shard_map/ppermute | solution.py:22
  73.4 0.9 %copy.8 = bf16[1,256,640]{2,1,0:T(8,128)(2,1)} copy(bf16[1,256,640]{1,2,0:T(8,128)(2,1)S(1)} %collective-permute-done.2) | data formatting | bytes 655360 | tf_op jit(solution)/shard_map/ppermute | solution.py:22
  (4 shorter events, 0.0 us)
Async XLA Ops:
  6.5 33.6 %copy-start = (f32[64,640]{1,0:T(8,128)S(1)}, f32[64,640]{1,0:T(8,128)}, u32[]{:S(2)}) copy-start(f32[64,640]{1,0:T(8,128)} %param.12) | copy-start | bytes 491524
  6.5 46.6 %all-gather.2.cloned.1.call-start = ((), (), s32[]{:S(2)}) async-start(), calls=%async_computation | async-start | bytes 5898240 | tf_op jit(solution)/shard_map/all_gather | solution.py:59
  16.9 16.8 %collective-permute-start = (bf16[2,256,640]{2,1,0:T(8,128)(2,1)S(1)}, bf16[2,256,640]{2,1,0:T(8,128)(2,1)S(1)}, u32[]{:S(2)}, u32[]{:S(2)}) collective-permute-start(bf16[2,256,640]{2,1,0:T(8,128)(2,1)S(1)} %get-tuple-element.10), channel_id=1, source_target_pairs={{0,4},{4,8},{8,12},{1,5},{5,9},{9,13},{2,6},{6,10},{10,14},{3,7},{... | collective-permute-start | bytes 1966088 | tf_op jit(solution)/shard_map/ppermute | solution.py:17
  21.0 16.9 %collective-permute-start.1 = (bf16[2,256,640]{2,1,0:T(8,128)(2,1)S(1)}, bf16[2,256,640]{2,1,0:T(8,128)(2,1)S(1)}, u32[]{:S(2)}, u32[]{:S(2)}) collective-permute-start(bf16[2,256,640]{2,1,0:T(8,128)(2,1)S(1)} %get-tuple-element.10), channel_id=1, source_target_pairs={{4,0},{8,4},{12,8},{5,1},{9,5},{13,9},{6,2},{10,6},{14,10},{7,3},{... | collective-permute-start | bytes 1966088 | tf_op jit(solution)/shard_map/ppermute | solution.py:17
  39.4 1.0 %copy-start.1 = (bf16[1,256,640]{2,1,0:T(8,128)(2,1)S(1)}, bf16[1,256,640]{2,1,0:T(8,128)(2,1)}, u32[]{:S(2)}) copy-start(bf16[1,256,640]{2,1,0:T(8,128)(2,1)} %param.7) | copy-start | bytes 983044
  39.4 1.0 %copy-start.2 = (f32[640]{0:T(1024)S(1)}, f32[640]{0:T(1024)}, u32[]{:S(2)}) copy-start(f32[640]{0:T(1024)} %param.10) | copy-start | bytes 7684
  62.4 11.1 %collective-permute-start.2 = (bf16[1,256,640]{1,2,0:T(8,128)(2,1)S(1)}, bf16[1,256,640]{1,2,0:T(8,128)(2,1)S(1)}, u32[]{:S(2)}, u32[]{:S(2)}) collective-permute-start(bf16[1,256,640]{1,2,0:T(8,128)(2,1)S(1)} %multiply_convert_fusion), channel_id=1, source_target_pairs={{0,12},{4,0},{8,4},{12,8},{1,13},{5,1},{9,5},{13,9},{2,14},{6,2},{... | collective-permute-start | bytes 983048 | tf_op jit(solution)/shard_map/ppermute | solution.py:22
Sparse Core Ops, SparseCore 0:
  39.6 13.4 all-gather.1
where the time goes:
time: 81.5 us; the launch traced here: 81.2 us
  waiting for transfers between devices  35.6 us (44%)
  between operations  14.2 us (17%)
  starting transfers between devices  9 us (11%)
  other arithmetic  8.14 us (10%)
  blocking collectives  5.87 us (7%)
  matrix products  4.75 us (6%)
  local copies, waits for them, and re-layouts  3.59 us (4%)
    ppermute x2, waiting for transfers between devices, shifted(): lax.ppermute(value, axis, [(source, source + steps) for source in range(l...  15.6 us
    all_gather x1, waiting for transfers between devices, body(): blocks = lax.all_gather(halves, 'seq', axis=2, tiled=True)  12.5 us
    ppermute x1, waiting for transfers between devices, from_behind(): return lax.ppermute(x, axis, [(i, (i + by) % peers) for i in range(peers)])  7.43 us
    psum x1, blocking collectives, body(): lax.psum((jnp.sum(query_wide * query_wide, axis=1), jnp.sum(key_wide * ke...  5.87 us
    ppermute x2, starting transfers between devices, shifted(): lax.ppermute(value, axis, [(source, source + steps) for source in range(l...  5.35 us
    ppermute x1, starting transfers between devices, from_behind(): return lax.ppermute(x, axis, [(i, (i + by) % peers) for i in range(peers)])  3.65 us
    another operation x2, other arithmetic, neighbour_halves(): return jnp.stack([beside[0], paired, beside[1]], axis=1)  2.62 us
    slice x1, local copies, waits for them, and re-layouts, body(): value_rows = blocks[1].reshape(3 * group_rows, local_width)  2.48 us
  transfers between devices with their start and end apart: 4, of which 4 were waited for; matrix products, arithmetic and copies ran while one was open for 0% of the time, Pallas kernels for 0%

commit v1 on v0

v1 whole, which is shorter than its diff:
```python
import functools
import math

import jax
import jax.numpy as jnp
from jax import lax
from jax.experimental import pallas as pl
from jax.experimental.pallas import tpu as pltpu
from jax.sharding import PartitionSpec as P

DH = 128
EPSILON = 1e-06
SCALE = 1.0 / (math.sqrt(DH) * math.log(2.0))
CHUNK_SHARE = (3, 2)

LIMIT = 8 << 20
VMEM = pl.BlockSpec(memory_space=pltpu.VMEM)
SMEM = pl.BlockSpec(memory_space=pltpu.SMEM)


def chunk_widths(heads):
    first = (heads * CHUNK_SHARE[0]) // sum(CHUNK_SHARE)
    return [w * DH for w in (first, heads - first) if w > 0]


def row_square_sums(ref):
    rows, width = ref.shape
    total = None
    for start in range(0, width, DH):
        wide = ref[:, start : start + DH].astype(jnp.float32)
        total = wide * wide if total is None else total + wide * wide
    return jnp.sum(total.T, axis=0, keepdims=True)


def squares_kernel(query_ref, key_ref, out_ref):
    out_ref[0:1, :] = row_square_sums(query_ref)
    out_ref[1:2, :] = row_square_sums(key_ref)


def squares(query, key):
    rows = query.shape[0]
    return pl.pallas_call(
        squares_kernel,
        out_shape=jax.ShapeDtypeStruct((2, rows), jnp.float32),
        in_specs=[VMEM, VMEM],
        out_specs=VMEM,
        name="squares",
        compiler_params=pltpu.CompilerParams(vmem_limit_bytes=LIMIT),
    )(query, key)


def normalize_kernel(full_width, query_ref, key_ref, own_ref, other_ref, qgain_ref, kgain_ref, qout_ref, *kout_refs):
    rows = query_ref.shape[0]
    total = own_ref[...] + other_ref[...] if other_ref is not None else own_ref[...]
    factor = lax.rsqrt(total / full_width + EPSILON)
    spread = [jnp.broadcast_to(factor[i : i + 1, :], (DH, rows)).T for i in range(2)]
    at = 0
    for kout_ref in kout_refs:
        for start in range(0, kout_ref.shape[1], DH):
            wide = key_ref[:, at : at + DH].astype(jnp.float32)
            kout_ref[:, start : start + DH] = (wide * spread[1] * kgain_ref[:, at : at + DH]).astype(jnp.bfloat16)
            at += DH
    for start in range(0, query_ref.shape[1], DH):
        wide = query_ref[:, start : start + DH].astype(jnp.float32)
        qout_ref[:, start : start + DH] = (wide * spread[0] * qgain_ref[:, start : start + DH]).astype(jnp.bfloat16)


def normalize(query, key, own, other, query_gain, key_gain, full_width, widths):
    rows, width = query.shape
    return pl.pallas_call(
        functools.partial(normalize_kernel, full_width),
        out_shape=[jax.ShapeDtypeStruct((rows, w), jnp.bfloat16) for w in [width] + widths],
        in_specs=[VMEM] * 6,
        out_specs=[VMEM] * (1 + len(widths)),
        name="normalize",
        compiler_params=pltpu.CompilerParams(vmem_limit_bytes=LIMIT),
    )(query, key, own, other, query_gain[None], key_gain[None])


def attend(column, query_ref, key_refs, value_refs, gate, out_ref):
    for start in range(0, out_ref.shape[1], DH):
        here = slice(start, start + DH)
        there = slice(column + start, column + start + DH)
        head_query = query_ref[:, there]
        scores = [
            lax.dot_general(
                head_query, key_ref[:, here], (((1,), (1,)), ((), ())), preferred_element_type=jnp.float32
            )
            for key_ref in key_refs
        ]
        row_max = jnp.max(functools.reduce(jnp.maximum, scores), axis=1, keepdims=True)
        shift = row_max * SCALE
        weights = [jnp.exp2(part * SCALE - shift) for part in scores]
        weight_sum = jnp.sum(functools.reduce(jnp.add, weights), axis=1, keepdims=True)
        summed = functools.reduce(
            jnp.add,
            [
                jnp.dot(part.astype(jnp.bfloat16), value_ref[:, there], preferred_element_type=jnp.float32)
                for part, value_ref in zip(weights, value_refs)
            ],
        )
        out_ref[:, here] = (gate[:, there] * (summed / weight_sum)).astype(jnp.bfloat16)


def attention_kernel(column, scalars_ref, query_ref, gate_ref, *refs):
    keys, values, out_ref = refs[0:6], refs[6:12], refs[12]
    gate = gate_ref[pl.ds(scalars_ref[1], 1), :]

    @pl.when(scalars_ref[0] == 1)
    def _():
        attend(column, query_ref, keys, values, gate, out_ref)

    @pl.when(scalars_ref[0] == 0)
    def _():
        attend(column, query_ref, keys[:4], values[:4], gate, out_ref)


def attention(column, scalars, query, gate_table, keys, values):
    rows, width = query.shape[0], keys[0].shape[1]
    count = 6 * rows * width * rows
    return pl.pallas_call(
        functools.partial(attention_kernel, column),
        out_shape=jax.ShapeDtypeStruct((rows, width), jnp.bfloat16),
        in_specs=[SMEM] + [VMEM] * 14,
        out_specs=VMEM,
        name="attention",
        compiler_params=pltpu.CompilerParams(vmem_limit_bytes=LIMIT),
        cost_estimate=pl.CostEstimate(flops=4 * count, bytes_accessed=26 * rows * width, transcendentals=count // DH),
    )(scalars, query, gate_table, *keys, *values)


def body(query_input, key_input, value_input, query_gain, key_gain, gate_table, levels):
    places, seq, tp = (lax.axis_size(name) for name in ("queue", "seq", "tp"))
    rows, width = query_input.shape[1:]
    widths = chunk_widths(width // DH)
    first_pairs = [(i, i ^ 1) for i in range(places)]
    second_pairs = []
    for i in range(places):
        for s in range(seq):
            to = (i, 1 - s) if i in (0, places - 1) else (((i - 1) ^ 1) + 1, s)
            second_pairs.append((i * seq + s, to[0] * seq + to[1]))
    swap_pairs = [(s, 1 - s) for s in range(seq)]
    roll_pairs = [(i, (i - 1) % places) for i in range(places)]

    first = lambda x: lax.ppermute(x, "queue", first_pairs)
    second = lambda x: lax.ppermute(x, ("queue", "seq"), second_pairs)
    swap = lambda x: lax.ppermute(x, "seq", swap_pairs)

    query, key, value = query_input[0], key_input[0], value_input[0]
    value_first, value_second = first(value), second(value)
    own = squares(query, key)
    if tp == 2:
        other = lax.ppermute(own, "tp", [(0, 1), (1, 0)])
    else:
        own, other = lax.psum(own, "tp"), jnp.zeros_like(own)
    query_normed, *keys_normed = normalize(query, key, own, other, query_gain, key_gain, width * tp, widths)
    keys_first, keys_second = [], []
    for part in keys_normed:
        keys_first.append(first(part))
        keys_second.append(second(part))
    value_swapped = swap(value)
    keys_swapped = [swap(part) for part in keys_normed]
    values = [value, value_swapped, value_first, swap(value_first), value_second, swap(value_second)]

    place = lax.axis_index("queue")
    inner = (place > 0) & (place < places - 1)
    scalars = jnp.stack([inner.astype(jnp.int32), levels[0]])
    outputs, column = [], 0
    for i, part in enumerate(keys_normed):
        keys = [part, keys_swapped[i], keys_first[i], swap(keys_first[i]), keys_second[i], swap(keys_second[i])]
        gated = attention(column, scalars, query_normed, gate_table, keys, values)
        outputs.append(lax.ppermute(gated, "queue", roll_pairs))
        column += widths[i]
    return jnp.concatenate(outputs, axis=1)[None]


def solution(mesh):
    spec = P(("grp", "queue"), "seq", "tp")
    in_specs = (spec, spec, spec, P("tp"), P("tp"), P(None, "tp"), P(("grp", "queue")))
    return jax.shard_map(body, mesh=mesh, in_specs=in_specs, out_specs=spec, check_vma=False)
```

time: 81.5 us -> 40 us (0.49)
  waiting for transfers between devices: 35.6 us -> 8.02 us
  starting transfers between devices: 9 us -> 22.6 us
  between operations: 14.2 us -> 0.82 us
  other arithmetic: 8.14 us -> 0.83 us
  blocking collectives: 5.87 us -> 0 us
  Pallas kernels: 0 us -> 4.86 us
  matrix products: 4.75 us -> 0 us
  local copies, waits for them, and re-layouts: 3.59 us -> 2.69 us
    ppermute x3 -> x18, waiting for transfers between devices: 23.1 us -> 8.02 us  [the longest x2 3.8 us: body(): outputs.append(lax.ppermute(gated, 'queue', roll_pairs))]
    ppermute x3 -> x18, starting transfers between devices: 9 us -> 22.6 us  [the longest x3 12.6 us: body(): first = lambda x: lax.ppermute(x, 'queue', first_pairs)]
    all_gather x1 -> x0, waiting for transfers between devices: 12.5 us -> none  [body(): blocks = lax.all_gather(halves, 'seq', axis=2, tiled=True)]
    psum x1 -> x0, blocking collectives: 5.87 us -> none  [body(): lax.psum((jnp.sum(query_wide * query_wide, axis=1), jnp.sum(key_wide * ke...]
    pallas_call x0 -> x4, Pallas kernels: none -> 4.86 us  [the longest x2 4.41 us: attention(): pl.pallas_call(functools.partial(attention_kernel, column), out_shape=jax...]
    dot_general x10 -> x0, matrix products: 4.75 us -> none  [the longest x5 2.46 us: body(): jnp.dot(weights.astype(jnp.bfloat16), head_value, preferred_element_type=...]
    reduce_sum x7 -> x0, other arithmetic: 4.08 us -> none  [the longest x5 1.81 us: body(): weight_sum = jnp.sum(weights, axis=-1, keepdims=True)]
    another operation x2 -> x1, other arithmetic: 2.62 us -> 0.07 us  [body(): scalars = jnp.stack([inner.astype(jnp.int32), levels[0]])]
  transfers between devices with their start and end apart: 4 -> 18, of which waited for: 4 -> 5; matrix products, arithmetic and copies ran while one was open for 0% -> 2% of each run, Pallas kernels for 0% -> 12%
where the time goes in v1:
time: 40 us; the launch traced here: 39.8 us
  starting transfers between devices  22.6 us (56%)
  waiting for transfers between devices  8.02 us (20%)
  Pallas kernels  4.86 us (12%)
  local copies, waits for them, and re-layouts  2.69 us (7%)
  other arithmetic  0.83 us (2%)
  between operations  0.82 us (2%)
    ppermute x3, starting transfers between devices, body(): first = lambda x: lax.ppermute(x, 'queue', first_pairs)  12.6 us
    ppermute x2, starting transfers between devices, body(): outputs.append(lax.ppermute(gated, 'queue', roll_pairs))  5.19 us
    pallas_call x2, Pallas kernels, attention(): pl.pallas_call(functools.partial(attention_kernel, column), out_shape=jax...  4.41 us
    ppermute x2, waiting for transfers between devices, body(): outputs.append(lax.ppermute(gated, 'queue', roll_pairs))  3.8 us
    ppermute x3, waiting for transfers between devices, body(): first = lambda x: lax.ppermute(x, 'queue', first_pairs)  2.61 us
    ppermute x9, starting transfers between devices, body(): swap = lambda x: lax.ppermute(x, 'seq', swap_pairs)  2.21 us
    unnamed x26, local copies, waits for them, and re-layouts  2 us
    ppermute x1, starting transfers between devices, body(): other = lax.ppermute(own, 'tp', [(0, 1), (1, 0)])  1.56 us
  transfers between devices with their start and end apart: 18, of which 5 were waited for; matrix products, arithmetic and copies ran while one was open for 2% of the time, Pallas kernels for 12%

profile of v1, /device:TPU:0, one launch (start us, length us, event | category | flops | bytes accessed | tf_op | source)
XLA Modules:
  0.0 39.8 jit_solution(687981273099857583)
XLA Ops:
  0.0 0.5 %collective-permute-start.9 = (bf16[256,640]{1,0:T(8,128)(2,1)}, bf16[256,640]{1,0:T(8,128)(2,1)S(1)}, u32[]{:S(2)}, u32[]{:S(2)}) collective-permute-start(bf16[256,640]{1,0:T(8,128)(2,1)} %bitcast.10), channel_id=1, source_target_pairs={{0,1},{1,0},{4,8},{5,9},{8,4},{9,5},{12,13},{13,12},{2,3},{3,2},{6... | collective-permute-start | bytes 983048 | tf_op jit(solution)/shard_map/ppermute | solution.py:146
  0.5 4.1 %collective-permute-start.7 = (bf16[256,640]{1,0:T(8,128)(2,1)}, bf16[256,640]{1,0:T(8,128)(2,1)S(1)}, u32[]{:S(2)}, u32[]{:S(2)}) collective-permute-start(bf16[256,640]{1,0:T(8,128)(2,1)} %bitcast.11), channel_id=1, source_target_pairs={{0,4},{4,0},{8,12},{12,8},{1,5},{5,1},{9,13},{13,9},{2,6},{6,2},{1... | collective-permute-start | bytes 983048 | tf_op jit(solution)/shard_map/ppermute | solution.py:145
  4.6 1.0 %copy-done = bf16[1,256,640]{2,1,0:T(8,128)(2,1)S(1)} copy-done((bf16[1,256,640]{2,1,0:T(8,128)(2,1)S(1)}, bf16[1,256,640]{2,1,0:T(8,128)(2,1)}, u32[]{:S(2)}) %copy-start) | copy-done | bytes 327704
  5.6 1.0 %copy-done.2 = bf16[1,256,640]{2,1,0:T(8,128)(2,1)S(1)} copy-done((bf16[1,256,640]{2,1,0:T(8,128)(2,1)S(1)}, bf16[1,256,640]{2,1,0:T(8,128)(2,1)}, u32[]{:S(2)}) %copy-start.2) | copy-done | bytes 327704
  6.6 0.2 squares.1.own_ref
  6.8 0.0 copy-start.12
  6.8 1.6 %collective-permute-start = (f32[2,256]{1,0:T(2,128)S(1)}, f32[2,256]{1,0:T(2,128)S(1)}, u32[]{:S(2)}, u32[]{:S(2)}) collective-permute-start(f32[2,256]{1,0:T(2,128)S(1)} %squares.1.own_ref), channel_id=1, source_target_pairs={{0,2},{2,0},{1,3},{3,1},{4,6},{6,4},{5,7},{7,5},{8,10},{10,8},{9,1... | collective-permute-start | bytes 6152 | tf_op jit(solution)/shard_map/ppermute | solution.py:153
  8.3 0.7 %broadcast_in_dim.9.qgain_ref = f32[1,640]{1,0:T(1,128)S(1)} reshape(f32[640]{0:T(1024)} %param.10) | data formatting | bytes 5120 | tf_op jit(solution)/shard_map/broadcast_in_dim | solution.py:77
  9.1 0.0 copy-start.5
  9.1 1.4 %collective-permute-done.other_ref = f32[2,256]{1,0:T(2,128)S(1)} collective-permute-done((f32[2,256]{1,0:T(2,128)S(1)}, f32[2,256]{1,0:T(2,128)S(1)}, u32[]{:S(2)}, u32[]{:S(2)}) %collective-permute-start) | collective-permute-done | bytes 2080 | tf_op jit(solution)/shard_map/ppermute | solution.py:153
  10.4 0.2 normalize.1
  10.7 0.0 copy-start.6
  10.7 0.1 collective-permute-start.4
  10.8 0.5 %collective-permute-start.15 = (bf16[256,256]{1,0:T(8,128)(2,1)S(1)}, bf16[256,256]{1,0:T(8,128)(2,1)S(1)}, u32[]{:S(2)}, u32[]{:S(2)}) collective-permute-start(bf16[256,256]{1,0:T(8,128)(2,1)S(1)} %get-tuple-element.10.refs_0_), channel_id=1, source_target_pairs={{0,1},{1,0},{4,8},{5,9},{8,4},{9,5},{12,13},{13,12},{2,3},{3,2},{6... | collective-permute-start | bytes 393224 | tf_op jit(solution)/shard_map/ppermute | solution.py:146
  11.3 1.5 %collective-permute-start.13 = (bf16[256,256]{1,0:T(8,128)(2,1)S(1)}, bf16[256,256]{1,0:T(8,128)(2,1)S(1)}, u32[]{:S(2)}, u32[]{:S(2)}) collective-permute-start(bf16[256,256]{1,0:T(8,128)(2,1)S(1)} %get-tuple-element.10.refs_0_), channel_id=1, source_target_pairs={{0,4},{4,0},{8,12},{12,8},{1,5},{5,1},{9,13},{13,9},{2,6},{6,2},{1... | collective-permute-start | bytes 393224 | tf_op jit(solution)/shard_map/ppermute | solution.py:145
  12.8 0.0 collective-permute-done.15.refs_4_
  12.8 6.9 %collective-permute-start.2 = (bf16[256,384]{1,0:T(8,128)(2,1)S(1)}, bf16[256,384]{1,0:T(8,128)(2,1)S(1)}, u32[]{:S(2)}, u32[]{:S(2)}) collective-permute-start(bf16[256,384]{1,0:T(8,128)(2,1)S(1)} %get-tuple-element.9.refs_0_), channel_id=1, source_target_pairs={{0,4},{4,0},{8,12},{12,8},{1,5},{5,1},{9,13},{13,9},{2,6},{6,2},{1... | collective-permute-start | bytes 589832 | tf_op jit(solution)/shard_map/ppermute | solution.py:145
  19.7 0.0 collective-permute-done.13.refs_2_
  19.7 0.0 collective-permute-start.1
  19.8 0.0 collective-permute-done.4.refs_4_
  19.8 0.5 %collective-permute-start.6 = (bf16[256,640]{1,0:T(8,128)(2,1)S(1)}, bf16[256,640]{1,0:T(8,128)(2,1)S(1)}, u32[]{:S(2)}, u32[]{:S(2)}) collective-permute-start(bf16[256,640]{1,0:T(8,128)(2,1)S(1)} %bitcast.12), channel_id=1, source_target_pairs={{0,1},{1,0},{2,3},{3,2},{4,5},{5,4},{6,7},{7,6},{8,9},{9,8},{10,11... | collective-permute-start | bytes 983048 | tf_op jit(solution)/shard_map/ppermute | solution.py:147
  20.3 0.0 collective-permute-done.9.refs_10_
  20.3 0.1 collective-permute-start.10
  20.4 0.0 collective-permute-done.7.refs_8_
  20.4 0.4 %collective-permute-start.8 = (bf16[256,640]{1,0:T(8,128)(2,1)S(1)}, bf16[256,640]{1,0:T(8,128)(2,1)S(1)}, u32[]{:S(2)}, u32[]{:S(2)}) collective-permute-start(bf16[256,640]{1,0:T(8,128)(2,1)S(1)} %collective-permute-done.7.refs_8_), channel_id=1, source_target_pairs={{0,1},{1,0},{2,3},{3,2},{4,5},{5,4},{6,7},{7,6},{8,9},{9,8},{10,11... | collective-permute-start | bytes 983048 | tf_op jit(solution)/shard_map/ppermute | solution.py:147
  20.8 2.6 %collective-permute-done.2.refs_2_ = bf16[256,384]{1,0:T(8,128)(2,1)S(1)} collective-permute-done((bf16[256,384]{1,0:T(8,128)(2,1)S(1)}, bf16[256,384]{1,0:T(8,128)(2,1)S(1)}, u32[]{:S(2)}, u32[]{:S(2)}) %collective-permute-start.2) | collective-permute-done | bytes 196640 | tf_op jit(solution)/shard_map/ppermute | solution.py:145
  23.4 0.0 collective-permute-start.5
  23.4 0.0 collective-permute-done.1.refs_1_
  23.4 0.5 %collective-permute-start.3 = (bf16[256,384]{1,0:T(8,128)(2,1)S(1)}, bf16[256,384]{1,0:T(8,128)(2,1)}, u32[]{:S(2)}, u32[]{:S(2)}) collective-permute-start(bf16[256,384]{1,0:T(8,128)(2,1)S(1)} %collective-permute-done.2.refs_2_), channel_id=1, source_target_pairs={{0,1},{1,0},{2,3},{3,2},{4,5},{5,4},{6,7},{7,6},{8,9},{9,8},{10,11... | collective-permute-start | bytes 589832 | tf_op jit(solution)/shard_map/ppermute | solution.py:147
  24.6 0.0 collective-permute-done.6.refs_7_
  24.6 0.1 collective-permute-start.12
  24.7 0.1 collective-permute-done.5.refs_5_
  24.8 0.3 collective-permute-start.16
  25.2 0.1 collective-permute-done.3.refs_3_
  25.2 0.2 collective-permute-start.14
  25.5 0.1 pad_add_fusion.scalars_ref
  25.6 0.0 collective-permute-done.10.refs_11_
  25.6 0.0 collective-permute-done.8.refs_9_
  25.6 0.0 copy-start.7
  25.6 2.7 %attention.2 = bf16[256,384]{1,0:T(8,128)(2,1)S(1)} custom-call(s32[2]{0:T(128)S(1)} %pad_add_fusion.scalars_ref, bf16[256,640]{1,0:T(8,128)(2,1)S(1)} %get-tuple-element.8.query_ref, f32[64,640]{1,0:T(8,128)S(1)} %copy-done.5, bf16[256,384]{1,0:T(8,128)(2,1)S(1)} %get-tuple-element.9.refs_0_, bf16[256,384]{1,0:T(8,128)(2,1)S(1)} %collective-permute-done.1.refs_1_, ...), custom_call_target="tpu_custom_call" | custom-call | flops 603979776 | bytes 2555904 | tf_op jit(solution)/shard_map/attention/pallas_call | solution.py:121
  28.3 2.6 %collective-permute-start.11 = (bf16[256,384]{1,0:T(8,128)(2,1)S(1)}, bf16[256,384]{1,0:T(8,128)(2,1)S(1)}, u32[]{:S(2)}, u32[]{:S(2)}) collective-permute-start(bf16[256,384]{1,0:T(8,128)(2,1)S(1)} %attention.2), channel_id=1, source_target_pairs={{0,12},{4,0},{8,4},{12,8},{1,13},{5,1},{9,5},{13,9},{2,14},{6,2},{... | collective-permute-start | bytes 589832 | tf_op jit(solution)/shard_map/ppermute | solution.py:172
  30.8 0.0 collective-permute-done.12.refs_1_
  30.8 0.0 collective-permute-done.14.refs_3_
  30.9 1.7 %attention.3 = bf16[256,256]{1,0:T(8,128)(2,1)S(1)} custom-call(s32[2]{0:T(128)S(1)} %pad_add_fusion.scalars_ref, bf16[256,640]{1,0:T(8,128)(2,1)S(1)} %get-tuple-element.8.query_ref, f32[64,640]{1,0:T(8,128)S(1)} %copy-done.5, bf16[256,256]{1,0:T(8,128)(2,1)S(1)} %copy-done.7, bf16[256,256]{1,0:T(8,128)(2,1)S(1)} %collective-permute-done.12.refs_1_, ...), custom_call_target="tpu_custom_call" | custom-call | flops 402653184 | bytes 1703936 | tf_op jit(solution)/shard_map/attention/pallas_call | solution.py:121
  32.6 2.6 %collective-permute-start.17 = (bf16[256,256]{1,0:T(8,128)(2,1)S(1)}, bf16[256,256]{1,0:T(8,128)(2,1)S(1)}, u32[]{:S(2)}, u32[]{:S(2)}) collective-permute-start(bf16[256,256]{1,0:T(8,128)(2,1)S(1)} %attention.3), channel_id=1, source_target_pairs={{0,12},{4,0},{8,4},{12,8},{1,13},{5,1},{9,5},{13,9},{2,14},{6,2},{... | collective-permute-start | bytes 393224 | tf_op jit(solution)/shard_map/ppermute | solution.py:172
  35.2 3.8 %collective-permute-done.17 = bf16[256,256]{1,0:T(8,128)(2,1)S(1)} collective-permute-done((bf16[256,256]{1,0:T(8,128)(2,1)S(1)}, bf16[256,256]{1,0:T(8,128)(2,1)S(1)}, u32[]{:S(2)}, u32[]{:S(2)}) %collective-permute-start.17) | collective-permute-done | bytes 131104 | tf_op jit(solution)/shard_map/ppermute | solution.py:172
  39.0 0.0 collective-permute-done.11
  39.0 0.8 %maximum_bitcast_fusion = bf16[1,256,640]{2,1,0:T(8,128)(2,1)} fusion(bf16[256,256]{1,0:T(8,128)(2,1)S(1)} %collective-permute-done.17, bf16[256,384]{1,0:T(8,128)(2,1)S(1)} %collective-permute-done.11), kind=kLoop, calls=%fused_computation | loop fusion | flops 655360 | bytes 655360 | tf_op jit(solution)/shard_map/broadcast_in_dim | solution.py:174
  (22 shorter events, 0.0 us)
Async XLA Ops:
  0.0 20.3 %collective-permute-start.9 = (bf16[256,640]{1,0:T(8,128)(2,1)}, bf16[256,640]{1,0:T(8,128)(2,1)S(1)}, u32[]{:S(2)}, u32[]{:S(2)}) collective-permute-start(bf16[256,640]{1,0:T(8,128)(2,1)} %bitcast.10), channel_id=1, source_target_pairs={{0,1},{1,0},{4,8},{5,9},{8,4},{9,5},{12,13},{13,12},{2,3},{3,2},{6... | collective-permute-start | bytes 983048 | tf_op jit(solution)/shard_map/ppermute | solution.py:146
  0.5 19.9 %collective-permute-start.7 = (bf16[256,640]{1,0:T(8,128)(2,1)}, bf16[256,640]{1,0:T(8,128)(2,1)S(1)}, u32[]{:S(2)}, u32[]{:S(2)}) collective-permute-start(bf16[256,640]{1,0:T(8,128)(2,1)} %bitcast.11), channel_id=1, source_target_pairs={{0,4},{4,0},{8,12},{12,8},{1,5},{5,1},{9,13},{13,9},{2,6},{6,2},{1... | collective-permute-start | bytes 983048 | tf_op jit(solution)/shard_map/ppermute | solution.py:145
  4.6 1.0 %copy-start = (bf16[1,256,640]{2,1,0:T(8,128)(2,1)S(1)}, bf16[1,256,640]{2,1,0:T(8,128)(2,1)}, u32[]{:S(2)}) copy-start(bf16[1,256,640]{2,1,0:T(8,128)(2,1)} %param.7) | copy-start | bytes 983044
  5.6 1.0 %copy-start.2 = (bf16[1,256,640]{2,1,0:T(8,128)(2,1)S(1)}, bf16[1,256,640]{2,1,0:T(8,128)(2,1)}, u32[]{:S(2)}) copy-start(bf16[1,256,640]{2,1,0:T(8,128)(2,1)} %param.8) | copy-start | bytes 983044
  6.6 3.9 %copy-start.1 = (bf16[1,256,640]{2,1,0:T(8,128)(2,1)S(1)}, bf16[1,256,640]{2,1,0:T(8,128)(2,1)}, u32[]{:S(2)}) copy-start(bf16[1,256,640]{2,1,0:T(8,128)(2,1)} %param.7) | copy-start | bytes 983044
  6.6 3.9 %copy-start.3 = (bf16[1,256,640]{2,1,0:T(8,128)(2,1)S(1)}, bf16[1,256,640]{2,1,0:T(8,128)(2,1)}, u32[]{:S(2)}) copy-start(bf16[1,256,640]{2,1,0:T(8,128)(2,1)} %param.8) | copy-start | bytes 983044
  6.8 2.3 %copy-start.12 = (f32[640]{0:T(1024)S(1)}, f32[640]{0:T(1024)}, u32[]{:S(2)}) copy-start(f32[640]{0:T(1024)} %param.11) | copy-start | bytes 7684
  6.8 3.7 %collective-permute-start = (f32[2,256]{1,0:T(2,128)S(1)}, f32[2,256]{1,0:T(2,128)S(1)}, u32[]{:S(2)}, u32[]{:S(2)}) collective-permute-start(f32[2,256]{1,0:T(2,128)S(1)} %squares.1.own_ref), channel_id=1, source_target_pairs={{0,2},{2,0},{1,3},{3,1},{4,6},{6,4},{5,7},{7,5},{8,10},{10,8},{9,1... | collective-permute-start | bytes 6152 | tf_op jit(solution)/shard_map/ppermute | solution.py:153
  9.0 10.7 %copy-start.4 = (bf16[1,256,640]{2,1,0:T(8,128)(2,1)S(1)}, bf16[1,256,640]{2,1,0:T(8,128)(2,1)}, u32[]{:S(2)}) copy-start(bf16[1,256,640]{2,1,0:T(8,128)(2,1)} %param.9) | copy-start | bytes 983044
  9.1 16.5 %copy-start.5 = (f32[64,640]{1,0:T(8,128)S(1)}, f32[64,640]{1,0:T(8,128)}, u32[]{:S(2)}) copy-start(f32[64,640]{1,0:T(8,128)} %gate_ref.3) | copy-start | bytes 491524
  10.7 12.7 %copy-start.6 = (bf16[256,256]{1,0:T(8,128)(2,1)}, bf16[256,256]{1,0:T(8,128)(2,1)S(1)}, u32[]{:S(2)}) copy-start(bf16[256,256]{1,0:T(8,128)(2,1)S(1)} %get-tuple-element.10.refs_0_) | copy-start | bytes 393220
  10.7 9.0 %collective-permute-start.4 = (bf16[256,384]{1,0:T(8,128)(2,1)S(1)}, bf16[256,384]{1,0:T(8,128)(2,1)S(1)}, u32[]{:S(2)}, u32[]{:S(2)}) collective-permute-start(bf16[256,384]{1,0:T(8,128)(2,1)S(1)} %get-tuple-element.9.refs_0_), channel_id=1, source_target_pairs={{0,1},{1,0},{4,8},{5,9},{8,4},{9,5},{12,13},{13,12},{2,3},{3,2},{6... | collective-permute-start | bytes 589832 | tf_op jit(solution)/shard_map/ppermute | solution.py:146
  10.8 2.0 %collective-permute-start.15 = (bf16[256,256]{1,0:T(8,128)(2,1)S(1)}, bf16[256,256]{1,0:T(8,128)(2,1)S(1)}, u32[]{:S(2)}, u32[]{:S(2)}) collective-permute-start(bf16[256,256]{1,0:T(8,128)(2,1)S(1)} %get-tuple-element.10.refs_0_), channel_id=1, source_target_pairs={{0,1},{1,0},{4,8},{5,9},{8,4},{9,5},{12,13},{13,12},{2,3},{3,2},{6... | collective-permute-start | bytes 393224 | tf_op jit(solution)/shard_map/ppermute | solution.py:146
  11.3 8.4 %collective-permute-start.13 = (bf16[256,256]{1,0:T(8,128)(2,1)S(1)}, bf16[256,256]{1,0:T(8,128)(2,1)S(1)}, u32[]{:S(2)}, u32[]{:S(2)}) collective-permute-start(bf16[256,256]{1,0:T(8,128)(2,1)S(1)} %get-tuple-element.10.refs_0_), channel_id=1, source_target_pairs={{0,4},{4,0},{8,12},{12,8},{1,5},{5,1},{9,13},{13,9},{2,6},{6,2},{1... | collective-permute-start | bytes 393224 | tf_op jit(solution)/shard_map/ppermute | solution.py:145
  12.8 11.1 %copy-start.8 = (bf16[256,256]{1,0:T(8,128)(2,1)}, bf16[256,256]{1,0:T(8,128)(2,1)S(1)}, u32[]{:S(2)}) copy-start(bf16[256,256]{1,0:T(8,128)(2,1)S(1)} %collective-permute-done.15.refs_4_) | copy-start | bytes 393220
  12.8 10.6 %collective-permute-start.2 = (bf16[256,384]{1,0:T(8,128)(2,1)S(1)}, bf16[256,384]{1,0:T(8,128)(2,1)S(1)}, u32[]{:S(2)}, u32[]{:S(2)}) collective-permute-start(bf16[256,384]{1,0:T(8,128)(2,1)S(1)} %get-tuple-element.9.refs_0_), channel_id=1, source_target_pairs={{0,4},{4,0},{8,12},{12,8},{1,5},{5,1},{9,13},{13,9},{2,6},{6,2},{1... | collective-permute-start | bytes 589832 | tf_op jit(solution)/shard_map/ppermute | solution.py:145
  19.7 4.2 %copy-start.10 = (bf16[256,256]{1,0:T(8,128)(2,1)}, bf16[256,256]{1,0:T(8,128)(2,1)S(1)}, u32[]{:S(2)}) copy-start(bf16[256,256]{1,0:T(8,128)(2,1)S(1)} %collective-permute-done.13.refs_2_) | copy-start | bytes 393220
  19.7 3.6 %collective-permute-start.1 = (bf16[256,384]{1,0:T(8,128)(2,1)S(1)}, bf16[256,384]{1,0:T(8,128)(2,1)S(1)}, u32[]{:S(2)}, u32[]{:S(2)}) collective-permute-start(bf16[256,384]{1,0:T(8,128)(2,1)S(1)} %get-tuple-element.9.refs_0_), channel_id=1, source_target_pairs={{0,1},{1,0},{2,3},{3,2},{4,5},{5,4},{6,7},{7,6},{8,9},{9,8},{10,11... | collective-permute-start | bytes 589832 | tf_op jit(solution)/shard_map/ppermute | solution.py:147
  19.8 4.8 %collective-permute-start.6 = (bf16[256,640]{1,0:T(8,128)(2,1)S(1)}, bf16[256,640]{1,0:T(8,128)(2,1)S(1)}, u32[]{:S(2)}, u32[]{:S(2)}) collective-permute-start(bf16[256,640]{1,0:T(8,128)(2,1)S(1)} %bitcast.12), channel_id=1, source_target_pairs={{0,1},{1,0},{2,3},{3,2},{4,5},{5,4},{6,7},{7,6},{8,9},{9,8},{10,11... | collective-permute-start | bytes 983048 | tf_op jit(solution)/shard_map/ppermute | solution.py:147
  20.3 5.3 %collective-permute-start.10 = (bf16[256,640]{1,0:T(8,128)(2,1)S(1)}, bf16[256,640]{1,0:T(8,128)(2,1)S(1)}, u32[]{:S(2)}, u32[]{:S(2)}) collective-permute-start(bf16[256,640]{1,0:T(8,128)(2,1)S(1)} %collective-permute-done.9.refs_10_), channel_id=1, source_target_pairs={{0,1},{1,0},{2,3},{3,2},{4,5},{5,4},{6,7},{7,6},{8,9},{9,8},{10,11... | collective-permute-start | bytes 983048 | tf_op jit(solution)/shard_map/ppermute | solution.py:147
  20.4 5.2 %collective-permute-start.8 = (bf16[256,640]{1,0:T(8,128)(2,1)S(1)}, bf16[256,640]{1,0:T(8,128)(2,1)S(1)}, u32[]{:S(2)}, u32[]{:S(2)}) collective-permute-start(bf16[256,640]{1,0:T(8,128)(2,1)S(1)} %collective-permute-done.7.refs_8_), channel_id=1, source_target_pairs={{0,1},{1,0},{2,3},{3,2},{4,5},{5,4},{6,7},{7,6},{8,9},{9,8},{10,11... | collective-permute-start | bytes 983048 | tf_op jit(solution)/shard_map/ppermute | solution.py:147
  23.4 1.4 %collective-permute-start.5 = (bf16[256,384]{1,0:T(8,128)(2,1)S(1)}, bf16[256,384]{1,0:T(8,128)(2,1)S(1)}, u32[]{:S(2)}, u32[]{:S(2)}) collective-permute-start(bf16[256,384]{1,0:T(8,128)(2,1)S(1)} %collective-permute-done.4.refs_4_), channel_id=1, source_target_pairs={{0,1},{1,0},{2,3},{3,2},{4,5},{5,4},{6,7},{7,6},{8,9},{9,8},{10,11... | collective-permute-start | bytes 589832 | tf_op jit(solution)/shard_map/ppermute | solution.py:147
  23.4 1.8 %collective-permute-start.3 = (bf16[256,384]{1,0:T(8,128)(2,1)S(1)}, bf16[256,384]{1,0:T(8,128)(2,1)}, u32[]{:S(2)}, u32[]{:S(2)}) collective-permute-start(bf16[256,384]{1,0:T(8,128)(2,1)S(1)} %collective-permute-done.2.refs_2_), channel_id=1, source_target_pairs={{0,1},{1,0},{2,3},{3,2},{4,5},{5,4},{6,7},{7,6},{8,9},{9,8},{10,11... | collective-permute-start | bytes 589832 | tf_op jit(solution)/shard_map/ppermute | solution.py:147
  24.6 6.3 %collective-permute-start.12 = (bf16[256,256]{1,0:T(8,128)(2,1)}, bf16[256,256]{1,0:T(8,128)(2,1)S(1)}, u32[]{:S(2)}, u32[]{:S(2)}) collective-permute-start(bf16[256,256]{1,0:T(8,128)(2,1)} %copy-done.6), channel_id=1, source_target_pairs={{0,1},{1,0},{2,3},{3,2},{4,5},{5,4},{6,7},{7,6},{8,9},{9,8},{10,11... | collective-permute-start | bytes 393224 | tf_op jit(solution)/shard_map/ppermute | solution.py:147
  24.8 6.0 %collective-permute-start.16 = (bf16[256,256]{1,0:T(8,128)(2,1)}, bf16[256,256]{1,0:T(8,128)(2,1)S(1)}, u32[]{:S(2)}, u32[]{:S(2)}) collective-permute-start(bf16[256,256]{1,0:T(8,128)(2,1)} %copy-done.8), channel_id=1, source_target_pairs={{0,1},{1,0},{2,3},{3,2},{4,5},{5,4},{6,7},{7,6},{8,9},{9,8},{10,11... | collective-permute-start | bytes 393224 | tf_op jit(solution)/shard_map/ppermute | solution.py:147
  25.2 5.6 %collective-permute-start.14 = (bf16[256,256]{1,0:T(8,128)(2,1)}, bf16[256,256]{1,0:T(8,128)(2,1)S(1)}, u32[]{:S(2)}, u32[]{:S(2)}) collective-permute-start(bf16[256,256]{1,0:T(8,128)(2,1)} %copy-done.10), channel_id=1, source_target_pairs={{0,1},{1,0},{2,3},{3,2},{4,5},{5,4},{6,7},{7,6},{8,9},{9,8},{10,11... | collective-permute-start | bytes 393224 | tf_op jit(solution)/shard_map/ppermute | solution.py:147
  25.6 5.3 %copy-start.7 = (bf16[256,256]{1,0:T(8,128)(2,1)S(1)}, bf16[256,256]{1,0:T(8,128)(2,1)}, u32[]{:S(2)}) copy-start(bf16[256,256]{1,0:T(8,128)(2,1)} %copy-done.6) | copy-start | bytes 393220
  25.6 5.3 %copy-start.9 = (bf16[256,256]{1,0:T(8,128)(2,1)S(1)}, bf16[256,256]{1,0:T(8,128)(2,1)}, u32[]{:S(2)}) copy-start(bf16[256,256]{1,0:T(8,128)(2,1)} %copy-done.8) | copy-start | bytes 393220
  25.6 5.3 %copy-start.11 = (bf16[256,256]{1,0:T(8,128)(2,1)S(1)}, bf16[256,256]{1,0:T(8,128)(2,1)}, u32[]{:S(2)}) copy-start(bf16[256,256]{1,0:T(8,128)(2,1)} %copy-done.10) | copy-start | bytes 393220
  28.3 10.8 %collective-permute-start.11 = (bf16[256,384]{1,0:T(8,128)(2,1)S(1)}, bf16[256,384]{1,0:T(8,128)(2,1)S(1)}, u32[]{:S(2)}, u32[]{:S(2)}) collective-permute-start(bf16[256,384]{1,0:T(8,128)(2,1)S(1)} %attention.2), channel_id=1, source_target_pairs={{0,12},{4,0},{8,4},{12,8},{1,13},{5,1},{9,5},{13,9},{2,14},{6,2},{... | collective-permute-start | bytes 589832 | tf_op jit(solution)/shard_map/ppermute | solution.py:172
  32.6 6.4 %collective-permute-start.17 = (bf16[256,256]{1,0:T(8,128)(2,1)S(1)}, bf16[256,256]{1,0:T(8,128)(2,1)S(1)}, u32[]{:S(2)}, u32[]{:S(2)}) collective-permute-start(bf16[256,256]{1,0:T(8,128)(2,1)S(1)} %attention.3), channel_id=1, source_target_pairs={{0,12},{4,0},{8,4},{12,8},{1,13},{5,1},{9,5},{13,9},{2,14},{6,2},{... | collective-permute-start | bytes 393224 | tf_op jit(solution)/shard_map/ppermute | solution.py:172

commit v2 on v1

v2 whole, which is shorter than its diff:
```python
import functools
import math

import jax
import jax.numpy as jnp
from jax import lax
from jax.experimental import pallas as pl
from jax.experimental.pallas import tpu as pltpu
from jax.sharding import PartitionSpec as P


DH = 128
EPSILON = 1e-06
SCALE = 1.0 / (math.sqrt(DH) * math.log(2.0))
CHUNK_SHARE = (3, 2)

LIMIT = 8 << 20
VMEM = pl.BlockSpec(memory_space=pltpu.VMEM)
HBM = pl.BlockSpec(memory_space=pltpu.HBM)
COPY_PARTS = 4
SMEM = pl.BlockSpec(memory_space=pltpu.SMEM)


def chunk_widths(heads):
    first = (heads * CHUNK_SHARE[0]) // sum(CHUNK_SHARE)
    return [w * DH for w in (first, heads - first) if w > 0]


def row_square_sums(ref):
    _, width = ref.shape
    total = None
    for start in range(0, width, DH):
        wide = ref[:, start : start + DH].astype(jnp.float32)
        total = wide * wide if total is None else total + wide * wide
    return jnp.sum(total.T, axis=0, keepdims=True)


def load_kernel(parts, *refs):
    query_hbm, key_hbm, value_hbm, *small_hbm = refs[:6]
    query_ref, key_ref, square_ref, *others = refs[6:-1]
    small_refs, value_refs, sems = others[:3], others[3:], refs[-1]
    copies = []

    def copy(source, target):
        copies.append(pltpu.make_async_copy(source, target, sems.at[len(copies)]))

    step = query_hbm.shape[0] // parts
    for source, target in ((query_hbm, query_ref), (key_hbm, key_ref)):
        for part in range(parts):
            copy(source.at[pl.ds(part * step, step)], target.at[pl.ds(part * step, step)])
    for source, target in zip(small_hbm, small_refs):
        copy(source, target)
    column = 0
    for target in value_refs:
        copy(value_hbm.at[:, pl.ds(column, target.shape[1])], target)
        column += target.shape[1]
    for started in copies:
        started.start()
    for which, ref in enumerate((query_ref, key_ref)):
        for started in copies[which * parts : (which + 1) * parts]:
            started.wait()
        square_ref[which : which + 1, :] = row_square_sums(ref)
    for started in copies[2 * parts :]:
        started.wait()


def load(query, key, value, query_gain, key_gain, gate_table, widths):
    rows, width = query.shape
    whole = jax.ShapeDtypeStruct((rows, width), query.dtype)
    sources = (query, key, value, query_gain, key_gain, gate_table)
    shapes = [whole, whole, jax.ShapeDtypeStruct((2, rows), jnp.float32)]
    shapes += [jax.ShapeDtypeStruct(x.shape, x.dtype) for x in sources[3:]]
    shapes += [jax.ShapeDtypeStruct((rows, chunk), value.dtype) for chunk in widths]
    return pl.pallas_call(
        functools.partial(load_kernel, COPY_PARTS),
        out_shape=shapes,
        in_specs=[HBM] * 6,
        out_specs=[VMEM] * len(shapes),
        scratch_shapes=[pltpu.SemaphoreType.DMA((2 * COPY_PARTS + 3 + len(widths),))],
        name="load",
        compiler_params=pltpu.CompilerParams(vmem_limit_bytes=LIMIT),
    )(*(pltpu.with_memory_space_constraint(x, pltpu.HBM) for x in sources))


def apply_norm(ref, factor, gain_ref, out_ref):
    rows, width = ref.shape
    spread = jnp.broadcast_to(factor, (DH, rows)).T
    for start in range(0, width, DH):
        here = slice(start, start + DH)
        wide = ref[:, here].astype(jnp.float32)
        out_ref[:, here] = (wide * spread * gain_ref[here]).astype(jnp.bfloat16)


def normalize_kernel(full_width, query_ref, key_ref, own_ref, other_ref, qgain_ref, kgain_ref, qout_ref, kout_ref, factor_ref):
    factor = lax.rsqrt((own_ref[...] + other_ref[...]) / full_width + EPSILON)
    factor_ref[...] = factor[1:2, :]
    apply_norm(key_ref, factor[1:2, :], kgain_ref, kout_ref)
    apply_norm(query_ref, factor[0:1, :], qgain_ref, qout_ref)


def normalize(query, key, own, other, query_gain, key_gain, full_width):
    rows = query.shape[0]
    kept = jax.ShapeDtypeStruct(query.shape, jnp.bfloat16)
    return pl.pallas_call(
        functools.partial(normalize_kernel, full_width),
        out_shape=[kept, kept, jax.ShapeDtypeStruct((1, rows), jnp.float32)],
        in_specs=[VMEM] * 6,
        out_specs=[VMEM] * 3,
        name="normalize",
        compiler_params=pltpu.CompilerParams(vmem_limit_bytes=LIMIT),
    )(query, key, own, other, query_gain, key_gain)


def normalize_two_kernel(a_ref, b_ref, afactor_ref, bfactor_ref, gain_ref, aout_ref, bout_ref):
    apply_norm(a_ref, afactor_ref[...], gain_ref, aout_ref)
    apply_norm(b_ref, bfactor_ref[...], gain_ref, bout_ref)


def normalize_two(a, b, afactor, bfactor, gain):
    kept = jax.ShapeDtypeStruct(a.shape, jnp.bfloat16)
    return pl.pallas_call(
        normalize_two_kernel,
        out_shape=[kept, kept],
        in_specs=[VMEM] * 5,
        out_specs=[VMEM] * 2,
        name="normalize_two",
        compiler_params=pltpu.CompilerParams(vmem_limit_bytes=LIMIT),
    )(a, b, afactor, bfactor, gain)


def with_used_blocks(work):
    place = lax.axis_index("queue")
    inner = (place > 0) & (place < lax.axis_size("queue") - 1)

    @pl.when(inner)
    def _():
        work(6)

    @pl.when(jnp.logical_not(inner))
    def _():
        work(4)


def scores_kernel(column, query_ref, *refs):
    keys, values = refs[0:6], refs[6:8]
    weight_ref, sum_ref, own_ref = refs[8:]
    rows = query_ref.shape[0]

    def work(used):
        for head in range(weight_ref.shape[0]):
            here = slice(head * DH, (head + 1) * DH)
            there = slice(column + head * DH, column + (head + 1) * DH)
            head_query = query_ref[:, there]
            scores = [
                lax.dot_general(
                    head_query, key_ref[:, there], (((1,), (1,)), ((), ())), preferred_element_type=jnp.float32
                )
                for key_ref in keys[:used]
            ]
            row_max = jnp.max(functools.reduce(jnp.maximum, scores), axis=1, keepdims=True)
            shift = row_max * SCALE
            weights = [jnp.exp2(part * SCALE - shift) for part in scores]
            weight_sum = jnp.sum(functools.reduce(jnp.add, weights), axis=1, keepdims=True)
            sum_ref[:, here] = jnp.broadcast_to(weight_sum, (rows, DH))
            low = [part.astype(jnp.bfloat16) for part in weights]
            for block in range(2, used):
                weight_ref[head, :, (block - 2) * rows : (block - 1) * rows] = low[block]
            own_ref[:, here] = functools.reduce(
                jnp.add,
                [
                    jnp.dot(part, value_ref[:, here], preferred_element_type=jnp.float32)
                    for part, value_ref in zip(low, values)
                ],
            )

    with_used_blocks(work)


def scores(column, width, query, keys, values):
    rows = query.shape[0]
    count = 6 * rows * width * rows
    return pl.pallas_call(
        functools.partial(scores_kernel, column),
        out_shape=[
            jax.ShapeDtypeStruct((width // DH, rows, 4 * rows), jnp.bfloat16),
            jax.ShapeDtypeStruct((rows, width), jnp.float32),
            jax.ShapeDtypeStruct((rows, width), jnp.float32),
        ],
        in_specs=[VMEM] * 9,
        out_specs=[VMEM] * 3,
        name="scores",
        compiler_params=pltpu.CompilerParams(vmem_limit_bytes=LIMIT),
        cost_estimate=pl.CostEstimate(flops=3 * count, bytes_accessed=26 * rows * width, transcendentals=count // DH),
    )(query, *keys, *values)


def gather_kernel(column, level_ref, gate_ref, weight_ref, sum_ref, own_ref, *refs):
    values, out_ref = refs[0:4], refs[4]
    rows = out_ref.shape[0]
    gate = gate_ref[pl.ds(level_ref[0], 1), :]

    def work(used):
        for head in range(out_ref.shape[1] // DH):
            here = slice(head * DH, (head + 1) * DH)
            there = slice(column + head * DH, column + (head + 1) * DH)
            summed = own_ref[:, here]
            for block in range(used - 2):
                summed += jnp.dot(
                    weight_ref[head, :, block * rows : (block + 1) * rows],
                    values[block][:, here],
                    preferred_element_type=jnp.float32,
                )
            out_ref[:, here] = (gate[:, there] * (summed / sum_ref[:, here])).astype(jnp.bfloat16)

    with_used_blocks(work)


def gather(column, width, levels, gate_table, weights, sums, own, values):
    rows = own.shape[0]
    count = 4 * rows * width * rows
    return pl.pallas_call(
        functools.partial(gather_kernel, column),
        out_shape=jax.ShapeDtypeStruct((rows, width), jnp.bfloat16),
        in_specs=[SMEM] + [VMEM] * 8,
        out_specs=VMEM,
        name="gather",
        compiler_params=pltpu.CompilerParams(vmem_limit_bytes=LIMIT),
        cost_estimate=pl.CostEstimate(flops=2 * count, bytes_accessed=26 * rows * width, transcendentals=0),
    )(levels, gate_table, weights, sums, own, *values)


def body(query_input, key_input, value_input, query_gain, key_gain, gate_table, levels):
    places, seq, tp = (lax.axis_size(name) for name in ("queue", "seq", "tp"))
    _, width = query_input.shape[1:]
    widths = chunk_widths(width // DH)
    first_pairs = [(i, i ^ 1) for i in range(places)]
    second_pairs = []
    for i in range(places):
        for s in range(seq):
            to = (i, 1 - s) if i in (0, places - 1) else (((i - 1) ^ 1) + 1, s)
            second_pairs.append((i * seq + s, to[0] * seq + to[1]))
    swap_pairs = [(s, 1 - s) for s in range(seq)]
    roll_pairs = [(i, (i - 1) % places) for i in range(places)]

    first = lambda x: lax.ppermute(x, "queue", first_pairs)
    second = lambda x: lax.ppermute(x, ("queue", "seq"), second_pairs)
    swap = lambda x: lax.ppermute(x, "seq", swap_pairs)

    query, key, value = query_input[0], key_input[0], value_input[0]
    key_first, key_second = first(key), second(key)
    query, key, own, query_gain, key_gain, gate_table, *value_parts = load(
        query, key, value, query_gain, key_gain, gate_table, widths
    )
    if tp == 2:
        other = lax.ppermute(own, "tp", [(0, 1), (1, 0)])
    else:
        own, other = lax.psum(own, "tp"), jnp.zeros_like(own)
    query_normed, key_normed, factor = normalize(query, key, own, other, query_gain, key_gain, width * tp)
    factor_first, factor_second = first(factor), second(factor)
    key_first, key_second = normalize_two(key_first, key_second, factor_first, factor_second, key_gain)
    keys = [key_normed, swap(key_normed), key_first, swap(key_first), key_second, swap(key_second)]
    outputs, column = [], 0
    for part in value_parts:
        chunk = part.shape[1]
        part_first, part_second = first(part), second(part)
        weights, sums, own = scores(column, chunk, query_normed, keys, [part, swap(part)])
        beside = [part_first, swap(part_first), part_second, swap(part_second)]
        gated = gather(column, chunk, levels, gate_table, weights, sums, own, beside)
        outputs.append(lax.ppermute(gated, "queue", roll_pairs))
        column += chunk
    return jnp.concatenate(outputs, axis=1)[None]


def solution(mesh):
    spec = P(("grp", "queue"), "seq", "tp")
    in_specs = (spec, spec, spec, P("tp"), P("tp"), P(None, "tp"), P(("grp", "queue")))
    return jax.shard_map(body, mesh=mesh, in_specs=in_specs, out_specs=spec, check_vma=False)
```

time: 40 us -> 41.5 us (1.038)
  waiting for transfers between devices: 8.02 us -> 15.5 us
  starting transfers between devices: 22.6 us -> 19.2 us
  local copies, waits for them, and re-layouts: 2.69 us -> 0 us
    ppermute x3 -> x4, waiting for transfers between devices: 2.61 us -> 8.01 us  [body(): first = lambda x: lax.ppermute(x, 'queue', first_pairs)]
    ppermute x3 -> x4, starting transfers between devices: 12.6 us -> 9.77 us  [body(): first = lambda x: lax.ppermute(x, 'queue', first_pairs)]
    unnamed x26 -> x0, local copies, waits for them, and re-layouts: 2 us -> none
    ppermute x3 -> x4, waiting for transfers between devices: 0.01 us -> 1.17 us  [body(): second = lambda x: lax.ppermute(x, ('queue', 'seq'), second_pairs)]
    ppermute x3 -> x4, starting transfers between devices: 1.06 us -> 0.33 us  [body(): second = lambda x: lax.ppermute(x, ('queue', 'seq'), second_pairs)]
    ppermute x1, waiting for transfers between devices: 1.38 us -> 2.09 us  [body(): other = lax.ppermute(own, 'tp', [(0, 1), (1, 0)])]
    broadcast_in_dim x2 -> x0, local copies, waits for them, and re-layouts: 0.69 us -> none  [the longest x1 0.69 us: normalize(): query_gain[None]]
    pallas_call x3 -> x6, Pallas kernels: 4.61 us -> 4.81 us  [the longest x2 2.46 us: scores(): pl.pallas_call(functools.partial(scores_kernel, column), out_shape=[jax.S...]
  transfers between devices with their start and end apart: 18 -> 20, of which waited for: 5 -> 5; matrix products, arithmetic and copies ran while one was open for 2% -> 0% of each run, Pallas kernels for 12% -> 12%
where the time goes in v2:
time: 41.5 us; the launch traced here: 41.3 us
  starting transfers between devices  19.2 us (46%)
  waiting for transfers between devices  15.5 us (37%)
  Pallas kernels  5.06 us (12%)
  other arithmetic  0.76 us (2%)
  between operations  0.76 us (2%)
    ppermute x4, starting transfers between devices, body(): first = lambda x: lax.ppermute(x, 'queue', first_pairs)  9.77 us
    ppermute x4, waiting for transfers between devices, body(): first = lambda x: lax.ppermute(x, 'queue', first_pairs)  8.01 us
    ppermute x2, starting transfers between devices, body(): outputs.append(lax.ppermute(gated, 'queue', roll_pairs))  5.06 us
    ppermute x2, waiting for transfers between devices, body(): outputs.append(lax.ppermute(gated, 'queue', roll_pairs))  4.21 us
    ppermute x9, starting transfers between devices, body(): swap = lambda x: lax.ppermute(x, 'seq', swap_pairs)  2.58 us
    pallas_call x2, Pallas kernels, scores(): pl.pallas_call(functools.partial(scores_kernel, column), out_shape=[jax.S...  2.46 us
    ppermute x1, waiting for transfers between devices, body(): other = lax.ppermute(own, 'tp', [(0, 1), (1, 0)])  2.09 us
    ppermute x1, starting transfers between devices, body(): other = lax.ppermute(own, 'tp', [(0, 1), (1, 0)])  1.49 us
  transfers between devices with their start and end apart: 20, of which 5 were waited for; matrix products, arithmetic and copies ran while one was open for 0% of the time, Pallas kernels for 12%

profile of v2, /device:TPU:0, one launch (start us, length us, event | category | flops | bytes accessed | tf_op | source)
XLA Modules:
  0.0 41.3 jit_solution(16903159842688646026)
XLA Ops:
  0.0 3.1 %collective-permute-start.2 = (bf16[256,640]{1,0:T(8,128)(2,1)}, bf16[256,640]{1,0:T(8,128)(2,1)S(1)}, u32[]{:S(2)}, u32[]{:S(2)}) collective-permute-start(bf16[256,640]{1,0:T(8,128)(2,1)} %bitcast.7), channel_id=1, source_target_pairs={{0,4},{4,0},{8,12},{12,8},{1,5},{5,1},{9,13},{13,9},{2,6},{6,2},{1... | collective-permute-start | bytes 983048 | tf_op jit(solution)/shard_map/ppermute | solution.py:245
  3.1 0.0 collective-permute-start.3
  3.1 1.4 %load.1 = (bf16[256,640]{1,0:T(8,128)(2,1)S(1)}, bf16[256,640]{1,0:T(8,128)(2,1)S(1)}, f32[2,256]{1,0:T(2,128)S(1)}, f32[640]{0:T(1024)S(1)}, f32[640]{0:T(1024)...) custom-call(bf16[256,640]{1,0:T(8,128)(2,1)} %bitcast.5, ...), custom_call_target="tpu_custom_call" | custom-call | tf_op jit(solution)/shard_map/load/pallas_call | solution.py:74
  4.5 0.6 %collective-permute-start.8 = (bf16[256,384]{1,0:T(8,128)(2,1)S(1)}, bf16[256,384]{1,0:T(8,128)(2,1)S(1)}, u32[]{:S(2)}, u32[]{:S(2)}) collective-permute-start(bf16[256,384]{1,0:T(8,128)(2,1)S(1)} %get-tuple-element.35.refs_6_), channel_id=1, source_target_pairs={{0,1},{1,0},{2,3},{3,2},{4,5},{5,4},{6,7},{7,6},{8,9},{9,8},{10,11... | collective-permute-start | bytes 589832 | tf_op jit(solution)/shard_map/ppermute | solution.py:247
  5.1 2.7 %collective-permute-start.15 = (bf16[256,256]{1,0:T(8,128)(2,1)S(1)}, bf16[256,256]{1,0:T(8,128)(2,1)S(1)}, u32[]{:S(2)}, u32[]{:S(2)}) collective-permute-start(bf16[256,256]{1,0:T(8,128)(2,1)S(1)} %get-tuple-element.39.refs_6_), channel_id=1, source_target_pairs={{0,4},{4,0},{8,12},{12,8},{1,5},{5,1},{9,13},{13,9},{2,6},{6,2},{1... | collective-permute-start | bytes 393224 | tf_op jit(solution)/shard_map/ppermute | solution.py:245
  7.8 1.5 %collective-permute-start = (f32[2,256]{1,0:T(2,128)S(1)}, f32[2,256]{1,0:T(2,128)S(1)}, u32[]{:S(2)}, u32[]{:S(2)}) collective-permute-start(f32[2,256]{1,0:T(2,128)S(1)} %get-tuple-element.27.own_ref), channel_id=1, source_target_pairs={{0,2},{2,0},{1,3},{3,1},{4,6},{6,4},{5,7},{7,5},{8,10},{10,8},{9,1... | collective-permute-start | bytes 6152 | tf_op jit(solution)/shard_map/ppermute | solution.py:255
  9.3 2.1 %collective-permute-done.other_ref = f32[2,256]{1,0:T(2,128)S(1)} collective-permute-done((f32[2,256]{1,0:T(2,128)S(1)}, f32[2,256]{1,0:T(2,128)S(1)}, u32[]{:S(2)}, u32[]{:S(2)}) %collective-permute-start) | collective-permute-done | bytes 2080 | tf_op jit(solution)/shard_map/ppermute | solution.py:255
  11.4 0.2 normalize.1
  11.6 0.1 collective-permute-start.4
  11.8 3.5 %collective-permute-done.4.afactor_ref = f32[1,256]{1,0:T(1,128)S(1)} collective-permute-done((f32[1,256]{1,0:T(1,128)S(1)}, f32[1,256]{1,0:T(1,128)S(1)}, u32[]{:S(2)}, u32[]{:S(2)}) %collective-permute-start.4) | collective-permute-done | bytes 1056 | tf_op jit(solution)/shard_map/ppermute | solution.py:245
  15.3 0.0 collective-permute-start.5
  15.3 1.2 %collective-permute-done.5.bfactor_ref = f32[1,256]{1,0:T(1,128)S(1)} collective-permute-done((f32[1,256]{1,0:T(1,128)S(1)}, f32[1,256]{1,0:T(1,128)S(1)}, u32[]{:S(2)}, u32[]{:S(2)}) %collective-permute-start.5) | collective-permute-done | bytes 1056 | tf_op jit(solution)/shard_map/ppermute | solution.py:246
  16.4 0.2 collective-permute-start.17
  16.6 0.0 collective-permute-done.15.refs_0_
  16.6 0.3 collective-permute-start.1
  17.0 0.0 collective-permute-done.2.a_ref
  17.0 3.9 %collective-permute-start.9 = (bf16[256,384]{1,0:T(8,128)(2,1)S(1)}, bf16[256,384]{1,0:T(8,128)(2,1)S(1)}, u32[]{:S(2)}, u32[]{:S(2)}) collective-permute-start(bf16[256,384]{1,0:T(8,128)(2,1)S(1)} %get-tuple-element.35.refs_6_), channel_id=1, source_target_pairs={{0,4},{4,0},{8,12},{12,8},{1,5},{5,1},{9,13},{13,9},{2,6},{6,2},{1... | collective-permute-start | bytes 589832 | tf_op jit(solution)/shard_map/ppermute | solution.py:245
  20.8 0.0 collective-permute-done.3.b_ref
  20.8 0.2 collective-permute-start.11
  21.0 0.2 normalize_two.1
  21.2 0.0 collective-permute-done.17.refs_2_
  21.2 0.4 %collective-permute-start.6 = (bf16[256,640]{1,0:T(8,128)(2,1)S(1)}, bf16[256,640]{1,0:T(8,128)(2,1)S(1)}, u32[]{:S(2)}, u32[]{:S(2)}) collective-permute-start(bf16[256,640]{1,0:T(8,128)(2,1)S(1)} %get-tuple-element.33.refs_2_), channel_id=1, source_target_pairs={{0,1},{1,0},{2,3},{3,2},{4,5},{5,4},{6,7},{7,6},{8,9},{9,8},{10,11... | collective-permute-start | bytes 983048 | tf_op jit(solution)/shard_map/ppermute | solution.py:247
  21.6 0.0 collective-permute-done.8.refs_7_
  21.7 0.2 collective-permute-start.7
  21.8 4.5 %collective-permute-done.9.refs_0_ = bf16[256,384]{1,0:T(8,128)(2,1)S(1)} collective-permute-done((bf16[256,384]{1,0:T(8,128)(2,1)S(1)}, bf16[256,384]{1,0:T(8,128)(2,1)S(1)}, u32[]{:S(2)}, u32[]{:S(2)}) %collective-permute-start.9) | collective-permute-done | bytes 196640 | tf_op jit(solution)/shard_map/ppermute | solution.py:245
  26.3 0.0 collective-permute-start.10
  26.3 0.0 collective-permute-done.11.refs_2_
  26.3 0.5 %collective-permute-start.12 = (bf16[256,384]{1,0:T(8,128)(2,1)S(1)}, bf16[256,384]{1,0:T(8,128)(2,1)S(1)}, u32[]{:S(2)}, u32[]{:S(2)}) collective-permute-start(bf16[256,384]{1,0:T(8,128)(2,1)S(1)} %collective-permute-done.11.refs_2_), channel_id=1, source_target_pairs={{0,1},{1,0},{2,3},{3,2},{4,5},{5,4},{6,7},{7,6},{8,9},{9,8},{10,11... | collective-permute-start | bytes 589832 | tf_op jit(solution)/shard_map/ppermute | solution.py:247
  26.8 0.0 collective-permute-done.1.refs_1_
  26.8 0.1 collective-permute-start.14
  26.9 0.0 collective-permute-done.6.refs_3_
  26.9 0.4 %collective-permute-start.16 = (bf16[256,256]{1,0:T(8,128)(2,1)S(1)}, bf16[256,256]{1,0:T(8,128)(2,1)S(1)}, u32[]{:S(2)}, u32[]{:S(2)}) collective-permute-start(bf16[256,256]{1,0:T(8,128)(2,1)S(1)} %collective-permute-done.15.refs_0_), channel_id=1, source_target_pairs={{0,1},{1,0},{2,3},{3,2},{4,5},{5,4},{6,7},{7,6},{8,9},{9,8},{10,11... | collective-permute-start | bytes 393224 | tf_op jit(solution)/shard_map/ppermute | solution.py:247
  27.4 0.0 collective-permute-done.7.refs_5_
  27.4 0.1 collective-permute-start.18
  28.1 1.4 %scores.2 = (bf16[3,256,1024]{2,1,0:T(8,128)(2,1)S(1)}, f32[256,384]{1,0:T(8,128)S(1)}, f32[256,384]{1,0:T(8,128)S(1)}) custom-call(bf16[256,640]{1,0:T(8,128)(2,1)S(1)} %get-tuple-element.30.query_ref, bf16[256,640]{1,0:T(8,128)(2,1)S(1)} %get-tuple-element.31.refs_0_, bf16[256,640]{1,0:T(8,128)(2,1)S(1)} %collective-permute-done.1.refs_1_, ...), custom_call_target="tpu_custom_call" | custom-call | flops 452984832 | bytes 2555904 | tf_op jit(solution)/shard_map/scores/pallas_call | solution.py:182
  29.5 0.0 collective-permute-done.10.refs_1_
  29.5 0.0 collective-permute-done.12.refs_3_
  29.5 0.4 gather.2
  29.9 1.4 %collective-permute-start.13 = (bf16[256,384]{1,0:T(8,128)(2,1)S(1)}, bf16[256,384]{1,0:T(8,128)(2,1)S(1)}, u32[]{:S(2)}, u32[]{:S(2)}) collective-permute-start(bf16[256,384]{1,0:T(8,128)(2,1)S(1)} %gather.2), channel_id=1, source_target_pairs={{0,12},{4,0},{8,4},{12,8},{1,13},{5,1},{9,5},{13,9},{2,14},{6,2},{... | collective-permute-start | bytes 589832 | tf_op jit(solution)/shard_map/ppermute | solution.py:269
  31.3 0.0 collective-permute-done.14.refs_7_
  31.3 1.0 %scores.3 = (bf16[2,256,1024]{2,1,0:T(8,128)(2,1)S(1)}, f32[256,256]{1,0:T(8,128)S(1)}, f32[256,256]{1,0:T(8,128)S(1)}) custom-call(bf16[256,640]{1,0:T(8,128)(2,1)S(1)} %get-tuple-element.30.query_ref, bf16[256,640]{1,0:T(8,128)(2,1)S(1)} %get-tuple-element.31.refs_0_, bf16[256,640]{1,0:T(8,128)(2,1)S(1)} %collective-permute-done.1.refs_1_, ...), custom_call_target="tpu_custom_call" | custom-call | flops 301989888 | bytes 1703936 | tf_op jit(solution)/shard_map/scores/pallas_call | solution.py:182
  32.4 0.0 collective-permute-done.16.refs_1_
  32.4 0.0 collective-permute-done.18.refs_3_
  32.4 0.3 gather.3
  32.7 3.7 %collective-permute-start.19 = (bf16[256,256]{1,0:T(8,128)(2,1)S(1)}, bf16[256,256]{1,0:T(8,128)(2,1)S(1)}, u32[]{:S(2)}, u32[]{:S(2)}) collective-permute-start(bf16[256,256]{1,0:T(8,128)(2,1)S(1)} %gather.3), channel_id=1, source_target_pairs={{0,12},{4,0},{8,4},{12,8},{1,13},{5,1},{9,5},{13,9},{2,14},{6,2},{... | collective-permute-start | bytes 393224 | tf_op jit(solution)/shard_map/ppermute | solution.py:269
  36.4 4.2 %collective-permute-done.19 = bf16[256,256]{1,0:T(8,128)(2,1)S(1)} collective-permute-done((bf16[256,256]{1,0:T(8,128)(2,1)S(1)}, bf16[256,256]{1,0:T(8,128)(2,1)S(1)}, u32[]{:S(2)}, u32[]{:S(2)}) %collective-permute-start.19) | collective-permute-done | bytes 131104 | tf_op jit(solution)/shard_map/ppermute | solution.py:269
  40.6 0.0 collective-permute-done.13
  40.6 0.8 %maximum_bitcast_fusion = bf16[1,256,640]{2,1,0:T(8,128)(2,1)} fusion(bf16[256,256]{1,0:T(8,128)(2,1)S(1)} %collective-permute-done.19, bf16[256,384]{1,0:T(8,128)(2,1)S(1)} %collective-permute-done.13), kind=kLoop, calls=%fused_computation | loop fusion | flops 655360 | bytes 655360 | tf_op jit(solution)/shard_map/broadcast_in_dim | solution.py:271
Async XLA Ops:
  0.0 17.0 %collective-permute-start.2 = (bf16[256,640]{1,0:T(8,128)(2,1)}, bf16[256,640]{1,0:T(8,128)(2,1)S(1)}, u32[]{:S(2)}, u32[]{:S(2)}) collective-permute-start(bf16[256,640]{1,0:T(8,128)(2,1)} %bitcast.7), channel_id=1, source_target_pairs={{0,4},{4,0},{8,12},{12,8},{1,5},{5,1},{9,13},{13,9},{2,6},{6,2},{1... | collective-permute-start | bytes 983048 | tf_op jit(solution)/shard_map/ppermute | solution.py:245
  3.1 17.8 %collective-permute-start.3 = (bf16[256,640]{1,0:T(8,128)(2,1)}, bf16[256,640]{1,0:T(8,128)(2,1)S(1)}, u32[]{:S(2)}, u32[]{:S(2)}) collective-permute-start(bf16[256,640]{1,0:T(8,128)(2,1)} %bitcast.8), channel_id=1, source_target_pairs={{0,1},{1,0},{4,8},{5,9},{8,4},{9,5},{12,13},{13,12},{2,3},{3,2},{6... | collective-permute-start | bytes 983048 | tf_op jit(solution)/shard_map/ppermute | solution.py:246
  4.5 17.2 %collective-permute-start.8 = (bf16[256,384]{1,0:T(8,128)(2,1)S(1)}, bf16[256,384]{1,0:T(8,128)(2,1)S(1)}, u32[]{:S(2)}, u32[]{:S(2)}) collective-permute-start(bf16[256,384]{1,0:T(8,128)(2,1)S(1)} %get-tuple-element.35.refs_6_), channel_id=1, source_target_pairs={{0,1},{1,0},{2,3},{3,2},{4,5},{5,4},{6,7},{7,6},{8,9},{9,8},{10,11... | collective-permute-start | bytes 589832 | tf_op jit(solution)/shard_map/ppermute | solution.py:247
  5.1 11.5 %collective-permute-start.15 = (bf16[256,256]{1,0:T(8,128)(2,1)S(1)}, bf16[256,256]{1,0:T(8,128)(2,1)S(1)}, u32[]{:S(2)}, u32[]{:S(2)}) collective-permute-start(bf16[256,256]{1,0:T(8,128)(2,1)S(1)} %get-tuple-element.39.refs_6_), channel_id=1, source_target_pairs={{0,4},{4,0},{8,12},{12,8},{1,5},{5,1},{9,13},{13,9},{2,6},{6,2},{1... | collective-permute-start | bytes 393224 | tf_op jit(solution)/shard_map/ppermute | solution.py:245
  7.8 3.6 %collective-permute-start = (f32[2,256]{1,0:T(2,128)S(1)}, f32[2,256]{1,0:T(2,128)S(1)}, u32[]{:S(2)}, u32[]{:S(2)}) collective-permute-start(f32[2,256]{1,0:T(2,128)S(1)} %get-tuple-element.27.own_ref), channel_id=1, source_target_pairs={{0,2},{2,0},{1,3},{3,1},{4,6},{6,4},{5,7},{7,5},{8,10},{10,8},{9,1... | collective-permute-start | bytes 6152 | tf_op jit(solution)/shard_map/ppermute | solution.py:255
  11.6 3.6 %collective-permute-start.4 = (f32[1,256]{1,0:T(1,128)S(1)}, f32[1,256]{1,0:T(1,128)S(1)}, u32[]{:S(2)}, u32[]{:S(2)}) collective-permute-start(f32[1,256]{1,0:T(1,128)S(1)} %get-tuple-element.32), channel_id=1, source_target_pairs={{0,4},{4,0},{8,12},{12,8},{1,5},{5,1},{9,13},{13,9},{2,6},{6,2},{1... | collective-permute-start | bytes 3080 | tf_op jit(solution)/shard_map/ppermute | solution.py:245
  15.3 1.2 %collective-permute-start.5 = (f32[1,256]{1,0:T(1,128)S(1)}, f32[1,256]{1,0:T(1,128)S(1)}, u32[]{:S(2)}, u32[]{:S(2)}) collective-permute-start(f32[1,256]{1,0:T(1,128)S(1)} %get-tuple-element.32), channel_id=1, source_target_pairs={{0,1},{1,0},{4,8},{5,9},{8,4},{9,5},{12,13},{13,12},{2,3},{3,2},{6... | collective-permute-start | bytes 3080 | tf_op jit(solution)/shard_map/ppermute | solution.py:246
  16.4 4.8 %collective-permute-start.17 = (bf16[256,256]{1,0:T(8,128)(2,1)S(1)}, bf16[256,256]{1,0:T(8,128)(2,1)S(1)}, u32[]{:S(2)}, u32[]{:S(2)}) collective-permute-start(bf16[256,256]{1,0:T(8,128)(2,1)S(1)} %get-tuple-element.39.refs_6_), channel_id=1, source_target_pairs={{0,1},{1,0},{4,8},{5,9},{8,4},{9,5},{12,13},{13,12},{2,3},{3,2},{6... | collective-permute-start | bytes 393224 | tf_op jit(solution)/shard_map/ppermute | solution.py:246
  16.6 10.2 %collective-permute-start.1 = (bf16[256,640]{1,0:T(8,128)(2,1)S(1)}, bf16[256,640]{1,0:T(8,128)(2,1)S(1)}, u32[]{:S(2)}, u32[]{:S(2)}) collective-permute-start(bf16[256,640]{1,0:T(8,128)(2,1)S(1)} %get-tuple-element.31.refs_0_), channel_id=1, source_target_pairs={{0,1},{1,0},{2,3},{3,2},{4,5},{5,4},{6,7},{7,6},{8,9},{9,8},{10,11... | collective-permute-start | bytes 983048 | tf_op jit(solution)/shard_map/ppermute | solution.py:247
  17.0 9.4 %collective-permute-start.9 = (bf16[256,384]{1,0:T(8,128)(2,1)S(1)}, bf16[256,384]{1,0:T(8,128)(2,1)S(1)}, u32[]{:S(2)}, u32[]{:S(2)}) collective-permute-start(bf16[256,384]{1,0:T(8,128)(2,1)S(1)} %get-tuple-element.35.refs_6_), channel_id=1, source_target_pairs={{0,4},{4,0},{8,12},{12,8},{1,5},{5,1},{9,13},{13,9},{2,6},{6,2},{1... | collective-permute-start | bytes 589832 | tf_op jit(solution)/shard_map/ppermute | solution.py:245
  20.8 5.5 %collective-permute-start.11 = (bf16[256,384]{1,0:T(8,128)(2,1)S(1)}, bf16[256,384]{1,0:T(8,128)(2,1)S(1)}, u32[]{:S(2)}, u32[]{:S(2)}) collective-permute-start(bf16[256,384]{1,0:T(8,128)(2,1)S(1)} %get-tuple-element.35.refs_6_), channel_id=1, source_target_pairs={{0,1},{1,0},{4,8},{5,9},{8,4},{9,5},{12,13},{13,12},{2,3},{3,2},{6... | collective-permute-start | bytes 589832 | tf_op jit(solution)/shard_map/ppermute | solution.py:246
  21.2 5.7 %collective-permute-start.6 = (bf16[256,640]{1,0:T(8,128)(2,1)S(1)}, bf16[256,640]{1,0:T(8,128)(2,1)S(1)}, u32[]{:S(2)}, u32[]{:S(2)}) collective-permute-start(bf16[256,640]{1,0:T(8,128)(2,1)S(1)} %get-tuple-element.33.refs_2_), channel_id=1, source_target_pairs={{0,1},{1,0},{2,3},{3,2},{4,5},{5,4},{6,7},{7,6},{8,9},{9,8},{10,11... | collective-permute-start | bytes 983048 | tf_op jit(solution)/shard_map/ppermute | solution.py:247
  21.7 5.7 %collective-permute-start.7 = (bf16[256,640]{1,0:T(8,128)(2,1)S(1)}, bf16[256,640]{1,0:T(8,128)(2,1)S(1)}, u32[]{:S(2)}, u32[]{:S(2)}) collective-permute-start(bf16[256,640]{1,0:T(8,128)(2,1)S(1)} %get-tuple-element.34.refs_4_), channel_id=1, source_target_pairs={{0,1},{1,0},{2,3},{3,2},{4,5},{5,4},{6,7},{7,6},{8,9},{9,8},{10,11... | collective-permute-start | bytes 983048 | tf_op jit(solution)/shard_map/ppermute | solution.py:247
  26.3 3.2 %collective-permute-start.10 = (bf16[256,384]{1,0:T(8,128)(2,1)S(1)}, bf16[256,384]{1,0:T(8,128)(2,1)S(1)}, u32[]{:S(2)}, u32[]{:S(2)}) collective-permute-start(bf16[256,384]{1,0:T(8,128)(2,1)S(1)} %collective-permute-done.9.refs_0_), channel_id=1, source_target_pairs={{0,1},{1,0},{2,3},{3,2},{4,5},{5,4},{6,7},{7,6},{8,9},{9,8},{10,11... | collective-permute-start | bytes 589832 | tf_op jit(solution)/shard_map/ppermute | solution.py:247
  26.3 3.2 %collective-permute-start.12 = (bf16[256,384]{1,0:T(8,128)(2,1)S(1)}, bf16[256,384]{1,0:T(8,128)(2,1)S(1)}, u32[]{:S(2)}, u32[]{:S(2)}) collective-permute-start(bf16[256,384]{1,0:T(8,128)(2,1)S(1)} %collective-permute-done.11.refs_2_), channel_id=1, source_target_pairs={{0,1},{1,0},{2,3},{3,2},{4,5},{5,4},{6,7},{7,6},{8,9},{9,8},{10,11... | collective-permute-start | bytes 589832 | tf_op jit(solution)/shard_map/ppermute | solution.py:247
  26.8 4.5 %collective-permute-start.14 = (bf16[256,256]{1,0:T(8,128)(2,1)S(1)}, bf16[256,256]{1,0:T(8,128)(2,1)S(1)}, u32[]{:S(2)}, u32[]{:S(2)}) collective-permute-start(bf16[256,256]{1,0:T(8,128)(2,1)S(1)} %get-tuple-element.39.refs_6_), channel_id=1, source_target_pairs={{0,1},{1,0},{2,3},{3,2},{4,5},{5,4},{6,7},{7,6},{8,9},{9,8},{10,11... | collective-permute-start | bytes 393224 | tf_op jit(solution)/shard_map/ppermute | solution.py:247
  26.9 5.4 %collective-permute-start.16 = (bf16[256,256]{1,0:T(8,128)(2,1)S(1)}, bf16[256,256]{1,0:T(8,128)(2,1)S(1)}, u32[]{:S(2)}, u32[]{:S(2)}) collective-permute-start(bf16[256,256]{1,0:T(8,128)(2,1)S(1)} %collective-permute-done.15.refs_0_), channel_id=1, source_target_pairs={{0,1},{1,0},{2,3},{3,2},{4,5},{5,4},{6,7},{7,6},{8,9},{9,8},{10,11... | collective-permute-start | bytes 393224 | tf_op jit(solution)/shard_map/ppermute | solution.py:247
  27.4 5.0 %collective-permute-start.18 = (bf16[256,256]{1,0:T(8,128)(2,1)S(1)}, bf16[256,256]{1,0:T(8,128)(2,1)S(1)}, u32[]{:S(2)}, u32[]{:S(2)}) collective-permute-start(bf16[256,256]{1,0:T(8,128)(2,1)S(1)} %collective-permute-done.17.refs_2_), channel_id=1, source_target_pairs={{0,1},{1,0},{2,3},{3,2},{4,5},{5,4},{6,7},{7,6},{8,9},{9,8},{10,11... | collective-permute-start | bytes 393224 | tf_op jit(solution)/shard_map/ppermute | solution.py:247
  29.9 10.6 %collective-permute-start.13 = (bf16[256,384]{1,0:T(8,128)(2,1)S(1)}, bf16[256,384]{1,0:T(8,128)(2,1)S(1)}, u32[]{:S(2)}, u32[]{:S(2)}) collective-permute-start(bf16[256,384]{1,0:T(8,128)(2,1)S(1)} %gather.2), channel_id=1, source_target_pairs={{0,12},{4,0},{8,4},{12,8},{1,13},{5,1},{9,5},{13,9},{2,14},{6,2},{... | collective-permute-start | bytes 589832 | tf_op jit(solution)/shard_map/ppermute | solution.py:269
  32.7 7.9 %collective-permute-start.19 = (bf16[256,256]{1,0:T(8,128)(2,1)S(1)}, bf16[256,256]{1,0:T(8,128)(2,1)S(1)}, u32[]{:S(2)}, u32[]{:S(2)}) collective-permute-start(bf16[256,256]{1,0:T(8,128)(2,1)S(1)} %gather.3), channel_id=1, source_target_pairs={{0,12},{4,0},{8,4},{12,8},{1,13},{5,1},{9,5},{13,9},{2,14},{6,2},{... | collective-permute-start | bytes 393224 | tf_op jit(solution)/shard_map/ppermute | solution.py:269

commit v3 on v2

--- a/solution.py
+++ b/solution.py
@@ -17,6 +17,7 @@
 LIMIT = 8 << 20
 VMEM = pl.BlockSpec(memory_space=pltpu.VMEM)
 HBM = pl.BlockSpec(memory_space=pltpu.HBM)
+ANY = pl.BlockSpec(memory_space=pl.ANY)
 COPY_PARTS = 4
 SMEM = pl.BlockSpec(memory_space=pltpu.SMEM)
 
@@ -35,51 +36,70 @@
     return jnp.sum(total.T, axis=0, keepdims=True)
 
 
-def load_kernel(parts, *refs):
-    query_hbm, key_hbm, value_hbm, *small_hbm = refs[:6]
-    query_ref, key_ref, square_ref, *others = refs[6:-1]
-    small_refs, value_refs, sems = others[:3], others[3:], refs[-1]
+def squares_kernel(query_hbm, key_hbm, query_ref, key_ref, out_ref, sems):
     copies = []
-
-    def copy(source, target):
-        copies.append(pltpu.make_async_copy(source, target, sems.at[len(copies)]))
-
-    step = query_hbm.shape[0] // parts
-    for source, target in ((query_hbm, query_ref), (key_hbm, key_ref)):
-        for part in range(parts):
-            copy(source.at[pl.ds(part * step, step)], target.at[pl.ds(part * step, step)])
-    for source, target in zip(small_hbm, small_refs):
-        copy(source, target)
+    for which, (source, target) in enumerate(((query_hbm, query_ref), (key_hbm, key_ref))):
+        step = source.shape[0] // COPY_PARTS
+        for part in range(COPY_PARTS):
+            rows = pl.ds(part * step, step)
+            copies.append(pltpu.make_async_copy(source.at[rows], target.at[rows], sems.at[which, part]))
+    for copy in copies:
+        copy.start()
+    for which, ref in enumerate((query_ref, key_ref)):
+        for copy in copies[which * COPY_PARTS : (which + 1) * COPY_PARTS]:
+            copy.wait()
+        out_ref[which : which + 1, :] = row_square_sums(ref)
+
+
+def squares(query, key):
+    rows, width = query.shape
+    kept = jax.ShapeDtypeStruct((rows, width), query.dtype)
+    return pl.pallas_call(
+        squares_kernel,
+        out_shape=[kept, kept, jax.ShapeDtypeStruct((2, rows), jnp.float32)],
+        in_specs=[HBM, HBM],
+        out_specs=[VMEM] * 3,
+        scratch_shapes=[pltpu.SemaphoreType.DMA((2, COPY_PARTS))],
+        name="squares",
+        compiler_params=pltpu.CompilerParams(vmem_limit_bytes=LIMIT),
+    )(*(pltpu.with_memory_space_constraint(x, pltpu.HBM) for x in (query, key)))
+
+
+def load_kernel(value_hbm, qgain_hbm, kgain_hbm, gate_hbm, levels_hbm, *refs):
+    qgain_ref, kgain_ref, gate_ref, *value_refs = refs[:-3]
+    table, level, sems = refs[-3:]
+    pairs = [(levels_hbm, level), (gate_hbm, table), (qgain_hbm, qgain_ref), (kgain_hbm, kgain_ref)]
     column = 0
     for target in value_refs:
-        copy(value_hbm.at[:, pl.ds(column, target.shape[1])], target)
+        pairs.append((value_hbm.at[:, pl.ds(column, target.shape[1])], target))
         column += target.shape[1]
-    for started in copies:
-        started.start()
-    for which, ref in enumerate((query_ref, key_ref)):
-        for started in copies[which * parts : (which + 1) * parts]:
-            started.wait()
-        square_ref[which : which + 1, :] = row_square_sums(ref)
-    for started in copies[2 * parts :]:
-        started.wait()
-
-
-def load(query, key, value, query_gain, key_gain, gate_table, widths):
-    rows, width = query.shape
-    whole = jax.ShapeDtypeStruct((rows, width), query.dtype)
-    sources = (query, key, value, query_gain, key_gain, gate_table)
-    shapes = [whole, whole, jax.ShapeDtypeStruct((2, rows), jnp.float32)]
-    shapes += [jax.ShapeDtypeStruct(x.shape, x.dtype) for x in sources[3:]]
+    copies = [pltpu.make_async_copy(*pair, sems.at[i]) for i, pair in enumerate(pairs)]
+    for copy in copies:
+        copy.start()
+    for copy in copies:
+        copy.wait()
+    gate_ref[...] = table[pl.ds(level[0], 1), :]
+
+
+def load(value, query_gain, key_gain, gate_table, levels, widths):
+    rows, width = value.shape
+    gain = jax.ShapeDtypeStruct(query_gain.shape, query_gain.dtype)
+    shapes = [gain, gain, jax.ShapeDtypeStruct((1, width), gate_table.dtype)]
     shapes += [jax.ShapeDtypeStruct((rows, chunk), value.dtype) for chunk in widths]
-    return pl.pallas_call(
-        functools.partial(load_kernel, COPY_PARTS),
+    sources = (value, query_gain, key_gain, gate_table)
+    return pl.pallas_call(
+        load_kernel,
         out_shape=shapes,
-        in_specs=[HBM] * 6,
+        in_specs=[HBM] * 4 + [ANY],
         out_specs=[VMEM] * len(shapes),
-        scratch_shapes=[pltpu.SemaphoreType.DMA((2 * COPY_PARTS + 3 + len(widths),))],
+        scratch_shapes=[
+            pltpu.VMEM(gate_table.shape, gate_table.dtype),
+            pltpu.SMEM(levels.shape, levels.dtype),
+            pltpu.SemaphoreType.DMA((4 + len(widths),)),
+        ],
         name="load",
         compiler_params=pltpu.CompilerParams(vmem_limit_bytes=LIMIT),
-    )(*(pltpu.with_memory_space_constraint(x, pltpu.HBM) for x in sources))
+    )(*(pltpu.with_memory_space_constraint(x, pltpu.HBM) for x in sources), levels)
 
 
 def apply_norm(ref, factor, gain_ref, out_ref):
@@ -194,10 +214,9 @@
     )(query, *keys, *values)
 
 
-def gather_kernel(column, level_ref, gate_ref, weight_ref, sum_ref, own_ref, *refs):
+def gather_kernel(column, gate_ref, weight_ref, sum_ref, own_ref, *refs):
     values, out_ref = refs[0:4], refs[4]
     rows = out_ref.shape[0]
-    gate = gate_ref[pl.ds(level_ref[0], 1), :]
 
     def work(used):
         for head in range(out_ref.shape[1] // DH):
@@ -210,23 +229,45 @@
                     values[block][:, here],
                     preferred_element_type=jnp.float32,
                 )
-            out_ref[:, here] = (gate[:, there] * (summed / sum_ref[:, here])).astype(jnp.bfloat16)
+            out_ref[:, here] = (gate_ref[:, there] * (summed / sum_ref[:, here])).astype(jnp.bfloat16)
 
     with_used_blocks(work)
 
 
-def gather(column, width, levels, gate_table, weights, sums, own, values):
+def gather(column, width, gate, weights, sums, own, values):
     rows = own.shape[0]
     count = 4 * rows * width * rows
     return pl.pallas_call(
         functools.partial(gather_kernel, column),
         out_shape=jax.ShapeDtypeStruct((rows, width), jnp.bfloat16),
-        in_specs=[SMEM] + [VMEM] * 8,
+        in_specs=[VMEM] * 8,
         out_specs=VMEM,
         name="gather",
         compiler_params=pltpu.CompilerParams(vmem_limit_bytes=LIMIT),
         cost_estimate=pl.CostEstimate(flops=2 * count, bytes_accessed=26 * rows * width, transcendentals=0),
-    )(levels, gate_table, weights, sums, own, *values)
+    )(gate, weights, sums, own, *values)
+
+
+def put_kernel(column, part_ref, *refs):
+    out_ref, sem = refs[-2:]
+    copy = pltpu.make_async_copy(part_ref, out_ref.at[:, pl.ds(column, part_ref.shape[1])], sem)
+    copy.start()
+    copy.wait()
+
+
+def put(part, column, whole, width):
+    rows = part.shape[0]
+    kept = [] if whole is None else [whole]
+    return pl.pallas_call(
+        functools.partial(put_kernel, column),
+        out_shape=jax.ShapeDtypeStruct((rows, width), part.dtype),
+        in_specs=[VMEM] + [HBM] * len(kept),
+        out_specs=HBM,
+        scratch_shapes=[pltpu.SemaphoreType.DMA],
+        input_output_aliases={1: 0} if kept else {},
+        name="put",
+        compiler_params=pltpu.CompilerParams(vmem_limit_bytes=LIMIT),
+    )(part, *kept)
 
 
 def body(query_input, key_input, value_input, query_gain, key_gain, gate_table, levels):
@@ -248,9 +289,8 @@
 
     query, key, value = query_input[0], key_input[0], value_input[0]
     key_first, key_second = first(key), second(key)
-    query, key, own, query_gain, key_gain, gate_table, *value_parts = load(
-        query, key, value, query_gain, key_gain, gate_table, widths
-    )
+    query, key, own = squares(query, key)
+    query_gain, key_gain, gate, *value_parts = load(value, query_gain, key_gain, gate_table, levels, widths)
     if tp == 2:
         other = lax.ppermute(own, "tp", [(0, 1), (1, 0)])
     else:
@@ -265,10 +305,14 @@
         part_first, part_second = first(part), second(part)
         weights, sums, own = scores(column, chunk, query_normed, keys, [part, swap(part)])
         beside = [part_first, swap(part_first), part_second, swap(part_second)]
-        gated = gather(column, chunk, levels, gate_table, weights, sums, own, beside)
+        gated = gather(column, chunk, gate, weights, sums, own, beside)
         outputs.append(lax.ppermute(gated, "queue", roll_pairs))
         column += chunk
-    return jnp.concatenate(outputs, axis=1)[None]
+    whole, column = None, 0
+    for part in outputs:
+        whole = put(part, column, whole, width)
+        column += part.shape[1]
+    return whole[None]
 
 
 def solution(mesh):

time: 41.5 us -> 42.2 us (1.017)
  Pallas kernels: 5.06 us -> 7.5 us
  starting transfers between devices: 19.2 us -> 18.3 us
  other arithmetic: 0.76 us -> 0 us
    pallas_call x1 -> x4, Pallas kernels: 1.44 us -> 3.89 us  [the longest x1 1.37 us: squares(): pl.pallas_call(squares_kernel, out_shape=[kept, kept, jax.ShapeDtypeStruc...]
    ppermute x4, starting transfers between devices: 9.77 us -> 8.72 us  [body(): first = lambda x: lax.ppermute(x, 'queue', first_pairs)]
    broadcast_in_dim x1 -> x0, other arithmetic: 0.76 us -> none  [body(): return jnp.concatenate(outputs, axis=1)[None]]
  transfers between devices with their start and end apart: 20 -> 20, of which waited for: 5 -> 6; matrix products, arithmetic and copies ran while one was open for 0% -> 0% of each run, Pallas kernels for 12% -> 16%
where the time goes in v3:
time: 42.2 us; the launch traced here: 42 us
  starting transfers between devices  18.3 us (43%)
  waiting for transfers between devices  15.4 us (36%)
  Pallas kernels  7.5 us (18%)
  between operations  0.78 us (2%)
    ppermute x4, starting transfers between devices, body(): first = lambda x: lax.ppermute(x, 'queue', first_pairs)  8.72 us
    ppermute x4, waiting for transfers between devices, body(): first = lambda x: lax.ppermute(x, 'queue', first_pairs)  8.07 us
    ppermute x2, starting transfers between devices, body(): outputs.append(lax.ppermute(gated, 'queue', roll_pairs))  5.07 us
    ppermute x2, waiting for transfers between devices, body(): outputs.append(lax.ppermute(gated, 'queue', roll_pairs))  4.08 us
    ppermute x9, starting transfers between devices, body(): swap = lambda x: lax.ppermute(x, 'seq', swap_pairs)  2.58 us
    pallas_call x2, Pallas kernels, scores(): pl.pallas_call(functools.partial(scores_kernel, column), out_shape=[jax.S...  2.44 us
    ppermute x1, waiting for transfers between devices, body(): other = lax.ppermute(own, 'tp', [(0, 1), (1, 0)])  2.09 us
    ppermute x1, starting transfers between devices, body(): other = lax.ppermute(own, 'tp', [(0, 1), (1, 0)])  1.56 us
  transfers between devices with their start and end apart: 20, of which 6 were waited for; matrix products, arithmetic and copies ran while one was open for 0% of the time, Pallas kernels for 16%

profile of v3, /device:TPU:0, one launch (start us, length us, event | category | flops | bytes accessed | tf_op | source)
XLA Modules:
  0.0 42.0 jit_solution(15091930231995358832)
XLA Ops:
  0.0 3.1 %collective-permute-start.2 = (bf16[256,640]{1,0:T(8,128)(2,1)}, bf16[256,640]{1,0:T(8,128)(2,1)S(1)}, u32[]{:S(2)}, u32[]{:S(2)}) collective-permute-start(bf16[256,640]{1,0:T(8,128)(2,1)} %bitcast.6), channel_id=1, source_target_pairs={{0,4},{4,0},{8,12},{12,8},{1,5},{5,1},{9,13},{13,9},{2,6},{6,2},{1... | collective-permute-start | bytes 983048 | tf_op jit(solution)/shard_map/ppermute | solution.py:286
  3.1 0.0 collective-permute-start.3
  3.7 1.2 %load.1 = (f32[640]{0:T(1024)S(1)}, f32[640]{0:T(1024)S(1)}, f32[1,640]{1,0:T(1,128)S(1)}, bf16[256,384]{1,0:T(8,128)(2,1)S(1)}, bf16[256,256]{1,0:T(8,128)(2,1)S(1)}) custom-call(bf16[256,640]{1,0:T(8,128)(2,1)} %bitcast.4, f32[640]{0:T(1024)} %qgain_hbm.1, f32[640]{0:T(1024)} %kgain_hbm.1, f32[64,640]{1,0:T(8,128)} %gate_hbm.1, s32[1]{0:T(128)S(6)} %copy.10.levels_hbm), custom_call_target="tpu_custom_call" | custom-call | tf_op jit(solution)/shard_map/load/pallas_call | solution.py:90
  4.9 0.6 %collective-permute-start.14 = (bf16[256,384]{1,0:T(8,128)(2,1)S(1)}, bf16[256,384]{1,0:T(8,128)(2,1)S(1)}, u32[]{:S(2)}, u32[]{:S(2)}) collective-permute-start(bf16[256,384]{1,0:T(8,128)(2,1)S(1)} %get-tuple-element.39.refs_6_), channel_id=1, source_target_pairs={{0,1},{1,0},{2,3},{3,2},{4,5},{5,4},{6,7},{7,6},{8,9},{9,8},{10,11... | collective-permute-start | bytes 589832 | tf_op jit(solution)/shard_map/ppermute | solution.py:288
  5.5 2.7 %collective-permute-start.9 = (bf16[256,256]{1,0:T(8,128)(2,1)S(1)}, bf16[256,256]{1,0:T(8,128)(2,1)S(1)}, u32[]{:S(2)}, u32[]{:S(2)}) collective-permute-start(bf16[256,256]{1,0:T(8,128)(2,1)S(1)} %get-tuple-element.35.refs_6_), channel_id=1, source_target_pairs={{0,4},{4,0},{8,12},{12,8},{1,5},{5,1},{9,13},{13,9},{2,6},{6,2},{1... | collective-permute-start | bytes 393224 | tf_op jit(solution)/shard_map/ppermute | solution.py:286
  8.2 1.4 %squares.1 = (bf16[256,640]{1,0:T(8,128)(2,1)S(1)}, bf16[256,640]{1,0:T(8,128)(2,1)S(1)}, f32[2,256]{1,0:T(2,128)S(1)}) custom-call(bf16[256,640]{1,0:T(8,128)(2,1)} %bitcast.5, bf16[256,640]{1,0:T(8,128)(2,1)} %bitcast.8), custom_call_target="tpu_custom_call" | custom-call | tf_op jit(solution)/shard_map/squares/pallas_call | solution.py:57
  9.6 1.6 %collective-permute-start = (f32[2,256]{1,0:T(2,128)S(1)}, f32[2,256]{1,0:T(2,128)S(1)}, u32[]{:S(2)}, u32[]{:S(2)}) collective-permute-start(f32[2,256]{1,0:T(2,128)S(1)} %get-tuple-element.27.own_ref), channel_id=1, source_target_pairs={{0,2},{2,0},{1,3},{3,1},{4,6},{6,4},{5,7},{7,5},{8,10},{10,8},{9,1... | collective-permute-start | bytes 6152 | tf_op jit(solution)/shard_map/ppermute | solution.py:295
  11.1 2.1 %collective-permute-done.other_ref = f32[2,256]{1,0:T(2,128)S(1)} collective-permute-done((f32[2,256]{1,0:T(2,128)S(1)}, f32[2,256]{1,0:T(2,128)S(1)}, u32[]{:S(2)}, u32[]{:S(2)}) %collective-permute-start) | collective-permute-done | bytes 2080 | tf_op jit(solution)/shard_map/ppermute | solution.py:295
  13.2 0.2 normalize.1
  13.5 0.1 collective-permute-start.4
  13.6 3.6 %collective-permute-done.4.afactor_ref = f32[1,256]{1,0:T(1,128)S(1)} collective-permute-done((f32[1,256]{1,0:T(1,128)S(1)}, f32[1,256]{1,0:T(1,128)S(1)}, u32[]{:S(2)}, u32[]{:S(2)}) %collective-permute-start.4) | collective-permute-done | bytes 1056 | tf_op jit(solution)/shard_map/ppermute | solution.py:286
  17.1 0.0 collective-permute-start.5
  17.1 1.2 %collective-permute-done.5.bfactor_ref = f32[1,256]{1,0:T(1,128)S(1)} collective-permute-done((f32[1,256]{1,0:T(1,128)S(1)}, f32[1,256]{1,0:T(1,128)S(1)}, u32[]{:S(2)}, u32[]{:S(2)}) %collective-permute-start.5) | collective-permute-done | bytes 1056 | tf_op jit(solution)/shard_map/ppermute | solution.py:287
  18.3 0.2 collective-permute-start.11
  18.4 0.0 collective-permute-done.9.refs_0_
  18.4 0.3 collective-permute-start.1
  18.8 0.0 collective-permute-done.2.a_ref
  18.8 2.9 %collective-permute-start.15 = (bf16[256,384]{1,0:T(8,128)(2,1)S(1)}, bf16[256,384]{1,0:T(8,128)(2,1)S(1)}, u32[]{:S(2)}, u32[]{:S(2)}) collective-permute-start(bf16[256,384]{1,0:T(8,128)(2,1)S(1)} %get-tuple-element.39.refs_6_), channel_id=1, source_target_pairs={{0,4},{4,0},{8,12},{12,8},{1,5},{5,1},{9,13},{13,9},{2,6},{6,2},{1... | collective-permute-start | bytes 589832 | tf_op jit(solution)/shard_map/ppermute | solution.py:286
  21.6 0.0 collective-permute-done.3.b_ref
  21.7 0.2 collective-permute-start.17
  21.8 0.2 normalize_two.1
  22.1 0.0 collective-permute-done.11.refs_2_
  22.1 0.4 collective-permute-start.6
  22.5 0.0 collective-permute-done.14.refs_7_
  22.5 0.2 collective-permute-start.7
  22.6 4.5 %collective-permute-done.15.refs_0_ = bf16[256,384]{1,0:T(8,128)(2,1)S(1)} collective-permute-done((bf16[256,384]{1,0:T(8,128)(2,1)S(1)}, bf16[256,384]{1,0:T(8,128)(2,1)S(1)}, u32[]{:S(2)}, u32[]{:S(2)}) %collective-permute-start.15) | collective-permute-done | bytes 196640 | tf_op jit(solution)/shard_map/ppermute | solution.py:286
  27.2 0.0 collective-permute-start.16
  27.2 0.0 collective-permute-done.17.refs_2_
  27.2 0.5 %collective-permute-start.18 = (bf16[256,384]{1,0:T(8,128)(2,1)S(1)}, bf16[256,384]{1,0:T(8,128)(2,1)S(1)}, u32[]{:S(2)}, u32[]{:S(2)}) collective-permute-start(bf16[256,384]{1,0:T(8,128)(2,1)S(1)} %collective-permute-done.17.refs_2_), channel_id=1, source_target_pairs={{0,1},{1,0},{2,3},{3,2},{4,5},{5,4},{6,7},{7,6},{8,9},{9,8},{10,11... | collective-permute-start | bytes 589832 | tf_op jit(solution)/shard_map/ppermute | solution.py:288
  27.7 0.0 collective-permute-done.1.refs_1_
  27.7 0.1 collective-permute-start.8
  27.7 0.0 collective-permute-done.6.refs_3_
  27.7 0.4 %collective-permute-start.10 = (bf16[256,256]{1,0:T(8,128)(2,1)S(1)}, bf16[256,256]{1,0:T(8,128)(2,1)S(1)}, u32[]{:S(2)}, u32[]{:S(2)}) collective-permute-start(bf16[256,256]{1,0:T(8,128)(2,1)S(1)} %collective-permute-done.9.refs_0_), channel_id=1, source_target_pairs={{0,1},{1,0},{2,3},{3,2},{4,5},{5,4},{6,7},{7,6},{8,9},{9,8},{10,11... | collective-permute-start | bytes 393224 | tf_op jit(solution)/shard_map/ppermute | solution.py:288
  28.2 0.0 collective-permute-done.7.refs_5_
  28.2 0.1 collective-permute-start.12
  28.3 1.4 %scores.3 = (bf16[3,256,1024]{2,1,0:T(8,128)(2,1)S(1)}, f32[256,384]{1,0:T(8,128)S(1)}, f32[256,384]{1,0:T(8,128)S(1)}) custom-call(bf16[256,640]{1,0:T(8,128)(2,1)S(1)} %get-tuple-element.30.query_ref, bf16[256,640]{1,0:T(8,128)(2,1)S(1)} %get-tuple-element.31.refs_0_, bf16[256,640]{1,0:T(8,128)(2,1)S(1)} %collective-permute-done.1.refs_1_, ...), custom_call_target="tpu_custom_call" | custom-call | flops 452984832 | bytes 2555904 | tf_op jit(solution)/shard_map/scores/pallas_call | solution.py:202
  29.7 0.0 collective-permute-done.16.refs_1_
  29.7 0.4 gather.3
  30.1 2.1 %collective-permute-start.19 = (bf16[256,384]{1,0:T(8,128)(2,1)S(1)}, bf16[256,384]{1,0:T(8,128)(2,1)S(1)}, u32[]{:S(2)}, u32[]{:S(2)}) collective-permute-start(bf16[256,384]{1,0:T(8,128)(2,1)S(1)} %gather.3), channel_id=1, source_target_pairs={{0,12},{4,0},{8,4},{12,8},{1,13},{5,1},{9,5},{13,9},{2,14},{6,2},{... | collective-permute-start | bytes 589832 | tf_op jit(solution)/shard_map/ppermute | solution.py:309
  32.2 0.0 collective-permute-done.8.refs_7_
  32.2 1.0 %scores.2 = (bf16[2,256,1024]{2,1,0:T(8,128)(2,1)S(1)}, f32[256,256]{1,0:T(8,128)S(1)}, f32[256,256]{1,0:T(8,128)S(1)}) custom-call(bf16[256,640]{1,0:T(8,128)(2,1)S(1)} %get-tuple-element.30.query_ref, bf16[256,640]{1,0:T(8,128)(2,1)S(1)} %get-tuple-element.31.refs_0_, bf16[256,640]{1,0:T(8,128)(2,1)S(1)} %collective-permute-done.1.refs_1_, ...), custom_call_target="tpu_custom_call" | custom-call | flops 301989888 | bytes 1703936 | tf_op jit(solution)/shard_map/scores/pallas_call | solution.py:202
  33.3 0.0 collective-permute-done.12.refs_3_
  33.3 0.3 gather.2
  33.6 3.0 %collective-permute-start.13 = (bf16[256,256]{1,0:T(8,128)(2,1)S(1)}, bf16[256,256]{1,0:T(8,128)(2,1)S(1)}, u32[]{:S(2)}, u32[]{:S(2)}) collective-permute-start(bf16[256,256]{1,0:T(8,128)(2,1)S(1)} %gather.2), channel_id=1, source_target_pairs={{0,12},{4,0},{8,4},{12,8},{1,13},{5,1},{9,5},{13,9},{2,14},{6,2},{... | collective-permute-start | bytes 393224 | tf_op jit(solution)/shard_map/ppermute | solution.py:309
  36.5 2.6 %collective-permute-done.19.part_ref = bf16[256,384]{1,0:T(8,128)(2,1)S(1)} collective-permute-done((bf16[256,384]{1,0:T(8,128)(2,1)S(1)}, bf16[256,384]{1,0:T(8,128)(2,1)S(1)}, u32[]{:S(2)}, u32[]{:S(2)}) %collective-permute-start.19) | collective-permute-done | bytes 196640 | tf_op jit(solution)/shard_map/ppermute | solution.py:309
  39.1 0.7 %put.2.refs_0_ = bf16[256,640]{1,0:T(8,128)(2,1)} custom-call(bf16[256,384]{1,0:T(8,128)(2,1)S(1)} %collective-permute-done.19.part_ref), custom_call_target="tpu_custom_call" | custom-call | tf_op jit(solution)/shard_map/put/pallas_call | solution.py:261
  39.8 1.5 %collective-permute-done.13.part_ref = bf16[256,256]{1,0:T(8,128)(2,1)S(1)} collective-permute-done((bf16[256,256]{1,0:T(8,128)(2,1)S(1)}, bf16[256,256]{1,0:T(8,128)(2,1)S(1)}, u32[]{:S(2)}, u32[]{:S(2)}) %collective-permute-start.13) | collective-permute-done | bytes 131104 | tf_op jit(solution)/shard_map/ppermute | solution.py:309
  41.3 0.7 %put.3 = bf16[256,640]{1,0:T(8,128)(2,1)} custom-call(bf16[256,256]{1,0:T(8,128)(2,1)S(1)} %collective-permute-done.13.part_ref, bf16[256,640]{1,0:T(8,128)(2,1)} %put.2.refs_0_), custom_call_target="tpu_custom_call", output_to_operand_aliasing={{}: (1, {})} | custom-call | tf_op jit(solution)/shard_map/put/pallas_call | solution.py:261
  (2 shorter events, 0.0 us)
Async XLA Ops:
  0.0 18.8 %collective-permute-start.2 = (bf16[256,640]{1,0:T(8,128)(2,1)}, bf16[256,640]{1,0:T(8,128)(2,1)S(1)}, u32[]{:S(2)}, u32[]{:S(2)}) collective-permute-start(bf16[256,640]{1,0:T(8,128)(2,1)} %bitcast.6), channel_id=1, source_target_pairs={{0,4},{4,0},{8,12},{12,8},{1,5},{5,1},{9,13},{13,9},{2,6},{6,2},{1... | collective-permute-start | bytes 983048 | tf_op jit(solution)/shard_map/ppermute | solution.py:286
  3.1 18.6 %collective-permute-start.3 = (bf16[256,640]{1,0:T(8,128)(2,1)}, bf16[256,640]{1,0:T(8,128)(2,1)S(1)}, u32[]{:S(2)}, u32[]{:S(2)}) collective-permute-start(bf16[256,640]{1,0:T(8,128)(2,1)} %bitcast.7), channel_id=1, source_target_pairs={{0,1},{1,0},{4,8},{5,9},{8,4},{9,5},{12,13},{13,12},{2,3},{3,2},{6... | collective-permute-start | bytes 983048 | tf_op jit(solution)/shard_map/ppermute | solution.py:287
  4.9 17.6 %collective-permute-start.14 = (bf16[256,384]{1,0:T(8,128)(2,1)S(1)}, bf16[256,384]{1,0:T(8,128)(2,1)S(1)}, u32[]{:S(2)}, u32[]{:S(2)}) collective-permute-start(bf16[256,384]{1,0:T(8,128)(2,1)S(1)} %get-tuple-element.39.refs_6_), channel_id=1, source_target_pairs={{0,1},{1,0},{2,3},{3,2},{4,5},{5,4},{6,7},{7,6},{8,9},{9,8},{10,11... | collective-permute-start | bytes 589832 | tf_op jit(solution)/shard_map/ppermute | solution.py:288
  5.5 13.0 %collective-permute-start.9 = (bf16[256,256]{1,0:T(8,128)(2,1)S(1)}, bf16[256,256]{1,0:T(8,128)(2,1)S(1)}, u32[]{:S(2)}, u32[]{:S(2)}) collective-permute-start(bf16[256,256]{1,0:T(8,128)(2,1)S(1)} %get-tuple-element.35.refs_6_), channel_id=1, source_target_pairs={{0,4},{4,0},{8,12},{12,8},{1,5},{5,1},{9,13},{13,9},{2,6},{6,2},{1... | collective-permute-start | bytes 393224 | tf_op jit(solution)/shard_map/ppermute | solution.py:286
  9.6 3.7 %collective-permute-start = (f32[2,256]{1,0:T(2,128)S(1)}, f32[2,256]{1,0:T(2,128)S(1)}, u32[]{:S(2)}, u32[]{:S(2)}) collective-permute-start(f32[2,256]{1,0:T(2,128)S(1)} %get-tuple-element.27.own_ref), channel_id=1, source_target_pairs={{0,2},{2,0},{1,3},{3,1},{4,6},{6,4},{5,7},{7,5},{8,10},{10,8},{9,1... | collective-permute-start | bytes 6152 | tf_op jit(solution)/shard_map/ppermute | solution.py:295
  13.5 3.6 %collective-permute-start.4 = (f32[1,256]{1,0:T(1,128)S(1)}, f32[1,256]{1,0:T(1,128)S(1)}, u32[]{:S(2)}, u32[]{:S(2)}) collective-permute-start(f32[1,256]{1,0:T(1,128)S(1)} %get-tuple-element.32), channel_id=1, source_target_pairs={{0,4},{4,0},{8,12},{12,8},{1,5},{5,1},{9,13},{13,9},{2,6},{6,2},{1... | collective-permute-start | bytes 3080 | tf_op jit(solution)/shard_map/ppermute | solution.py:286
  17.1 1.2 %collective-permute-start.5 = (f32[1,256]{1,0:T(1,128)S(1)}, f32[1,256]{1,0:T(1,128)S(1)}, u32[]{:S(2)}, u32[]{:S(2)}) collective-permute-start(f32[1,256]{1,0:T(1,128)S(1)} %get-tuple-element.32), channel_id=1, source_target_pairs={{0,1},{1,0},{4,8},{5,9},{8,4},{9,5},{12,13},{13,12},{2,3},{3,2},{6... | collective-permute-start | bytes 3080 | tf_op jit(solution)/shard_map/ppermute | solution.py:287
  18.3 3.8 %collective-permute-start.11 = (bf16[256,256]{1,0:T(8,128)(2,1)S(1)}, bf16[256,256]{1,0:T(8,128)(2,1)S(1)}, u32[]{:S(2)}, u32[]{:S(2)}) collective-permute-start(bf16[256,256]{1,0:T(8,128)(2,1)S(1)} %get-tuple-element.35.refs_6_), channel_id=1, source_target_pairs={{0,1},{1,0},{4,8},{5,9},{8,4},{9,5},{12,13},{13,12},{2,3},{3,2},{6... | collective-permute-start | bytes 393224 | tf_op jit(solution)/shard_map/ppermute | solution.py:287
  18.4 9.2 %collective-permute-start.1 = (bf16[256,640]{1,0:T(8,128)(2,1)S(1)}, bf16[256,640]{1,0:T(8,128)(2,1)S(1)}, u32[]{:S(2)}, u32[]{:S(2)}) collective-permute-start(bf16[256,640]{1,0:T(8,128)(2,1)S(1)} %get-tuple-element.31.refs_0_), channel_id=1, source_target_pairs={{0,1},{1,0},{2,3},{3,2},{4,5},{5,4},{6,7},{7,6},{8,9},{9,8},{10,11... | collective-permute-start | bytes 983048 | tf_op jit(solution)/shard_map/ppermute | solution.py:288
  18.8 8.4 %collective-permute-start.15 = (bf16[256,384]{1,0:T(8,128)(2,1)S(1)}, bf16[256,384]{1,0:T(8,128)(2,1)S(1)}, u32[]{:S(2)}, u32[]{:S(2)}) collective-permute-start(bf16[256,384]{1,0:T(8,128)(2,1)S(1)} %get-tuple-element.39.refs_6_), channel_id=1, source_target_pairs={{0,4},{4,0},{8,12},{12,8},{1,5},{5,1},{9,13},{13,9},{2,6},{6,2},{1... | collective-permute-start | bytes 589832 | tf_op jit(solution)/shard_map/ppermute | solution.py:286
  21.7 5.5 %collective-permute-start.17 = (bf16[256,384]{1,0:T(8,128)(2,1)S(1)}, bf16[256,384]{1,0:T(8,128)(2,1)S(1)}, u32[]{:S(2)}, u32[]{:S(2)}) collective-permute-start(bf16[256,384]{1,0:T(8,128)(2,1)S(1)} %get-tuple-element.39.refs_6_), channel_id=1, source_target_pairs={{0,1},{1,0},{4,8},{5,9},{8,4},{9,5},{12,13},{13,12},{2,3},{3,2},{6... | collective-permute-start | bytes 589832 | tf_op jit(solution)/shard_map/ppermute | solution.py:287
  22.1 5.7 %collective-permute-start.6 = (bf16[256,640]{1,0:T(8,128)(2,1)S(1)}, bf16[256,640]{1,0:T(8,128)(2,1)S(1)}, u32[]{:S(2)}, u32[]{:S(2)}) collective-permute-start(bf16[256,640]{1,0:T(8,128)(2,1)S(1)} %get-tuple-element.33.refs_2_), channel_id=1, source_target_pairs={{0,1},{1,0},{2,3},{3,2},{4,5},{5,4},{6,7},{7,6},{8,9},{9,8},{10,11... | collective-permute-start | bytes 983048 | tf_op jit(solution)/shard_map/ppermute | solution.py:288
  22.5 5.7 %collective-permute-start.7 = (bf16[256,640]{1,0:T(8,128)(2,1)S(1)}, bf16[256,640]{1,0:T(8,128)(2,1)S(1)}, u32[]{:S(2)}, u32[]{:S(2)}) collective-permute-start(bf16[256,640]{1,0:T(8,128)(2,1)S(1)} %get-tuple-element.34.refs_4_), channel_id=1, source_target_pairs={{0,1},{1,0},{2,3},{3,2},{4,5},{5,4},{6,7},{7,6},{8,9},{9,8},{10,11... | collective-permute-start | bytes 983048 | tf_op jit(solution)/shard_map/ppermute | solution.py:288
  27.2 2.5 %collective-permute-start.16 = (bf16[256,384]{1,0:T(8,128)(2,1)S(1)}, bf16[256,384]{1,0:T(8,128)(2,1)S(1)}, u32[]{:S(2)}, u32[]{:S(2)}) collective-permute-start(bf16[256,384]{1,0:T(8,128)(2,1)S(1)} %collective-permute-done.15.refs_0_), channel_id=1, source_target_pairs={{0,1},{1,0},{2,3},{3,2},{4,5},{5,4},{6,7},{7,6},{8,9},{9,8},{10,11... | collective-permute-start | bytes 589832 | tf_op jit(solution)/shard_map/ppermute | solution.py:288
  27.2 2.5 %collective-permute-start.18 = (bf16[256,384]{1,0:T(8,128)(2,1)S(1)}, bf16[256,384]{1,0:T(8,128)(2,1)S(1)}, u32[]{:S(2)}, u32[]{:S(2)}) collective-permute-start(bf16[256,384]{1,0:T(8,128)(2,1)S(1)} %collective-permute-done.17.refs_2_), channel_id=1, source_target_pairs={{0,1},{1,0},{2,3},{3,2},{4,5},{5,4},{6,7},{7,6},{8,9},{9,8},{10,11... | collective-permute-start | bytes 589832 | tf_op jit(solution)/shard_map/ppermute | solution.py:288
  27.7 4.5 %collective-permute-start.8 = (bf16[256,256]{1,0:T(8,128)(2,1)S(1)}, bf16[256,256]{1,0:T(8,128)(2,1)S(1)}, u32[]{:S(2)}, u32[]{:S(2)}) collective-permute-start(bf16[256,256]{1,0:T(8,128)(2,1)S(1)} %get-tuple-element.35.refs_6_), channel_id=1, source_target_pairs={{0,1},{1,0},{2,3},{3,2},{4,5},{5,4},{6,7},{7,6},{8,9},{9,8},{10,11... | collective-permute-start | bytes 393224 | tf_op jit(solution)/shard_map/ppermute | solution.py:288
  27.7 5.5 %collective-permute-start.10 = (bf16[256,256]{1,0:T(8,128)(2,1)S(1)}, bf16[256,256]{1,0:T(8,128)(2,1)S(1)}, u32[]{:S(2)}, u32[]{:S(2)}) collective-permute-start(bf16[256,256]{1,0:T(8,128)(2,1)S(1)} %collective-permute-done.9.refs_0_), channel_id=1, source_target_pairs={{0,1},{1,0},{2,3},{3,2},{4,5},{5,4},{6,7},{7,6},{8,9},{9,8},{10,11... | collective-permute-start | bytes 393224 | tf_op jit(solution)/shard_map/ppermute | solution.py:288
  28.2 5.1 %collective-permute-start.12 = (bf16[256,256]{1,0:T(8,128)(2,1)S(1)}, bf16[256,256]{1,0:T(8,128)(2,1)S(1)}, u32[]{:S(2)}, u32[]{:S(2)}) collective-permute-start(bf16[256,256]{1,0:T(8,128)(2,1)S(1)} %collective-permute-done.11.refs_2_), channel_id=1, source_target_pairs={{0,1},{1,0},{2,3},{3,2},{4,5},{5,4},{6,7},{7,6},{8,9},{9,8},{10,11... | collective-permute-start | bytes 393224 | tf_op jit(solution)/shard_map/ppermute | solution.py:288
  30.1 9.0 %collective-permute-start.19 = (bf16[256,384]{1,0:T(8,128)(2,1)S(1)}, bf16[256,384]{1,0:T(8,128)(2,1)S(1)}, u32[]{:S(2)}, u32[]{:S(2)}) collective-permute-start(bf16[256,384]{1,0:T(8,128)(2,1)S(1)} %gather.3), channel_id=1, source_target_pairs={{0,12},{4,0},{8,4},{12,8},{1,13},{5,1},{9,5},{13,9},{2,14},{6,2},{... | collective-permute-start | bytes 589832 | tf_op jit(solution)/shard_map/ppermute | solution.py:309
  33.6 7.7 %collective-permute-start.13 = (bf16[256,256]{1,0:T(8,128)(2,1)S(1)}, bf16[256,256]{1,0:T(8,128)(2,1)S(1)}, u32[]{:S(2)}, u32[]{:S(2)}) collective-permute-start(bf16[256,256]{1,0:T(8,128)(2,1)S(1)} %gather.2), channel_id=1, source_target_pairs={{0,12},{4,0},{8,4},{12,8},{1,13},{5,1},{9,5},{13,9},{2,14},{6,2},{... | collective-permute-start | bytes 393224 | tf_op jit(solution)/shard_map/ppermute | solution.py:309

commit v4 on v3

--- a/solution.py
+++ b/solution.py
@@ -166,32 +166,39 @@
     weight_ref, sum_ref, own_ref = refs[8:]
     rows = query_ref.shape[0]
 
+    heads = weight_ref.shape[0]
+
+    def score(head, used):
+        there = slice(column + head * DH, column + (head + 1) * DH)
+        head_query = query_ref[:, there]
+        return [
+            lax.dot_general(
+                head_query, key_ref[:, there], (((1,), (1,)), ((), ())), preferred_element_type=jnp.float32
+            )
+            for key_ref in keys[:used]
+        ]
+
     def work(used):
-        for head in range(weight_ref.shape[0]):
+        later = score(0, used)
+        for head in range(heads):
             here = slice(head * DH, (head + 1) * DH)
-            there = slice(column + head * DH, column + (head + 1) * DH)
-            head_query = query_ref[:, there]
-            scores = [
-                lax.dot_general(
-                    head_query, key_ref[:, there], (((1,), (1,)), ((), ())), preferred_element_type=jnp.float32
-                )
-                for key_ref in keys[:used]
-            ]
-            row_max = jnp.max(functools.reduce(jnp.maximum, scores), axis=1, keepdims=True)
+            now = later
+            row_max = jnp.max(functools.reduce(jnp.maximum, now), axis=1, keepdims=True)
+            if head + 1 < heads:
+                later = score(head + 1, used)
             shift = row_max * SCALE
-            weights = [jnp.exp2(part * SCALE - shift) for part in scores]
-            weight_sum = jnp.sum(functools.reduce(jnp.add, weights), axis=1, keepdims=True)
-            sum_ref[:, here] = jnp.broadcast_to(weight_sum, (rows, DH))
-            low = [part.astype(jnp.bfloat16) for part in weights]
-            for block in range(2, used):
-                weight_ref[head, :, (block - 2) * rows : (block - 1) * rows] = low[block]
-            own_ref[:, here] = functools.reduce(
-                jnp.add,
-                [
-                    jnp.dot(part, value_ref[:, here], preferred_element_type=jnp.float32)
-                    for part, value_ref in zip(low, values)
-                ],
-            )
+            total, own = None, None
+            for block, part in enumerate(now):
+                weights = jnp.exp2(part * SCALE - shift)
+                total = weights if total is None else total + weights
+                low = weights.astype(jnp.bfloat16)
+                if block < 2:
+                    product = jnp.dot(low, values[block][:, here], preferred_element_type=jnp.float32)
+                    own = product if own is None else own + product
+                else:
+                    weight_ref[head, :, (block - 2) * rows : (block - 1) * rows] = low
+            sum_ref[:, here] = jnp.broadcast_to(jnp.sum(total, axis=1, keepdims=True), (rows, DH))
+            own_ref[:, here] = own
 
     with_used_blocks(work)
 

time: 42.2 us -> 42 us (level)
  Pallas kernels: 7.5 us -> 7.07 us
    pallas_call x2, Pallas kernels: 2.44 us -> 2.01 us  [scores(): pl.pallas_call(functools.partial(scores_kernel, column), out_shape=[jax.S...]
  transfers between devices with their start and end apart: 20 -> 20, of which waited for: 6 -> 6; matrix products, arithmetic and copies ran while one was open for 0% -> 0% of each run, Pallas kernels for 16% -> 15%
where the time goes in v4:
time: 42 us; the launch traced here: 41.8 us
  starting transfers between devices  18.4 us (44%)
  waiting for transfers between devices  15.6 us (37%)
  Pallas kernels  7.07 us (17%)
  between operations  0.77 us (2%)
    ppermute x4, starting transfers between devices, body(): first = lambda x: lax.ppermute(x, 'queue', first_pairs)  8.72 us
    ppermute x4, waiting for transfers between devices, body(): first = lambda x: lax.ppermute(x, 'queue', first_pairs)  8.07 us
    ppermute x2, starting transfers between devices, body(): outputs.append(lax.ppermute(gated, 'queue', roll_pairs))  5.18 us
    ppermute x2, waiting for transfers between devices, body(): outputs.append(lax.ppermute(gated, 'queue', roll_pairs))  4.24 us
    ppermute x9, starting transfers between devices, body(): swap = lambda x: lax.ppermute(x, 'seq', swap_pairs)  2.58 us
    ppermute x1, waiting for transfers between devices, body(): other = lax.ppermute(own, 'tp', [(0, 1), (1, 0)])  2.09 us
    pallas_call x2, Pallas kernels, scores(): pl.pallas_call(functools.partial(scores_kernel, column), out_shape=[jax.S...  2.01 us
    ppermute x1, starting transfers between devices, body(): other = lax.ppermute(own, 'tp', [(0, 1), (1, 0)])  1.56 us
  transfers between devices with their start and end apart: 20, of which 6 were waited for; matrix products, arithmetic and copies ran while one was open for 0% of the time, Pallas kernels for 15%

profile of v4, /device:TPU:0, one launch (start us, length us, event | category | flops | bytes accessed | tf_op | source)
XLA Modules:
  0.0 41.8 jit_solution(1528031661096988041)
XLA Ops:
  0.0 3.1 %collective-permute-start.2 = (bf16[256,640]{1,0:T(8,128)(2,1)}, bf16[256,640]{1,0:T(8,128)(2,1)S(1)}, u32[]{:S(2)}, u32[]{:S(2)}) collective-permute-start(bf16[256,640]{1,0:T(8,128)(2,1)} %bitcast.6), channel_id=1, source_target_pairs={{0,4},{4,0},{8,12},{12,8},{1,5},{5,1},{9,13},{13,9},{2,6},{6,2},{1... | collective-permute-start | bytes 983048 | tf_op jit(solution)/shard_map/ppermute | solution.py:293
  3.1 0.0 collective-permute-start.3
  3.7 1.2 %load.1 = (f32[640]{0:T(1024)S(1)}, f32[640]{0:T(1024)S(1)}, f32[1,640]{1,0:T(1,128)S(1)}, bf16[256,384]{1,0:T(8,128)(2,1)S(1)}, bf16[256,256]{1,0:T(8,128)(2,1)S(1)}) custom-call(bf16[256,640]{1,0:T(8,128)(2,1)} %bitcast.4, f32[640]{0:T(1024)} %qgain_hbm.1, f32[640]{0:T(1024)} %kgain_hbm.1, f32[64,640]{1,0:T(8,128)} %gate_hbm.1, s32[1]{0:T(128)S(6)} %copy.10.levels_hbm), custom_call_target="tpu_custom_call" | custom-call | tf_op jit(solution)/shard_map/load/pallas_call | solution.py:90
  4.9 0.6 %collective-permute-start.14 = (bf16[256,384]{1,0:T(8,128)(2,1)S(1)}, bf16[256,384]{1,0:T(8,128)(2,1)S(1)}, u32[]{:S(2)}, u32[]{:S(2)}) collective-permute-start(bf16[256,384]{1,0:T(8,128)(2,1)S(1)} %get-tuple-element.39.refs_6_), channel_id=1, source_target_pairs={{0,1},{1,0},{2,3},{3,2},{4,5},{5,4},{6,7},{7,6},{8,9},{9,8},{10,11... | collective-permute-start | bytes 589832 | tf_op jit(solution)/shard_map/ppermute | solution.py:295
  5.5 2.7 %collective-permute-start.9 = (bf16[256,256]{1,0:T(8,128)(2,1)S(1)}, bf16[256,256]{1,0:T(8,128)(2,1)S(1)}, u32[]{:S(2)}, u32[]{:S(2)}) collective-permute-start(bf16[256,256]{1,0:T(8,128)(2,1)S(1)} %get-tuple-element.35.refs_6_), channel_id=1, source_target_pairs={{0,4},{4,0},{8,12},{12,8},{1,5},{5,1},{9,13},{13,9},{2,6},{6,2},{1... | collective-permute-start | bytes 393224 | tf_op jit(solution)/shard_map/ppermute | solution.py:293
  8.2 1.4 %squares.1 = (bf16[256,640]{1,0:T(8,128)(2,1)S(1)}, bf16[256,640]{1,0:T(8,128)(2,1)S(1)}, f32[2,256]{1,0:T(2,128)S(1)}) custom-call(bf16[256,640]{1,0:T(8,128)(2,1)} %bitcast.5, bf16[256,640]{1,0:T(8,128)(2,1)} %bitcast.8), custom_call_target="tpu_custom_call" | custom-call | tf_op jit(solution)/shard_map/squares/pallas_call | solution.py:57
  9.6 1.6 %collective-permute-start = (f32[2,256]{1,0:T(2,128)S(1)}, f32[2,256]{1,0:T(2,128)S(1)}, u32[]{:S(2)}, u32[]{:S(2)}) collective-permute-start(f32[2,256]{1,0:T(2,128)S(1)} %get-tuple-element.27.own_ref), channel_id=1, source_target_pairs={{0,2},{2,0},{1,3},{3,1},{4,6},{6,4},{5,7},{7,5},{8,10},{10,8},{9,1... | collective-permute-start | bytes 6152 | tf_op jit(solution)/shard_map/ppermute | solution.py:302
  11.1 2.1 %collective-permute-done.other_ref = f32[2,256]{1,0:T(2,128)S(1)} collective-permute-done((f32[2,256]{1,0:T(2,128)S(1)}, f32[2,256]{1,0:T(2,128)S(1)}, u32[]{:S(2)}, u32[]{:S(2)}) %collective-permute-start) | collective-permute-done | bytes 2080 | tf_op jit(solution)/shard_map/ppermute | solution.py:302
  13.2 0.2 normalize.1
  13.5 0.1 collective-permute-start.4
  13.6 3.6 %collective-permute-done.4.afactor_ref = f32[1,256]{1,0:T(1,128)S(1)} collective-permute-done((f32[1,256]{1,0:T(1,128)S(1)}, f32[1,256]{1,0:T(1,128)S(1)}, u32[]{:S(2)}, u32[]{:S(2)}) %collective-permute-start.4) | collective-permute-done | bytes 1056 | tf_op jit(solution)/shard_map/ppermute | solution.py:293
  17.1 0.0 collective-permute-start.5
  17.1 1.2 %collective-permute-done.5.bfactor_ref = f32[1,256]{1,0:T(1,128)S(1)} collective-permute-done((f32[1,256]{1,0:T(1,128)S(1)}, f32[1,256]{1,0:T(1,128)S(1)}, u32[]{:S(2)}, u32[]{:S(2)}) %collective-permute-start.5) | collective-permute-done | bytes 1056 | tf_op jit(solution)/shard_map/ppermute | solution.py:294
  18.3 0.2 collective-permute-start.11
  18.4 0.0 collective-permute-done.9.refs_0_
  18.4 0.3 collective-permute-start.1
  18.8 0.0 collective-permute-done.2.a_ref
  18.8 2.9 %collective-permute-start.15 = (bf16[256,384]{1,0:T(8,128)(2,1)S(1)}, bf16[256,384]{1,0:T(8,128)(2,1)S(1)}, u32[]{:S(2)}, u32[]{:S(2)}) collective-permute-start(bf16[256,384]{1,0:T(8,128)(2,1)S(1)} %get-tuple-element.39.refs_6_), channel_id=1, source_target_pairs={{0,4},{4,0},{8,12},{12,8},{1,5},{5,1},{9,13},{13,9},{2,6},{6,2},{1... | collective-permute-start | bytes 589832 | tf_op jit(solution)/shard_map/ppermute | solution.py:293
  21.6 0.0 collective-permute-done.3.b_ref
  21.7 0.2 collective-permute-start.17
  21.8 0.2 normalize_two.1
  22.1 0.0 collective-permute-done.11.refs_2_
  22.1 0.4 collective-permute-start.6
  22.5 0.0 collective-permute-done.14.refs_7_
  22.5 0.2 collective-permute-start.7
  22.6 4.5 %collective-permute-done.15.refs_0_ = bf16[256,384]{1,0:T(8,128)(2,1)S(1)} collective-permute-done((bf16[256,384]{1,0:T(8,128)(2,1)S(1)}, bf16[256,384]{1,0:T(8,128)(2,1)S(1)}, u32[]{:S(2)}, u32[]{:S(2)}) %collective-permute-start.15) | collective-permute-done | bytes 196640 | tf_op jit(solution)/shard_map/ppermute | solution.py:293
  27.2 0.0 collective-permute-start.16
  27.2 0.0 collective-permute-done.17.refs_2_
  27.2 0.5 %collective-permute-start.18 = (bf16[256,384]{1,0:T(8,128)(2,1)S(1)}, bf16[256,384]{1,0:T(8,128)(2,1)S(1)}, u32[]{:S(2)}, u32[]{:S(2)}) collective-permute-start(bf16[256,384]{1,0:T(8,128)(2,1)S(1)} %collective-permute-done.17.refs_2_), channel_id=1, source_target_pairs={{0,1},{1,0},{2,3},{3,2},{4,5},{5,4},{6,7},{7,6},{8,9},{9,8},{10,11... | collective-permute-start | bytes 589832 | tf_op jit(solution)/shard_map/ppermute | solution.py:295
  27.7 0.0 collective-permute-done.1.refs_1_
  27.7 0.1 collective-permute-start.8
  27.7 0.0 collective-permute-done.6.refs_3_
  27.7 0.4 %collective-permute-start.10 = (bf16[256,256]{1,0:T(8,128)(2,1)S(1)}, bf16[256,256]{1,0:T(8,128)(2,1)S(1)}, u32[]{:S(2)}, u32[]{:S(2)}) collective-permute-start(bf16[256,256]{1,0:T(8,128)(2,1)S(1)} %collective-permute-done.9.refs_0_), channel_id=1, source_target_pairs={{0,1},{1,0},{2,3},{3,2},{4,5},{5,4},{6,7},{7,6},{8,9},{9,8},{10,11... | collective-permute-start | bytes 393224 | tf_op jit(solution)/shard_map/ppermute | solution.py:295
  28.2 0.0 collective-permute-done.7.refs_5_
  28.2 0.1 collective-permute-start.12
  28.3 1.2 %scores.3 = (bf16[3,256,1024]{2,1,0:T(8,128)(2,1)S(1)}, f32[256,384]{1,0:T(8,128)S(1)}, f32[256,384]{1,0:T(8,128)S(1)}) custom-call(bf16[256,640]{1,0:T(8,128)(2,1)S(1)} %get-tuple-element.30.query_ref, bf16[256,640]{1,0:T(8,128)(2,1)S(1)} %get-tuple-element.31.refs_0_, bf16[256,640]{1,0:T(8,128)(2,1)S(1)} %collective-permute-done.1.refs_1_, ...), custom_call_target="tpu_custom_call" | custom-call | flops 452984832 | bytes 2555904 | tf_op jit(solution)/shard_map/scores/pallas_call | solution.py:209
  29.4 0.0 collective-permute-done.16.refs_1_
  29.4 0.0 collective-permute-done.18.refs_3_
  29.4 0.4 gather.3
  29.8 2.1 %collective-permute-start.19 = (bf16[256,384]{1,0:T(8,128)(2,1)S(1)}, bf16[256,384]{1,0:T(8,128)(2,1)S(1)}, u32[]{:S(2)}, u32[]{:S(2)}) collective-permute-start(bf16[256,384]{1,0:T(8,128)(2,1)S(1)} %gather.3), channel_id=1, source_target_pairs={{0,12},{4,0},{8,4},{12,8},{1,13},{5,1},{9,5},{13,9},{2,14},{6,2},{... | collective-permute-start | bytes 589832 | tf_op jit(solution)/shard_map/ppermute | solution.py:316
  32.0 0.9 %scores.2 = (bf16[2,256,1024]{2,1,0:T(8,128)(2,1)S(1)}, f32[256,256]{1,0:T(8,128)S(1)}, f32[256,256]{1,0:T(8,128)S(1)}) custom-call(bf16[256,640]{1,0:T(8,128)(2,1)S(1)} %get-tuple-element.30.query_ref, bf16[256,640]{1,0:T(8,128)(2,1)S(1)} %get-tuple-element.31.refs_0_, bf16[256,640]{1,0:T(8,128)(2,1)S(1)} %collective-permute-done.1.refs_1_, ...), custom_call_target="tpu_custom_call" | custom-call | flops 301989888 | bytes 1703936 | tf_op jit(solution)/shard_map/scores/pallas_call | solution.py:209
  32.8 0.0 collective-permute-done.12.refs_3_
  32.8 0.3 gather.2
  33.2 3.1 %collective-permute-start.13 = (bf16[256,256]{1,0:T(8,128)(2,1)S(1)}, bf16[256,256]{1,0:T(8,128)(2,1)S(1)}, u32[]{:S(2)}, u32[]{:S(2)}) collective-permute-start(bf16[256,256]{1,0:T(8,128)(2,1)S(1)} %gather.2), channel_id=1, source_target_pairs={{0,12},{4,0},{8,4},{12,8},{1,13},{5,1},{9,5},{13,9},{2,14},{6,2},{... | collective-permute-start | bytes 393224 | tf_op jit(solution)/shard_map/ppermute | solution.py:316
  36.2 2.7 %collective-permute-done.19.part_ref = bf16[256,384]{1,0:T(8,128)(2,1)S(1)} collective-permute-done((bf16[256,384]{1,0:T(8,128)(2,1)S(1)}, bf16[256,384]{1,0:T(8,128)(2,1)S(1)}, u32[]{:S(2)}, u32[]{:S(2)}) %collective-permute-start.19) | collective-permute-done | bytes 196640 | tf_op jit(solution)/shard_map/ppermute | solution.py:316
  39.0 0.7 %put.2.refs_0_ = bf16[256,640]{1,0:T(8,128)(2,1)} custom-call(bf16[256,384]{1,0:T(8,128)(2,1)S(1)} %collective-permute-done.19.part_ref), custom_call_target="tpu_custom_call" | custom-call | tf_op jit(solution)/shard_map/put/pallas_call | solution.py:268
  39.7 1.5 %collective-permute-done.13.part_ref = bf16[256,256]{1,0:T(8,128)(2,1)S(1)} collective-permute-done((bf16[256,256]{1,0:T(8,128)(2,1)S(1)}, bf16[256,256]{1,0:T(8,128)(2,1)S(1)}, u32[]{:S(2)}, u32[]{:S(2)}) %collective-permute-start.13) | collective-permute-done | bytes 131104 | tf_op jit(solution)/shard_map/ppermute | solution.py:316
  41.2 0.7 %put.3 = bf16[256,640]{1,0:T(8,128)(2,1)} custom-call(bf16[256,256]{1,0:T(8,128)(2,1)S(1)} %collective-permute-done.13.part_ref, bf16[256,640]{1,0:T(8,128)(2,1)} %put.2.refs_0_), custom_call_target="tpu_custom_call", output_to_operand_aliasing={{}: (1, {})} | custom-call | tf_op jit(solution)/shard_map/put/pallas_call | solution.py:268
  (2 shorter events, 0.0 us)
Async XLA Ops:
  0.0 18.8 %collective-permute-start.2 = (bf16[256,640]{1,0:T(8,128)(2,1)}, bf16[256,640]{1,0:T(8,128)(2,1)S(1)}, u32[]{:S(2)}, u32[]{:S(2)}) collective-permute-start(bf16[256,640]{1,0:T(8,128)(2,1)} %bitcast.6), channel_id=1, source_target_pairs={{0,4},{4,0},{8,12},{12,8},{1,5},{5,1},{9,13},{13,9},{2,6},{6,2},{1... | collective-permute-start | bytes 983048 | tf_op jit(solution)/shard_map/ppermute | solution.py:293
  3.1 18.6 %collective-permute-start.3 = (bf16[256,640]{1,0:T(8,128)(2,1)}, bf16[256,640]{1,0:T(8,128)(2,1)S(1)}, u32[]{:S(2)}, u32[]{:S(2)}) collective-permute-start(bf16[256,640]{1,0:T(8,128)(2,1)} %bitcast.7), channel_id=1, source_target_pairs={{0,1},{1,0},{4,8},{5,9},{8,4},{9,5},{12,13},{13,12},{2,3},{3,2},{6... | collective-permute-start | bytes 983048 | tf_op jit(solution)/shard_map/ppermute | solution.py:294
  4.9 17.6 %collective-permute-start.14 = (bf16[256,384]{1,0:T(8,128)(2,1)S(1)}, bf16[256,384]{1,0:T(8,128)(2,1)S(1)}, u32[]{:S(2)}, u32[]{:S(2)}) collective-permute-start(bf16[256,384]{1,0:T(8,128)(2,1)S(1)} %get-tuple-element.39.refs_6_), channel_id=1, source_target_pairs={{0,1},{1,0},{2,3},{3,2},{4,5},{5,4},{6,7},{7,6},{8,9},{9,8},{10,11... | collective-permute-start | bytes 589832 | tf_op jit(solution)/shard_map/ppermute | solution.py:295
  5.5 13.0 %collective-permute-start.9 = (bf16[256,256]{1,0:T(8,128)(2,1)S(1)}, bf16[256,256]{1,0:T(8,128)(2,1)S(1)}, u32[]{:S(2)}, u32[]{:S(2)}) collective-permute-start(bf16[256,256]{1,0:T(8,128)(2,1)S(1)} %get-tuple-element.35.refs_6_), channel_id=1, source_target_pairs={{0,4},{4,0},{8,12},{12,8},{1,5},{5,1},{9,13},{13,9},{2,6},{6,2},{1... | collective-permute-start | bytes 393224 | tf_op jit(solution)/shard_map/ppermute | solution.py:293
  9.6 3.7 %collective-permute-start = (f32[2,256]{1,0:T(2,128)S(1)}, f32[2,256]{1,0:T(2,128)S(1)}, u32[]{:S(2)}, u32[]{:S(2)}) collective-permute-start(f32[2,256]{1,0:T(2,128)S(1)} %get-tuple-element.27.own_ref), channel_id=1, source_target_pairs={{0,2},{2,0},{1,3},{3,1},{4,6},{6,4},{5,7},{7,5},{8,10},{10,8},{9,1... | collective-permute-start | bytes 6152 | tf_op jit(solution)/shard_map/ppermute | solution.py:302
  13.5 3.6 %collective-permute-start.4 = (f32[1,256]{1,0:T(1,128)S(1)}, f32[1,256]{1,0:T(1,128)S(1)}, u32[]{:S(2)}, u32[]{:S(2)}) collective-permute-start(f32[1,256]{1,0:T(1,128)S(1)} %get-tuple-element.32), channel_id=1, source_target_pairs={{0,4},{4,0},{8,12},{12,8},{1,5},{5,1},{9,13},{13,9},{2,6},{6,2},{1... | collective-permute-start | bytes 3080 | tf_op jit(solution)/shard_map/ppermute | solution.py:293
  17.1 1.2 %collective-permute-start.5 = (f32[1,256]{1,0:T(1,128)S(1)}, f32[1,256]{1,0:T(1,128)S(1)}, u32[]{:S(2)}, u32[]{:S(2)}) collective-permute-start(f32[1,256]{1,0:T(1,128)S(1)} %get-tuple-element.32), channel_id=1, source_target_pairs={{0,1},{1,0},{4,8},{5,9},{8,4},{9,5},{12,13},{13,12},{2,3},{3,2},{6... | collective-permute-start | bytes 3080 | tf_op jit(solution)/shard_map/ppermute | solution.py:294
  18.3 3.8 %collective-permute-start.11 = (bf16[256,256]{1,0:T(8,128)(2,1)S(1)}, bf16[256,256]{1,0:T(8,128)(2,1)S(1)}, u32[]{:S(2)}, u32[]{:S(2)}) collective-permute-start(bf16[256,256]{1,0:T(8,128)(2,1)S(1)} %get-tuple-element.35.refs_6_), channel_id=1, source_target_pairs={{0,1},{1,0},{4,8},{5,9},{8,4},{9,5},{12,13},{13,12},{2,3},{3,2},{6... | collective-permute-start | bytes 393224 | tf_op jit(solution)/shard_map/ppermute | solution.py:294
  18.4 9.2 %collective-permute-start.1 = (bf16[256,640]{1,0:T(8,128)(2,1)S(1)}, bf16[256,640]{1,0:T(8,128)(2,1)S(1)}, u32[]{:S(2)}, u32[]{:S(2)}) collective-permute-start(bf16[256,640]{1,0:T(8,128)(2,1)S(1)} %get-tuple-element.31.refs_0_), channel_id=1, source_target_pairs={{0,1},{1,0},{2,3},{3,2},{4,5},{5,4},{6,7},{7,6},{8,9},{9,8},{10,11... | collective-permute-start | bytes 983048 | tf_op jit(solution)/shard_map/ppermute | solution.py:295
  18.8 8.4 %collective-permute-start.15 = (bf16[256,384]{1,0:T(8,128)(2,1)S(1)}, bf16[256,384]{1,0:T(8,128)(2,1)S(1)}, u32[]{:S(2)}, u32[]{:S(2)}) collective-permute-start(bf16[256,384]{1,0:T(8,128)(2,1)S(1)} %get-tuple-element.39.refs_6_), channel_id=1, source_target_pairs={{0,4},{4,0},{8,12},{12,8},{1,5},{5,1},{9,13},{13,9},{2,6},{6,2},{1... | collective-permute-start | bytes 589832 | tf_op jit(solution)/shard_map/ppermute | solution.py:293
  21.7 5.5 %collective-permute-start.17 = (bf16[256,384]{1,0:T(8,128)(2,1)S(1)}, bf16[256,384]{1,0:T(8,128)(2,1)S(1)}, u32[]{:S(2)}, u32[]{:S(2)}) collective-permute-start(bf16[256,384]{1,0:T(8,128)(2,1)S(1)} %get-tuple-element.39.refs_6_), channel_id=1, source_target_pairs={{0,1},{1,0},{4,8},{5,9},{8,4},{9,5},{12,13},{13,12},{2,3},{3,2},{6... | collective-permute-start | bytes 589832 | tf_op jit(solution)/shard_map/ppermute | solution.py:294
  22.1 5.7 %collective-permute-start.6 = (bf16[256,640]{1,0:T(8,128)(2,1)S(1)}, bf16[256,640]{1,0:T(8,128)(2,1)S(1)}, u32[]{:S(2)}, u32[]{:S(2)}) collective-permute-start(bf16[256,640]{1,0:T(8,128)(2,1)S(1)} %get-tuple-element.33.refs_2_), channel_id=1, source_target_pairs={{0,1},{1,0},{2,3},{3,2},{4,5},{5,4},{6,7},{7,6},{8,9},{9,8},{10,11... | collective-permute-start | bytes 983048 | tf_op jit(solution)/shard_map/ppermute | solution.py:295
  22.5 5.7 %collective-permute-start.7 = (bf16[256,640]{1,0:T(8,128)(2,1)S(1)}, bf16[256,640]{1,0:T(8,128)(2,1)S(1)}, u32[]{:S(2)}, u32[]{:S(2)}) collective-permute-start(bf16[256,640]{1,0:T(8,128)(2,1)S(1)} %get-tuple-element.34.refs_4_), channel_id=1, source_target_pairs={{0,1},{1,0},{2,3},{3,2},{4,5},{5,4},{6,7},{7,6},{8,9},{9,8},{10,11... | collective-permute-start | bytes 983048 | tf_op jit(solution)/shard_map/ppermute | solution.py:295
  27.2 2.3 %collective-permute-start.16 = (bf16[256,384]{1,0:T(8,128)(2,1)S(1)}, bf16[256,384]{1,0:T(8,128)(2,1)S(1)}, u32[]{:S(2)}, u32[]{:S(2)}) collective-permute-start(bf16[256,384]{1,0:T(8,128)(2,1)S(1)} %collective-permute-done.15.refs_0_), channel_id=1, source_target_pairs={{0,1},{1,0},{2,3},{3,2},{4,5},{5,4},{6,7},{7,6},{8,9},{9,8},{10,11... | collective-permute-start | bytes 589832 | tf_op jit(solution)/shard_map/ppermute | solution.py:295
  27.2 2.3 %collective-permute-start.18 = (bf16[256,384]{1,0:T(8,128)(2,1)S(1)}, bf16[256,384]{1,0:T(8,128)(2,1)S(1)}, u32[]{:S(2)}, u32[]{:S(2)}) collective-permute-start(bf16[256,384]{1,0:T(8,128)(2,1)S(1)} %collective-permute-done.17.refs_2_), channel_id=1, source_target_pairs={{0,1},{1,0},{2,3},{3,2},{4,5},{5,4},{6,7},{7,6},{8,9},{9,8},{10,11... | collective-permute-start | bytes 589832 | tf_op jit(solution)/shard_map/ppermute | solution.py:295
  27.7 4.3 %collective-permute-start.8 = (bf16[256,256]{1,0:T(8,128)(2,1)S(1)}, bf16[256,256]{1,0:T(8,128)(2,1)S(1)}, u32[]{:S(2)}, u32[]{:S(2)}) collective-permute-start(bf16[256,256]{1,0:T(8,128)(2,1)S(1)} %get-tuple-element.35.refs_6_), channel_id=1, source_target_pairs={{0,1},{1,0},{2,3},{3,2},{4,5},{5,4},{6,7},{7,6},{8,9},{9,8},{10,11... | collective-permute-start | bytes 393224 | tf_op jit(solution)/shard_map/ppermute | solution.py:295
  27.7 5.1 %collective-permute-start.10 = (bf16[256,256]{1,0:T(8,128)(2,1)S(1)}, bf16[256,256]{1,0:T(8,128)(2,1)S(1)}, u32[]{:S(2)}, u32[]{:S(2)}) collective-permute-start(bf16[256,256]{1,0:T(8,128)(2,1)S(1)} %collective-permute-done.9.refs_0_), channel_id=1, source_target_pairs={{0,1},{1,0},{2,3},{3,2},{4,5},{5,4},{6,7},{7,6},{8,9},{9,8},{10,11... | collective-permute-start | bytes 393224 | tf_op jit(solution)/shard_map/ppermute | solution.py:295
  28.2 4.6 %collective-permute-start.12 = (bf16[256,256]{1,0:T(8,128)(2,1)S(1)}, bf16[256,256]{1,0:T(8,128)(2,1)S(1)}, u32[]{:S(2)}, u32[]{:S(2)}) collective-permute-start(bf16[256,256]{1,0:T(8,128)(2,1)S(1)} %collective-permute-done.11.refs_2_), channel_id=1, source_target_pairs={{0,1},{1,0},{2,3},{3,2},{4,5},{5,4},{6,7},{7,6},{8,9},{9,8},{10,11... | collective-permute-start | bytes 393224 | tf_op jit(solution)/shard_map/ppermute | solution.py:295
  29.8 9.1 %collective-permute-start.19 = (bf16[256,384]{1,0:T(8,128)(2,1)S(1)}, bf16[256,384]{1,0:T(8,128)(2,1)S(1)}, u32[]{:S(2)}, u32[]{:S(2)}) collective-permute-start(bf16[256,384]{1,0:T(8,128)(2,1)S(1)} %gather.3), channel_id=1, source_target_pairs={{0,12},{4,0},{8,4},{12,8},{1,13},{5,1},{9,5},{13,9},{2,14},{6,2},{... | collective-permute-start | bytes 589832 | tf_op jit(solution)/shard_map/ppermute | solution.py:316
  33.2 8.0 %collective-permute-start.13 = (bf16[256,256]{1,0:T(8,128)(2,1)S(1)}, bf16[256,256]{1,0:T(8,128)(2,1)S(1)}, u32[]{:S(2)}, u32[]{:S(2)}) collective-permute-start(bf16[256,256]{1,0:T(8,128)(2,1)S(1)} %gather.2), channel_id=1, source_target_pairs={{0,12},{4,0},{8,4},{12,8},{1,13},{5,1},{9,5},{13,9},{2,14},{6,2},{... | collective-permute-start | bytes 393224 | tf_op jit(solution)/shard_map/ppermute | solution.py:316

commit v5 on v4

--- a/solution.py
+++ b/solution.py
@@ -111,41 +111,39 @@
         out_ref[:, here] = (wide * spread * gain_ref[here]).astype(jnp.bfloat16)
 
 
-def normalize_kernel(full_width, query_ref, key_ref, own_ref, other_ref, qgain_ref, kgain_ref, qout_ref, kout_ref, factor_ref):
+def normalize_kernel(full_width, query_ref, key_ref, own_ref, other_ref, qgain_ref, kgain_ref, qout_ref, kout_ref):
     factor = lax.rsqrt((own_ref[...] + other_ref[...]) / full_width + EPSILON)
-    factor_ref[...] = factor[1:2, :]
     apply_norm(key_ref, factor[1:2, :], kgain_ref, kout_ref)
     apply_norm(query_ref, factor[0:1, :], qgain_ref, qout_ref)
 
 
 def normalize(query, key, own, other, query_gain, key_gain, full_width):
-    rows = query.shape[0]
     kept = jax.ShapeDtypeStruct(query.shape, jnp.bfloat16)
     return pl.pallas_call(
         functools.partial(normalize_kernel, full_width),
-        out_shape=[kept, kept, jax.ShapeDtypeStruct((1, rows), jnp.float32)],
+        out_shape=[kept, kept],
         in_specs=[VMEM] * 6,
-        out_specs=[VMEM] * 3,
+        out_specs=[VMEM] * 2,
         name="normalize",
         compiler_params=pltpu.CompilerParams(vmem_limit_bytes=LIMIT),
     )(query, key, own, other, query_gain, key_gain)
 
 
-def normalize_two_kernel(a_ref, b_ref, afactor_ref, bfactor_ref, gain_ref, aout_ref, bout_ref):
-    apply_norm(a_ref, afactor_ref[...], gain_ref, aout_ref)
-    apply_norm(b_ref, bfactor_ref[...], gain_ref, bout_ref)
-
-
-def normalize_two(a, b, afactor, bfactor, gain):
+def normalize_two_kernel(full_width, a_ref, b_ref, atotal_ref, btotal_ref, gain_ref, aout_ref, bout_ref):
+    for ref, total_ref, out_ref in ((a_ref, atotal_ref, aout_ref), (b_ref, btotal_ref, bout_ref)):
+        apply_norm(ref, lax.rsqrt(total_ref[...] / full_width + EPSILON), gain_ref, out_ref)
+
+
+def normalize_two(a, b, atotal, btotal, gain, full_width):
     kept = jax.ShapeDtypeStruct(a.shape, jnp.bfloat16)
     return pl.pallas_call(
-        normalize_two_kernel,
+        functools.partial(normalize_two_kernel, full_width),
         out_shape=[kept, kept],
         in_specs=[VMEM] * 5,
         out_specs=[VMEM] * 2,
         name="normalize_two",
         compiler_params=pltpu.CompilerParams(vmem_limit_bytes=LIMIT),
-    )(a, b, afactor, bfactor, gain)
+    )(a, b, atotal, btotal, gain)
 
 
 def with_used_blocks(work):
@@ -302,9 +300,12 @@
         other = lax.ppermute(own, "tp", [(0, 1), (1, 0)])
     else:
         own, other = lax.psum(own, "tp"), jnp.zeros_like(own)
-    query_normed, key_normed, factor = normalize(query, key, own, other, query_gain, key_gain, width * tp)
-    factor_first, factor_second = first(factor), second(factor)
-    key_first, key_second = normalize_two(key_first, key_second, factor_first, factor_second, key_gain)
+    query_normed, key_normed = normalize(query, key, own, other, query_gain, key_gain, width * tp)
+    total = own[1:2] + other[1:2]
+    total_first, total_second = first(total), second(total)
+    key_first, key_second = normalize_two(
+        key_first, key_second, total_first, total_second, key_gain, width * tp
+    )
     keys = [key_normed, swap(key_normed), key_first, swap(key_first), key_second, swap(key_second)]
     outputs, column = [], 0
     for part in value_parts:

time: 42 us -> 43.6 us (1.038)
  starting transfers between devices: 18.4 us -> 20.4 us
  waiting for transfers between devices: 15.6 us -> 15.1 us
    ppermute x1, waiting for transfers between devices: 2.09 us -> 0.01 us  [body(): other = lax.ppermute(own, 'tp', [(0, 1), (1, 0)])]
    ppermute x4, waiting for transfers between devices: 8.07 us -> 9.95 us  [body(): first = lambda x: lax.ppermute(x, 'queue', first_pairs)]
    ppermute x1, starting transfers between devices: 1.56 us -> 3.03 us  [body(): other = lax.ppermute(own, 'tp', [(0, 1), (1, 0)])]
    ppermute x4, starting transfers between devices: 8.72 us -> 10.1 us  [body(): first = lambda x: lax.ppermute(x, 'queue', first_pairs)]
    ppermute x9, starting transfers between devices: 2.58 us -> 2.08 us  [body(): swap = lambda x: lax.ppermute(x, 'seq', swap_pairs)]
  transfers between devices with their start and end apart: 20 -> 20, of which waited for: 6 -> 5; matrix products, arithmetic and copies ran while one was open for 0% -> 0% of each run, Pallas kernels for 15% -> 12%
where the time goes in v5:
time: 43.6 us; the launch traced here: 43.4 us
  starting transfers between devices  20.4 us (47%)
  waiting for transfers between devices  15.1 us (35%)
  Pallas kernels  7.09 us (16%)
  between operations  0.78 us (2%)
    ppermute x4, starting transfers between devices, body(): first = lambda x: lax.ppermute(x, 'queue', first_pairs)  10.1 us
    ppermute x4, waiting for transfers between devices, body(): first = lambda x: lax.ppermute(x, 'queue', first_pairs)  9.95 us
    ppermute x2, starting transfers between devices, body(): outputs.append(lax.ppermute(gated, 'queue', roll_pairs))  4.86 us
    ppermute x2, waiting for transfers between devices, body(): outputs.append(lax.ppermute(gated, 'queue', roll_pairs))  4.01 us
    ppermute x1, starting transfers between devices, body(): other = lax.ppermute(own, 'tp', [(0, 1), (1, 0)])  3.03 us
    ppermute x9, starting transfers between devices, body(): swap = lambda x: lax.ppermute(x, 'seq', swap_pairs)  2.08 us
    pallas_call x2, Pallas kernels, scores(): pl.pallas_call(functools.partial(scores_kernel, column), out_shape=[jax.S...  2.02 us
    pallas_call x1, Pallas kernels, squares(): pl.pallas_call(squares_kernel, out_shape=[kept, kept, jax.ShapeDtypeStruc...  1.37 us
  transfers between devices with their start and end apart: 20, of which 5 were waited for; matrix products, arithmetic and copies ran while one was open for 0% of the time, Pallas kernels for 12%

profile of v5, /device:TPU:0, one launch (start us, length us, event | category | flops | bytes accessed | tf_op | source)
XLA Modules:
  0.0 43.4 jit_solution(12000378330353409173)
XLA Ops:
  0.0 1.4 %squares.1 = (bf16[256,640]{1,0:T(8,128)(2,1)S(1)}, bf16[256,640]{1,0:T(8,128)(2,1)S(1)}, f32[2,256]{1,0:T(2,128)S(1)}) custom-call(bf16[256,640]{1,0:T(8,128)(2,1)} %bitcast.4, bf16[256,640]{1,0:T(8,128)(2,1)} %bitcast.6), custom_call_target="tpu_custom_call" | custom-call | tf_op jit(solution)/shard_map/squares/pallas_call | solution.py:57
  1.4 3.0 %collective-permute-start = (f32[2,256]{1,0:T(2,128)S(1)}, f32[2,256]{1,0:T(2,128)S(1)}, u32[]{:S(2)}, u32[]{:S(2)}) collective-permute-start(f32[2,256]{1,0:T(2,128)S(1)} %get-tuple-element.26.own_ref), channel_id=1, source_target_pairs={{0,2},{2,0},{1,3},{3,1},{4,6},{6,4},{5,7},{7,5},{8,10},{10,8},{9,1... | collective-permute-start | bytes 6152 | tf_op jit(solution)/shard_map/ppermute | solution.py:300
  4.4 1.6 %collective-permute-start.2 = (bf16[256,640]{1,0:T(8,128)(2,1)}, bf16[256,640]{1,0:T(8,128)(2,1)S(1)}, u32[]{:S(2)}, u32[]{:S(2)}) collective-permute-start(bf16[256,640]{1,0:T(8,128)(2,1)} %bitcast.7), channel_id=1, source_target_pairs={{0,4},{4,0},{8,12},{12,8},{1,5},{5,1},{9,13},{13,9},{2,6},{6,2},{1... | collective-permute-start | bytes 983048 | tf_op jit(solution)/shard_map/ppermute | solution.py:291
  6.0 0.0 collective-permute-start.3
  6.6 1.2 %load.1 = (f32[640]{0:T(1024)S(1)}, f32[640]{0:T(1024)S(1)}, f32[1,640]{1,0:T(1,128)S(1)}, bf16[256,384]{1,0:T(8,128)(2,1)S(1)}, bf16[256,256]{1,0:T(8,128)(2,1)S(1)}) custom-call(bf16[256,640]{1,0:T(8,128)(2,1)} %bitcast.5, f32[640]{0:T(1024)} %qgain_hbm.1, f32[640]{0:T(1024)} %kgain_hbm.1, f32[64,640]{1,0:T(8,128)} %gate_hbm.1, s32[1]{0:T(128)S(6)} %copy.10.levels_hbm), custom_call_target="tpu_custom_call" | custom-call | tf_op jit(solution)/shard_map/load/pallas_call | solution.py:90
  7.8 3.2 %collective-permute-start.9 = (bf16[256,256]{1,0:T(8,128)(2,1)S(1)}, bf16[256,256]{1,0:T(8,128)(2,1)S(1)}, u32[]{:S(2)}, u32[]{:S(2)}) collective-permute-start(bf16[256,256]{1,0:T(8,128)(2,1)S(1)} %get-tuple-element.33.refs_6_), channel_id=1, source_target_pairs={{0,4},{4,0},{8,12},{12,8},{1,5},{5,1},{9,13},{13,9},{2,6},{6,2},{1... | collective-permute-start | bytes 393224 | tf_op jit(solution)/shard_map/ppermute | solution.py:291
  11.0 0.0 collective-permute-start.14
  11.0 0.0 collective-permute-done.other_ref
  11.1 0.2 collective-permute-start.4
  11.2 5.4 %collective-permute-done.4.atotal_ref = f32[1,256]{1,0:T(1,128)S(1)} collective-permute-done((f32[1,256]{1,0:T(1,128)S(1)}, f32[1,256]{1,0:T(1,128)S(1)}, u32[]{:S(2)}, u32[]{:S(2)}) %collective-permute-start.4) | collective-permute-done | bytes 1056 | tf_op jit(solution)/shard_map/ppermute | solution.py:291
  16.7 0.0 collective-permute-start.5
  16.7 1.2 %collective-permute-done.5.btotal_ref = f32[1,256]{1,0:T(1,128)S(1)} collective-permute-done((f32[1,256]{1,0:T(1,128)S(1)}, f32[1,256]{1,0:T(1,128)S(1)}, u32[]{:S(2)}, u32[]{:S(2)}) %collective-permute-start.5) | collective-permute-done | bytes 1056 | tf_op jit(solution)/shard_map/ppermute | solution.py:292
  17.8 0.2 collective-permute-start.11
  18.0 0.2 normalize.1
  18.3 0.0 collective-permute-done.9.refs_0_
  18.3 0.4 collective-permute-start.1
  18.7 0.0 collective-permute-done.2.a_ref
  18.7 5.1 %collective-permute-start.15 = (bf16[256,384]{1,0:T(8,128)(2,1)S(1)}, bf16[256,384]{1,0:T(8,128)(2,1)S(1)}, u32[]{:S(2)}, u32[]{:S(2)}) collective-permute-start(bf16[256,384]{1,0:T(8,128)(2,1)S(1)} %get-tuple-element.37.refs_6_), channel_id=1, source_target_pairs={{0,4},{4,0},{8,12},{12,8},{1,5},{5,1},{9,13},{13,9},{2,6},{6,2},{1... | collective-permute-start | bytes 589832 | tf_op jit(solution)/shard_map/ppermute | solution.py:291
  23.8 0.0 collective-permute-done.3.b_ref
  23.8 0.1 collective-permute-start.17
  24.0 0.2 normalize_two.1
  24.2 0.0 collective-permute-done.11.refs_2_
  24.2 0.4 collective-permute-start.6
  24.7 0.0 collective-permute-done.14.refs_7_
  24.7 0.1 collective-permute-start.7
  24.8 4.5 %collective-permute-done.15.refs_0_ = bf16[256,384]{1,0:T(8,128)(2,1)S(1)} collective-permute-done((bf16[256,384]{1,0:T(8,128)(2,1)S(1)}, bf16[256,384]{1,0:T(8,128)(2,1)S(1)}, u32[]{:S(2)}, u32[]{:S(2)}) %collective-permute-start.15) | collective-permute-done | bytes 196640 | tf_op jit(solution)/shard_map/ppermute | solution.py:291
  29.3 0.0 collective-permute-start.16
  29.3 0.0 collective-permute-done.17.refs_2_
  29.3 0.5 %collective-permute-start.18 = (bf16[256,384]{1,0:T(8,128)(2,1)S(1)}, bf16[256,384]{1,0:T(8,128)(2,1)S(1)}, u32[]{:S(2)}, u32[]{:S(2)}) collective-permute-start(bf16[256,384]{1,0:T(8,128)(2,1)S(1)} %collective-permute-done.17.refs_2_), channel_id=1, source_target_pairs={{0,1},{1,0},{2,3},{3,2},{4,5},{5,4},{6,7},{7,6},{8,9},{9,8},{10,11... | collective-permute-start | bytes 589832 | tf_op jit(solution)/shard_map/ppermute | solution.py:293
  29.8 0.0 collective-permute-done.1.refs_1_
  29.8 0.1 collective-permute-start.8
  29.9 0.0 collective-permute-done.6.refs_3_
  29.9 0.4 %collective-permute-start.10 = (bf16[256,256]{1,0:T(8,128)(2,1)S(1)}, bf16[256,256]{1,0:T(8,128)(2,1)S(1)}, u32[]{:S(2)}, u32[]{:S(2)}) collective-permute-start(bf16[256,256]{1,0:T(8,128)(2,1)S(1)} %collective-permute-done.9.refs_0_), channel_id=1, source_target_pairs={{0,1},{1,0},{2,3},{3,2},{4,5},{5,4},{6,7},{7,6},{8,9},{9,8},{10,11... | collective-permute-start | bytes 393224 | tf_op jit(solution)/shard_map/ppermute | solution.py:293
  30.3 0.1 collective-permute-start.12
  30.4 1.2 %scores.3 = (bf16[3,256,1024]{2,1,0:T(8,128)(2,1)S(1)}, f32[256,384]{1,0:T(8,128)S(1)}, f32[256,384]{1,0:T(8,128)S(1)}) custom-call(bf16[256,640]{1,0:T(8,128)(2,1)S(1)} %get-tuple-element.29.query_ref, bf16[256,640]{1,0:T(8,128)(2,1)S(1)} %get-tuple-element.30.refs_0_, bf16[256,640]{1,0:T(8,128)(2,1)S(1)} %collective-permute-done.1.refs_1_, ...), custom_call_target="tpu_custom_call" | custom-call | flops 452984832 | bytes 2555904 | tf_op jit(solution)/shard_map/scores/pallas_call | solution.py:207
  31.6 0.0 collective-permute-done.18.refs_3_
  31.6 0.4 gather.3
  32.0 1.4 %collective-permute-start.19 = (bf16[256,384]{1,0:T(8,128)(2,1)S(1)}, bf16[256,384]{1,0:T(8,128)(2,1)S(1)}, u32[]{:S(2)}, u32[]{:S(2)}) collective-permute-start(bf16[256,384]{1,0:T(8,128)(2,1)S(1)} %gather.3), channel_id=1, source_target_pairs={{0,12},{4,0},{8,4},{12,8},{1,13},{5,1},{9,5},{13,9},{2,14},{6,2},{... | collective-permute-start | bytes 589832 | tf_op jit(solution)/shard_map/ppermute | solution.py:317
  33.4 0.0 collective-permute-done.8.refs_7_
  33.4 0.9 %scores.2 = (bf16[2,256,1024]{2,1,0:T(8,128)(2,1)S(1)}, f32[256,256]{1,0:T(8,128)S(1)}, f32[256,256]{1,0:T(8,128)S(1)}) custom-call(bf16[256,640]{1,0:T(8,128)(2,1)S(1)} %get-tuple-element.29.query_ref, bf16[256,640]{1,0:T(8,128)(2,1)S(1)} %get-tuple-element.30.refs_0_, bf16[256,640]{1,0:T(8,128)(2,1)S(1)} %collective-permute-done.1.refs_1_, ...), custom_call_target="tpu_custom_call" | custom-call | flops 301989888 | bytes 1703936 | tf_op jit(solution)/shard_map/scores/pallas_call | solution.py:207
  34.3 0.0 collective-permute-done.10.refs_1_
  34.3 0.0 collective-permute-done.12.refs_3_
  34.3 0.3 gather.2
  34.6 3.5 %collective-permute-start.13 = (bf16[256,256]{1,0:T(8,128)(2,1)S(1)}, bf16[256,256]{1,0:T(8,128)(2,1)S(1)}, u32[]{:S(2)}, u32[]{:S(2)}) collective-permute-start(bf16[256,256]{1,0:T(8,128)(2,1)S(1)} %gather.2), channel_id=1, source_target_pairs={{0,12},{4,0},{8,4},{12,8},{1,13},{5,1},{9,5},{13,9},{2,14},{6,2},{... | collective-permute-start | bytes 393224 | tf_op jit(solution)/shard_map/ppermute | solution.py:317
  38.1 2.1 %collective-permute-done.19.part_ref = bf16[256,384]{1,0:T(8,128)(2,1)S(1)} collective-permute-done((bf16[256,384]{1,0:T(8,128)(2,1)S(1)}, bf16[256,384]{1,0:T(8,128)(2,1)S(1)}, u32[]{:S(2)}, u32[]{:S(2)}) %collective-permute-start.19) | collective-permute-done | bytes 196640 | tf_op jit(solution)/shard_map/ppermute | solution.py:317
  40.2 0.7 %put.2.refs_0_ = bf16[256,640]{1,0:T(8,128)(2,1)} custom-call(bf16[256,384]{1,0:T(8,128)(2,1)S(1)} %collective-permute-done.19.part_ref), custom_call_target="tpu_custom_call" | custom-call | tf_op jit(solution)/shard_map/put/pallas_call | solution.py:266
  40.9 1.9 %collective-permute-done.13.part_ref = bf16[256,256]{1,0:T(8,128)(2,1)S(1)} collective-permute-done((bf16[256,256]{1,0:T(8,128)(2,1)S(1)}, bf16[256,256]{1,0:T(8,128)(2,1)S(1)}, u32[]{:S(2)}, u32[]{:S(2)}) %collective-permute-start.13) | collective-permute-done | bytes 131104 | tf_op jit(solution)/shard_map/ppermute | solution.py:317
  42.8 0.7 %put.3 = bf16[256,640]{1,0:T(8,128)(2,1)} custom-call(bf16[256,256]{1,0:T(8,128)(2,1)S(1)} %collective-permute-done.13.part_ref, bf16[256,640]{1,0:T(8,128)(2,1)} %put.2.refs_0_), custom_call_target="tpu_custom_call", output_to_operand_aliasing={{}: (1, {})} | custom-call | tf_op jit(solution)/shard_map/put/pallas_call | solution.py:266
  (3 shorter events, 0.0 us)
Async XLA Ops:
  1.4 9.7 %collective-permute-start = (f32[2,256]{1,0:T(2,128)S(1)}, f32[2,256]{1,0:T(2,128)S(1)}, u32[]{:S(2)}, u32[]{:S(2)}) collective-permute-start(f32[2,256]{1,0:T(2,128)S(1)} %get-tuple-element.26.own_ref), channel_id=1, source_target_pairs={{0,2},{2,0},{1,3},{3,1},{4,6},{6,4},{5,7},{7,5},{8,10},{10,8},{9,1... | collective-permute-start | bytes 6152 | tf_op jit(solution)/shard_map/ppermute | solution.py:300
  4.4 14.3 %collective-permute-start.2 = (bf16[256,640]{1,0:T(8,128)(2,1)}, bf16[256,640]{1,0:T(8,128)(2,1)S(1)}, u32[]{:S(2)}, u32[]{:S(2)}) collective-permute-start(bf16[256,640]{1,0:T(8,128)(2,1)} %bitcast.7), channel_id=1, source_target_pairs={{0,4},{4,0},{8,12},{12,8},{1,5},{5,1},{9,13},{13,9},{2,6},{6,2},{1... | collective-permute-start | bytes 983048 | tf_op jit(solution)/shard_map/ppermute | solution.py:291
  6.0 17.8 %collective-permute-start.3 = (bf16[256,640]{1,0:T(8,128)(2,1)}, bf16[256,640]{1,0:T(8,128)(2,1)S(1)}, u32[]{:S(2)}, u32[]{:S(2)}) collective-permute-start(bf16[256,640]{1,0:T(8,128)(2,1)} %bitcast.8), channel_id=1, source_target_pairs={{0,1},{1,0},{4,8},{5,9},{8,4},{9,5},{12,13},{13,12},{2,3},{3,2},{6... | collective-permute-start | bytes 983048 | tf_op jit(solution)/shard_map/ppermute | solution.py:292
  7.8 10.4 %collective-permute-start.9 = (bf16[256,256]{1,0:T(8,128)(2,1)S(1)}, bf16[256,256]{1,0:T(8,128)(2,1)S(1)}, u32[]{:S(2)}, u32[]{:S(2)}) collective-permute-start(bf16[256,256]{1,0:T(8,128)(2,1)S(1)} %get-tuple-element.33.refs_6_), channel_id=1, source_target_pairs={{0,4},{4,0},{8,12},{12,8},{1,5},{5,1},{9,13},{13,9},{2,6},{6,2},{1... | collective-permute-start | bytes 393224 | tf_op jit(solution)/shard_map/ppermute | solution.py:291
  11.0 13.6 %collective-permute-start.14 = (bf16[256,384]{1,0:T(8,128)(2,1)S(1)}, bf16[256,384]{1,0:T(8,128)(2,1)S(1)}, u32[]{:S(2)}, u32[]{:S(2)}) collective-permute-start(bf16[256,384]{1,0:T(8,128)(2,1)S(1)} %get-tuple-element.37.refs_6_), channel_id=1, source_target_pairs={{0,1},{1,0},{2,3},{3,2},{4,5},{5,4},{6,7},{7,6},{8,9},{9,8},{10,11... | collective-permute-start | bytes 589832 | tf_op jit(solution)/shard_map/ppermute | solution.py:293
  11.1 5.6 %collective-permute-start.4 = (f32[1,256]{1,0:T(1,128)S(1)}, f32[1,256]{1,0:T(1,128)S(1)}, u32[]{:S(2)}, u32[]{:S(2)}) collective-permute-start(f32[1,256]{1,0:T(1,128)S(1)} %slice_add_fusion), channel_id=1, source_target_pairs={{0,4},{4,0},{8,12},{12,8},{1,5},{5,1},{9,13},{13,9},{2,6},{6,2},{1... | collective-permute-start | bytes 3080 | tf_op jit(solution)/shard_map/ppermute | solution.py:291
  16.7 1.2 %collective-permute-start.5 = (f32[1,256]{1,0:T(1,128)S(1)}, f32[1,256]{1,0:T(1,128)S(1)}, u32[]{:S(2)}, u32[]{:S(2)}) collective-permute-start(f32[1,256]{1,0:T(1,128)S(1)} %slice_add_fusion), channel_id=1, source_target_pairs={{0,1},{1,0},{4,8},{5,9},{8,4},{9,5},{12,13},{13,12},{2,3},{3,2},{6... | collective-permute-start | bytes 3080 | tf_op jit(solution)/shard_map/ppermute | solution.py:292
  17.8 6.4 %collective-permute-start.11 = (bf16[256,256]{1,0:T(8,128)(2,1)S(1)}, bf16[256,256]{1,0:T(8,128)(2,1)S(1)}, u32[]{:S(2)}, u32[]{:S(2)}) collective-permute-start(bf16[256,256]{1,0:T(8,128)(2,1)S(1)} %get-tuple-element.33.refs_6_), channel_id=1, source_target_pairs={{0,1},{1,0},{4,8},{5,9},{8,4},{9,5},{12,13},{13,12},{2,3},{3,2},{6... | collective-permute-start | bytes 393224 | tf_op jit(solution)/shard_map/ppermute | solution.py:292
  18.3 11.6 %collective-permute-start.1 = (bf16[256,640]{1,0:T(8,128)(2,1)S(1)}, bf16[256,640]{1,0:T(8,128)(2,1)S(1)}, u32[]{:S(2)}, u32[]{:S(2)}) collective-permute-start(bf16[256,640]{1,0:T(8,128)(2,1)S(1)} %get-tuple-element.30.refs_0_), channel_id=1, source_target_pairs={{0,1},{1,0},{2,3},{3,2},{4,5},{5,4},{6,7},{7,6},{8,9},{9,8},{10,11... | collective-permute-start | bytes 983048 | tf_op jit(solution)/shard_map/ppermute | solution.py:293
  18.7 10.6 %collective-permute-start.15 = (bf16[256,384]{1,0:T(8,128)(2,1)S(1)}, bf16[256,384]{1,0:T(8,128)(2,1)S(1)}, u32[]{:S(2)}, u32[]{:S(2)}) collective-permute-start(bf16[256,384]{1,0:T(8,128)(2,1)S(1)} %get-tuple-element.37.refs_6_), channel_id=1, source_target_pairs={{0,4},{4,0},{8,12},{12,8},{1,5},{5,1},{9,13},{13,9},{2,6},{6,2},{1... | collective-permute-start | bytes 589832 | tf_op jit(solution)/shard_map/ppermute | solution.py:291
  23.8 5.5 %collective-permute-start.17 = (bf16[256,384]{1,0:T(8,128)(2,1)S(1)}, bf16[256,384]{1,0:T(8,128)(2,1)S(1)}, u32[]{:S(2)}, u32[]{:S(2)}) collective-permute-start(bf16[256,384]{1,0:T(8,128)(2,1)S(1)} %get-tuple-element.37.refs_6_), channel_id=1, source_target_pairs={{0,1},{1,0},{4,8},{5,9},{8,4},{9,5},{12,13},{13,12},{2,3},{3,2},{6... | collective-permute-start | bytes 589832 | tf_op jit(solution)/shard_map/ppermute | solution.py:292
  24.2 5.7 %collective-permute-start.6 = (bf16[256,640]{1,0:T(8,128)(2,1)S(1)}, bf16[256,640]{1,0:T(8,128)(2,1)S(1)}, u32[]{:S(2)}, u32[]{:S(2)}) collective-permute-start(bf16[256,640]{1,0:T(8,128)(2,1)S(1)} %get-tuple-element.31.refs_2_), channel_id=1, source_target_pairs={{0,1},{1,0},{2,3},{3,2},{4,5},{5,4},{6,7},{7,6},{8,9},{9,8},{10,11... | collective-permute-start | bytes 983048 | tf_op jit(solution)/shard_map/ppermute | solution.py:293
  24.7 5.7 %collective-permute-start.7 = (bf16[256,640]{1,0:T(8,128)(2,1)S(1)}, bf16[256,640]{1,0:T(8,128)(2,1)S(1)}, u32[]{:S(2)}, u32[]{:S(2)}) collective-permute-start(bf16[256,640]{1,0:T(8,128)(2,1)S(1)} %get-tuple-element.32.refs_4_), channel_id=1, source_target_pairs={{0,1},{1,0},{2,3},{3,2},{4,5},{5,4},{6,7},{7,6},{8,9},{9,8},{10,11... | collective-permute-start | bytes 983048 | tf_op jit(solution)/shard_map/ppermute | solution.py:293
  29.3 2.3 %collective-permute-start.16 = (bf16[256,384]{1,0:T(8,128)(2,1)S(1)}, bf16[256,384]{1,0:T(8,128)(2,1)S(1)}, u32[]{:S(2)}, u32[]{:S(2)}) collective-permute-start(bf16[256,384]{1,0:T(8,128)(2,1)S(1)} %collective-permute-done.15.refs_0_), channel_id=1, source_target_pairs={{0,1},{1,0},{2,3},{3,2},{4,5},{5,4},{6,7},{7,6},{8,9},{9,8},{10,11... | collective-permute-start | bytes 589832 | tf_op jit(solution)/shard_map/ppermute | solution.py:293
  29.3 2.3 %collective-permute-start.18 = (bf16[256,384]{1,0:T(8,128)(2,1)S(1)}, bf16[256,384]{1,0:T(8,128)(2,1)S(1)}, u32[]{:S(2)}, u32[]{:S(2)}) collective-permute-start(bf16[256,384]{1,0:T(8,128)(2,1)S(1)} %collective-permute-done.17.refs_2_), channel_id=1, source_target_pairs={{0,1},{1,0},{2,3},{3,2},{4,5},{5,4},{6,7},{7,6},{8,9},{9,8},{10,11... | collective-permute-start | bytes 589832 | tf_op jit(solution)/shard_map/ppermute | solution.py:293
  29.8 3.6 %collective-permute-start.8 = (bf16[256,256]{1,0:T(8,128)(2,1)S(1)}, bf16[256,256]{1,0:T(8,128)(2,1)S(1)}, u32[]{:S(2)}, u32[]{:S(2)}) collective-permute-start(bf16[256,256]{1,0:T(8,128)(2,1)S(1)} %get-tuple-element.33.refs_6_), channel_id=1, source_target_pairs={{0,1},{1,0},{2,3},{3,2},{4,5},{5,4},{6,7},{7,6},{8,9},{9,8},{10,11... | collective-permute-start | bytes 393224 | tf_op jit(solution)/shard_map/ppermute | solution.py:293
  29.9 4.4 %collective-permute-start.10 = (bf16[256,256]{1,0:T(8,128)(2,1)S(1)}, bf16[256,256]{1,0:T(8,128)(2,1)S(1)}, u32[]{:S(2)}, u32[]{:S(2)}) collective-permute-start(bf16[256,256]{1,0:T(8,128)(2,1)S(1)} %collective-permute-done.9.refs_0_), channel_id=1, source_target_pairs={{0,1},{1,0},{2,3},{3,2},{4,5},{5,4},{6,7},{7,6},{8,9},{9,8},{10,11... | collective-permute-start | bytes 393224 | tf_op jit(solution)/shard_map/ppermute | solution.py:293
  30.3 3.9 %collective-permute-start.12 = (bf16[256,256]{1,0:T(8,128)(2,1)S(1)}, bf16[256,256]{1,0:T(8,128)(2,1)S(1)}, u32[]{:S(2)}, u32[]{:S(2)}) collective-permute-start(bf16[256,256]{1,0:T(8,128)(2,1)S(1)} %collective-permute-done.11.refs_2_), channel_id=1, source_target_pairs={{0,1},{1,0},{2,3},{3,2},{4,5},{5,4},{6,7},{7,6},{8,9},{9,8},{10,11... | collective-permute-start | bytes 393224 | tf_op jit(solution)/shard_map/ppermute | solution.py:293
  32.0 8.2 %collective-permute-start.19 = (bf16[256,384]{1,0:T(8,128)(2,1)S(1)}, bf16[256,384]{1,0:T(8,128)(2,1)S(1)}, u32[]{:S(2)}, u32[]{:S(2)}) collective-permute-start(bf16[256,384]{1,0:T(8,128)(2,1)S(1)} %gather.3), channel_id=1, source_target_pairs={{0,12},{4,0},{8,4},{12,8},{1,13},{5,1},{9,5},{13,9},{2,14},{6,2},{... | collective-permute-start | bytes 589832 | tf_op jit(solution)/shard_map/ppermute | solution.py:317
  34.6 8.2 %collective-permute-start.13 = (bf16[256,256]{1,0:T(8,128)(2,1)S(1)}, bf16[256,256]{1,0:T(8,128)(2,1)S(1)}, u32[]{:S(2)}, u32[]{:S(2)}) collective-permute-start(bf16[256,256]{1,0:T(8,128)(2,1)S(1)} %gather.2), channel_id=1, source_target_pairs={{0,12},{4,0},{8,4},{12,8},{1,13},{5,1},{9,5},{13,9},{2,14},{6,2},{... | collective-permute-start | bytes 393224 | tf_op jit(solution)/shard_map/ppermute | solution.py:317

commit v6 on v5

--- a/solution.py
+++ b/solution.py
@@ -14,7 +14,7 @@
 SCALE = 1.0 / (math.sqrt(DH) * math.log(2.0))
 CHUNK_SHARE = (3, 2)
 
-LIMIT = 8 << 20
+LIMIT = 16 << 20
 VMEM = pl.BlockSpec(memory_space=pltpu.VMEM)
 HBM = pl.BlockSpec(memory_space=pltpu.HBM)
 ANY = pl.BlockSpec(memory_space=pl.ANY)
@@ -219,45 +219,84 @@
     )(query, *keys, *values)
 
 
-def gather_kernel(column, gate_ref, weight_ref, sum_ref, own_ref, *refs):
-    values, out_ref = refs[0:4], refs[4]
+def half_kernel(weight_ref, own_ref, first_ref, second_ref, out_ref):
+    rows = out_ref.shape[0]
+
+    def work(used):
+        for head in range(out_ref.shape[1] // DH):
+            here = slice(head * DH, (head + 1) * DH)
+            summed = own_ref[:, here]
+            for block, value_ref in ((0, first_ref), (2, second_ref)):
+                if block < used - 2:
+                    summed += jnp.dot(
+                        weight_ref[head, :, block * rows : (block + 1) * rows],
+                        value_ref[:, here],
+                        preferred_element_type=jnp.float32,
+                    )
+            out_ref[:, here] = summed
+
+    with_used_blocks(work)
+
+
+def gather_kernel(column, gate_ref, weight_ref, sum_ref, half_ref, first_ref, second_ref, out_ref):
     rows = out_ref.shape[0]
 
     def work(used):
         for head in range(out_ref.shape[1] // DH):
             here = slice(head * DH, (head + 1) * DH)
             there = slice(column + head * DH, column + (head + 1) * DH)
-            summed = own_ref[:, here]
-            for block in range(used - 2):
-                summed += jnp.dot(
-                    weight_ref[head, :, block * rows : (block + 1) * rows],
-                    values[block][:, here],
-                    preferred_element_type=jnp.float32,
-                )
+            summed = half_ref[:, here]
+            for block, value_ref in ((1, first_ref), (3, second_ref)):
+                if block < used - 2:
+                    summed += jnp.dot(
+                        weight_ref[head, :, block * rows : (block + 1) * rows],
+                        value_ref[:, here],
+                        preferred_element_type=jnp.float32,
+                    )
             out_ref[:, here] = (gate_ref[:, there] * (summed / sum_ref[:, here])).astype(jnp.bfloat16)
 
     with_used_blocks(work)
 
 
-def gather(column, width, gate, weights, sums, own, values):
-    rows = own.shape[0]
-    count = 4 * rows * width * rows
+def half(weights, own, values):
+    return pl.pallas_call(
+        half_kernel,
+        out_shape=jax.ShapeDtypeStruct(own.shape, own.dtype),
+        in_specs=[VMEM] * 4,
+        out_specs=VMEM,
+        name="half",
+        compiler_params=pltpu.CompilerParams(vmem_limit_bytes=LIMIT),
+        cost_estimate=pl.CostEstimate(flops=4 * own.size * own.shape[0], bytes_accessed=6 * own.size, transcendentals=0),
+    )(weights, own, *values)
+
+
+def gather(column, gate, weights, sums, summed, values):
+    rows, width = summed.shape
     return pl.pallas_call(
         functools.partial(gather_kernel, column),
         out_shape=jax.ShapeDtypeStruct((rows, width), jnp.bfloat16),
-        in_specs=[VMEM] * 8,
+        in_specs=[VMEM] * 6,
         out_specs=VMEM,
         name="gather",
         compiler_params=pltpu.CompilerParams(vmem_limit_bytes=LIMIT),
-        cost_estimate=pl.CostEstimate(flops=2 * count, bytes_accessed=26 * rows * width, transcendentals=0),
-    )(gate, weights, sums, own, *values)
+        cost_estimate=pl.CostEstimate(flops=4 * rows * width * rows, bytes_accessed=6 * rows * width, transcendentals=0),
+    )(gate, weights, sums, summed, *values)
 
 
 def put_kernel(column, part_ref, *refs):
-    out_ref, sem = refs[-2:]
-    copy = pltpu.make_async_copy(part_ref, out_ref.at[:, pl.ds(column, part_ref.shape[1])], sem)
-    copy.start()
-    copy.wait()
+    out_ref, sems = refs[-2:]
+    rows, width = part_ref.shape
+    step = rows // COPY_PARTS
+    copies = []
+    for part in range(COPY_PARTS):
+        here = pl.ds(part * step, step)
+        copies.append(
+            pltpu.make_async_copy(part_ref.at[here], out_ref.at[here, pl.ds(column, width)], sems.at[part])
+        )
+    for copy in copies:
+        copy.start()
+    for copy in copies:
+        copy.wait()
 
 
 def put(part, column, whole, width):
@@ -268,7 +307,7 @@
         out_shape=jax.ShapeDtypeStruct((rows, width), part.dtype),
         in_specs=[VMEM] + [HBM] * len(kept),
         out_specs=HBM,
-        scratch_shapes=[pltpu.SemaphoreType.DMA],
+        scratch_shapes=[pltpu.SemaphoreType.DMA((COPY_PARTS,))],
         input_output_aliases={1: 0} if kept else {},
         name="put",
         compiler_params=pltpu.CompilerParams(vmem_limit_bytes=LIMIT),
@@ -312,8 +351,9 @@
         chunk = part.shape[1]
         part_first, part_second = first(part), second(part)
         weights, sums, own = scores(column, chunk, query_normed, keys, [part, swap(part)])
-        beside = [part_first, swap(part_first), part_second, swap(part_second)]
-        gated = gather(column, chunk, gate, weights, sums, own, beside)
+        summed = half(weights, own, [part_first, part_second])
+        swapped = [swap(part_first), swap(part_second)]
+        gated = gather(column, gate, weights, sums, summed, swapped)
         outputs.append(lax.ppermute(gated, "queue", roll_pairs))
         column += chunk
     whole, column = None, 0

time: 43.6 us -> 43.8 us (level)
    pallas_call x0 -> x2, Pallas kernels: none -> 0.49 us  [half(): pl.pallas_call(half_kernel, out_shape=jax.ShapeDtypeStruct(own.shape, own...]
where the time goes in v6:
time: 43.8 us; the launch traced here: 43.6 us
  starting transfers between devices  20.4 us (47%)
  waiting for transfers between devices  15 us (34%)
  Pallas kernels  7.44 us (17%)
  between operations  0.8 us (2%)
    ppermute x4, starting transfers between devices, body(): first = lambda x: lax.ppermute(x, 'queue', first_pairs)  10.1 us
    ppermute x4, waiting for transfers between devices, body(): first = lambda x: lax.ppermute(x, 'queue', first_pairs)  9.95 us
    ppermute x2, starting transfers between devices, body(): outputs.append(lax.ppermute(gated, 'queue', roll_pairs))  4.85 us
    ppermute x2, waiting for transfers between devices, body(): outputs.append(lax.ppermute(gated, 'queue', roll_pairs))  3.83 us
    ppermute x1, starting transfers between devices, body(): other = lax.ppermute(own, 'tp', [(0, 1), (1, 0)])  3.03 us
    ppermute x9, starting transfers between devices, body(): swap = lambda x: lax.ppermute(x, 'seq', swap_pairs)  2.08 us
    pallas_call x2, Pallas kernels, scores(): pl.pallas_call(functools.partial(scores_kernel, column), out_shape=[jax.S...  2.02 us
    pallas_call x2, Pallas kernels, put(): pl.pallas_call(functools.partial(put_kernel, column), out_shape=jax.Shape...  1.38 us
  transfers between devices with their start and end apart: 20, of which 5 were waited for; matrix products, arithmetic and copies ran while one was open for 0% of the time, Pallas kernels for 12%

profile of v6, /device:TPU:0, one launch (start us, length us, event | category | flops | bytes accessed | tf_op | source)
XLA Modules:
  0.0 43.6 jit_solution(14188798717279471600)
XLA Ops:
  0.0 1.4 %squares.1 = (bf16[256,640]{1,0:T(8,128)(2,1)S(1)}, bf16[256,640]{1,0:T(8,128)(2,1)S(1)}, f32[2,256]{1,0:T(2,128)S(1)}) custom-call(bf16[256,640]{1,0:T(8,128)(2,1)} %bitcast.4, bf16[256,640]{1,0:T(8,128)(2,1)} %bitcast.6), custom_call_target="tpu_custom_call" | custom-call | tf_op jit(solution)/shard_map/squares/pallas_call | solution.py:57
  1.4 3.0 %collective-permute-start = (f32[2,256]{1,0:T(2,128)S(1)}, f32[2,256]{1,0:T(2,128)S(1)}, u32[]{:S(2)}, u32[]{:S(2)}) collective-permute-start(f32[2,256]{1,0:T(2,128)S(1)} %get-tuple-element.26.own_ref), channel_id=1, source_target_pairs={{0,2},{2,0},{1,3},{3,1},{4,6},{6,4},{5,7},{7,5},{8,10},{10,8},{9,1... | collective-permute-start | bytes 6152 | tf_op jit(solution)/shard_map/ppermute | solution.py:339
  4.4 1.6 %collective-permute-start.2 = (bf16[256,640]{1,0:T(8,128)(2,1)}, bf16[256,640]{1,0:T(8,128)(2,1)S(1)}, u32[]{:S(2)}, u32[]{:S(2)}) collective-permute-start(bf16[256,640]{1,0:T(8,128)(2,1)} %bitcast.7), channel_id=1, source_target_pairs={{0,4},{4,0},{8,12},{12,8},{1,5},{5,1},{9,13},{13,9},{2,6},{6,2},{1... | collective-permute-start | bytes 983048 | tf_op jit(solution)/shard_map/ppermute | solution.py:330
  6.0 0.0 collective-permute-start.3
  6.6 1.2 %load.1 = (f32[640]{0:T(1024)S(1)}, f32[640]{0:T(1024)S(1)}, f32[1,640]{1,0:T(1,128)S(1)}, bf16[256,384]{1,0:T(8,128)(2,1)S(1)}, bf16[256,256]{1,0:T(8,128)(2,1)S(1)}) custom-call(bf16[256,640]{1,0:T(8,128)(2,1)} %bitcast.5, f32[640]{0:T(1024)} %qgain_hbm.1, f32[640]{0:T(1024)} %kgain_hbm.1, f32[64,640]{1,0:T(8,128)} %gate_hbm.1, s32[1]{0:T(128)S(6)} %copy.10.levels_hbm), custom_call_target="tpu_custom_call" | custom-call | tf_op jit(solution)/shard_map/load/pallas_call | solution.py:90
  7.8 3.2 %collective-permute-start.9 = (bf16[256,256]{1,0:T(8,128)(2,1)S(1)}, bf16[256,256]{1,0:T(8,128)(2,1)S(1)}, u32[]{:S(2)}, u32[]{:S(2)}) collective-permute-start(bf16[256,256]{1,0:T(8,128)(2,1)S(1)} %get-tuple-element.33.refs_6_), channel_id=1, source_target_pairs={{0,4},{4,0},{8,12},{12,8},{1,5},{5,1},{9,13},{13,9},{2,6},{6,2},{1... | collective-permute-start | bytes 393224 | tf_op jit(solution)/shard_map/ppermute | solution.py:330
  11.0 0.0 collective-permute-start.14
  11.0 0.0 collective-permute-done.other_ref
  11.1 0.2 collective-permute-start.4
  11.2 5.4 %collective-permute-done.4.atotal_ref = f32[1,256]{1,0:T(1,128)S(1)} collective-permute-done((f32[1,256]{1,0:T(1,128)S(1)}, f32[1,256]{1,0:T(1,128)S(1)}, u32[]{:S(2)}, u32[]{:S(2)}) %collective-permute-start.4) | collective-permute-done | bytes 1056 | tf_op jit(solution)/shard_map/ppermute | solution.py:330
  16.7 0.0 collective-permute-start.5
  16.7 1.2 %collective-permute-done.5.btotal_ref = f32[1,256]{1,0:T(1,128)S(1)} collective-permute-done((f32[1,256]{1,0:T(1,128)S(1)}, f32[1,256]{1,0:T(1,128)S(1)}, u32[]{:S(2)}, u32[]{:S(2)}) %collective-permute-start.5) | collective-permute-done | bytes 1056 | tf_op jit(solution)/shard_map/ppermute | solution.py:331
  17.8 0.2 collective-permute-start.10
  18.0 0.2 normalize.1
  18.3 0.0 collective-permute-done.9.first_ref
  18.3 0.4 collective-permute-start.1
  18.7 0.0 collective-permute-done.2.a_ref
  18.7 5.1 %collective-permute-start.15 = (bf16[256,384]{1,0:T(8,128)(2,1)S(1)}, bf16[256,384]{1,0:T(8,128)(2,1)S(1)}, u32[]{:S(2)}, u32[]{:S(2)}) collective-permute-start(bf16[256,384]{1,0:T(8,128)(2,1)S(1)} %get-tuple-element.37.refs_6_), channel_id=1, source_target_pairs={{0,4},{4,0},{8,12},{12,8},{1,5},{5,1},{9,13},{13,9},{2,6},{6,2},{1... | collective-permute-start | bytes 589832 | tf_op jit(solution)/shard_map/ppermute | solution.py:330
  23.8 0.0 collective-permute-done.3.b_ref
  23.8 0.1 collective-permute-start.16
  24.0 0.2 normalize_two.1
  24.2 0.0 collective-permute-done.10.second_ref
  24.2 0.4 collective-permute-start.6
  24.7 0.0 collective-permute-done.14.refs_7_
  24.7 0.1 collective-permute-start.7
  24.8 4.5 %collective-permute-done.15.first_ref = bf16[256,384]{1,0:T(8,128)(2,1)S(1)} collective-permute-done((bf16[256,384]{1,0:T(8,128)(2,1)S(1)}, bf16[256,384]{1,0:T(8,128)(2,1)S(1)}, u32[]{:S(2)}, u32[]{:S(2)}) %collective-permute-start.15) | collective-permute-done | bytes 196640 | tf_op jit(solution)/shard_map/ppermute | solution.py:330
  29.3 0.0 collective-permute-done.16.second_ref
  29.3 0.5 %collective-permute-start.18 = (bf16[256,384]{1,0:T(8,128)(2,1)S(1)}, bf16[256,384]{1,0:T(8,128)(2,1)S(1)}, u32[]{:S(2)}, u32[]{:S(2)}) collective-permute-start(bf16[256,384]{1,0:T(8,128)(2,1)S(1)} %collective-permute-done.16.second_ref), channel_id=1, source_target_pairs={{0,1},{1,0},{2,3},{3,2},{4,5},{5,4},{6,7},{7,6},{8,9},{9,8},{10,11... | collective-permute-start | bytes 589832 | tf_op jit(solution)/shard_map/ppermute | solution.py:332
  29.8 0.0 collective-permute-done.1.refs_1_
  29.8 0.1 collective-permute-start.8
  29.9 0.4 %collective-permute-start.11 = (bf16[256,256]{1,0:T(8,128)(2,1)S(1)}, bf16[256,256]{1,0:T(8,128)(2,1)S(1)}, u32[]{:S(2)}, u32[]{:S(2)}) collective-permute-start(bf16[256,256]{1,0:T(8,128)(2,1)S(1)} %collective-permute-done.9.first_ref), channel_id=1, source_target_pairs={{0,1},{1,0},{2,3},{3,2},{4,5},{5,4},{6,7},{7,6},{8,9},{9,8},{10,11... | collective-permute-start | bytes 393224 | tf_op jit(solution)/shard_map/ppermute | solution.py:332
  30.3 0.0 collective-permute-done.7.refs_5_
  30.3 0.1 collective-permute-start.12
  30.4 1.2 %scores.3 = (bf16[3,256,1024]{2,1,0:T(8,128)(2,1)S(1)}, f32[256,384]{1,0:T(8,128)S(1)}, f32[256,384]{1,0:T(8,128)S(1)}) custom-call(bf16[256,640]{1,0:T(8,128)(2,1)S(1)} %get-tuple-element.29.query_ref, bf16[256,640]{1,0:T(8,128)(2,1)S(1)} %get-tuple-element.30.refs_0_, bf16[256,640]{1,0:T(8,128)(2,1)S(1)} %collective-permute-done.1.refs_1_, ...), custom_call_target="tpu_custom_call" | custom-call | flops 452984832 | bytes 2555904 | tf_op jit(solution)/shard_map/scores/pallas_call | solution.py:207
  31.6 0.3 half.3.half_ref
  31.9 0.0 collective-permute-done.17.first_ref
  31.9 0.3 gather.3
  32.2 1.4 %collective-permute-start.19 = (bf16[256,384]{1,0:T(8,128)(2,1)S(1)}, bf16[256,384]{1,0:T(8,128)(2,1)S(1)}, u32[]{:S(2)}, u32[]{:S(2)}) collective-permute-start(bf16[256,384]{1,0:T(8,128)(2,1)S(1)} %gather.3), channel_id=1, source_target_pairs={{0,12},{4,0},{8,4},{12,8},{1,13},{5,1},{9,5},{13,9},{2,14},{6,2},{... | collective-permute-start | bytes 589832 | tf_op jit(solution)/shard_map/ppermute | solution.py:357
  33.6 0.0 collective-permute-done.8.refs_7_
  33.6 0.9 %scores.2 = (bf16[2,256,1024]{2,1,0:T(8,128)(2,1)S(1)}, f32[256,256]{1,0:T(8,128)S(1)}, f32[256,256]{1,0:T(8,128)S(1)}) custom-call(bf16[256,640]{1,0:T(8,128)(2,1)S(1)} %get-tuple-element.29.query_ref, bf16[256,640]{1,0:T(8,128)(2,1)S(1)} %get-tuple-element.30.refs_0_, bf16[256,640]{1,0:T(8,128)(2,1)S(1)} %collective-permute-done.1.refs_1_, ...), custom_call_target="tpu_custom_call" | custom-call | flops 301989888 | bytes 1703936 | tf_op jit(solution)/shard_map/scores/pallas_call | solution.py:207
  34.4 0.2 half.2.half_ref
  34.7 0.0 collective-permute-done.11.first_ref
  34.7 0.2 gather.2
  34.9 3.4 %collective-permute-start.13 = (bf16[256,256]{1,0:T(8,128)(2,1)S(1)}, bf16[256,256]{1,0:T(8,128)(2,1)S(1)}, u32[]{:S(2)}, u32[]{:S(2)}) collective-permute-start(bf16[256,256]{1,0:T(8,128)(2,1)S(1)} %gather.2), channel_id=1, source_target_pairs={{0,12},{4,0},{8,4},{12,8},{1,13},{5,1},{9,5},{13,9},{2,14},{6,2},{... | collective-permute-start | bytes 393224 | tf_op jit(solution)/shard_map/ppermute | solution.py:357
  38.4 2.0 %collective-permute-done.19.part_ref = bf16[256,384]{1,0:T(8,128)(2,1)S(1)} collective-permute-done((bf16[256,384]{1,0:T(8,128)(2,1)S(1)}, bf16[256,384]{1,0:T(8,128)(2,1)S(1)}, u32[]{:S(2)}, u32[]{:S(2)}) %collective-permute-start.19) | collective-permute-done | bytes 196640 | tf_op jit(solution)/shard_map/ppermute | solution.py:357
  40.4 0.7 %put.2.refs_0_ = bf16[256,640]{1,0:T(8,128)(2,1)} custom-call(bf16[256,384]{1,0:T(8,128)(2,1)S(1)} %collective-permute-done.19.part_ref), custom_call_target="tpu_custom_call" | custom-call | tf_op jit(solution)/shard_map/put/pallas_call | solution.py:305
  41.1 1.9 %collective-permute-done.13.part_ref = bf16[256,256]{1,0:T(8,128)(2,1)S(1)} collective-permute-done((bf16[256,256]{1,0:T(8,128)(2,1)S(1)}, bf16[256,256]{1,0:T(8,128)(2,1)S(1)}, u32[]{:S(2)}, u32[]{:S(2)}) %collective-permute-start.13) | collective-permute-done | bytes 131104 | tf_op jit(solution)/shard_map/ppermute | solution.py:357
  42.9 0.7 %put.3 = bf16[256,640]{1,0:T(8,128)(2,1)} custom-call(bf16[256,256]{1,0:T(8,128)(2,1)S(1)} %collective-permute-done.13.part_ref, bf16[256,640]{1,0:T(8,128)(2,1)} %put.2.refs_0_), custom_call_target="tpu_custom_call", output_to_operand_aliasing={{}: (1, {})} | custom-call | tf_op jit(solution)/shard_map/put/pallas_call | solution.py:305
  (5 shorter events, 0.0 us)
Async XLA Ops:
  1.4 9.7 %collective-permute-start = (f32[2,256]{1,0:T(2,128)S(1)}, f32[2,256]{1,0:T(2,128)S(1)}, u32[]{:S(2)}, u32[]{:S(2)}) collective-permute-start(f32[2,256]{1,0:T(2,128)S(1)} %get-tuple-element.26.own_ref), channel_id=1, source_target_pairs={{0,2},{2,0},{1,3},{3,1},{4,6},{6,4},{5,7},{7,5},{8,10},{10,8},{9,1... | collective-permute-start | bytes 6152 | tf_op jit(solution)/shard_map/ppermute | solution.py:339
  4.4 14.3 %collective-permute-start.2 = (bf16[256,640]{1,0:T(8,128)(2,1)}, bf16[256,640]{1,0:T(8,128)(2,1)S(1)}, u32[]{:S(2)}, u32[]{:S(2)}) collective-permute-start(bf16[256,640]{1,0:T(8,128)(2,1)} %bitcast.7), channel_id=1, source_target_pairs={{0,4},{4,0},{8,12},{12,8},{1,5},{5,1},{9,13},{13,9},{2,6},{6,2},{1... | collective-permute-start | bytes 983048 | tf_op jit(solution)/shard_map/ppermute | solution.py:330
  6.0 17.8 %collective-permute-start.3 = (bf16[256,640]{1,0:T(8,128)(2,1)}, bf16[256,640]{1,0:T(8,128)(2,1)S(1)}, u32[]{:S(2)}, u32[]{:S(2)}) collective-permute-start(bf16[256,640]{1,0:T(8,128)(2,1)} %bitcast.8), channel_id=1, source_target_pairs={{0,1},{1,0},{4,8},{5,9},{8,4},{9,5},{12,13},{13,12},{2,3},{3,2},{6... | collective-permute-start | bytes 983048 | tf_op jit(solution)/shard_map/ppermute | solution.py:331
  7.8 10.4 %collective-permute-start.9 = (bf16[256,256]{1,0:T(8,128)(2,1)S(1)}, bf16[256,256]{1,0:T(8,128)(2,1)S(1)}, u32[]{:S(2)}, u32[]{:S(2)}) collective-permute-start(bf16[256,256]{1,0:T(8,128)(2,1)S(1)} %get-tuple-element.33.refs_6_), channel_id=1, source_target_pairs={{0,4},{4,0},{8,12},{12,8},{1,5},{5,1},{9,13},{13,9},{2,6},{6,2},{1... | collective-permute-start | bytes 393224 | tf_op jit(solution)/shard_map/ppermute | solution.py:330
  11.0 13.6 %collective-permute-start.14 = (bf16[256,384]{1,0:T(8,128)(2,1)S(1)}, bf16[256,384]{1,0:T(8,128)(2,1)S(1)}, u32[]{:S(2)}, u32[]{:S(2)}) collective-permute-start(bf16[256,384]{1,0:T(8,128)(2,1)S(1)} %get-tuple-element.37.refs_6_), channel_id=1, source_target_pairs={{0,1},{1,0},{2,3},{3,2},{4,5},{5,4},{6,7},{7,6},{8,9},{9,8},{10,11... | collective-permute-start | bytes 589832 | tf_op jit(solution)/shard_map/ppermute | solution.py:332
  11.1 5.6 %collective-permute-start.4 = (f32[1,256]{1,0:T(1,128)S(1)}, f32[1,256]{1,0:T(1,128)S(1)}, u32[]{:S(2)}, u32[]{:S(2)}) collective-permute-start(f32[1,256]{1,0:T(1,128)S(1)} %slice_add_fusion), channel_id=1, source_target_pairs={{0,4},{4,0},{8,12},{12,8},{1,5},{5,1},{9,13},{13,9},{2,6},{6,2},{1... | collective-permute-start | bytes 3080 | tf_op jit(solution)/shard_map/ppermute | solution.py:330
  16.7 1.2 %collective-permute-start.5 = (f32[1,256]{1,0:T(1,128)S(1)}, f32[1,256]{1,0:T(1,128)S(1)}, u32[]{:S(2)}, u32[]{:S(2)}) collective-permute-start(f32[1,256]{1,0:T(1,128)S(1)} %slice_add_fusion), channel_id=1, source_target_pairs={{0,1},{1,0},{4,8},{5,9},{8,4},{9,5},{12,13},{13,12},{2,3},{3,2},{6... | collective-permute-start | bytes 3080 | tf_op jit(solution)/shard_map/ppermute | solution.py:331
  17.8 6.4 %collective-permute-start.10 = (bf16[256,256]{1,0:T(8,128)(2,1)S(1)}, bf16[256,256]{1,0:T(8,128)(2,1)S(1)}, u32[]{:S(2)}, u32[]{:S(2)}) collective-permute-start(bf16[256,256]{1,0:T(8,128)(2,1)S(1)} %get-tuple-element.33.refs_6_), channel_id=1, source_target_pairs={{0,1},{1,0},{4,8},{5,9},{8,4},{9,5},{12,13},{13,12},{2,3},{3,2},{6... | collective-permute-start | bytes 393224 | tf_op jit(solution)/shard_map/ppermute | solution.py:331
  18.3 11.6 %collective-permute-start.1 = (bf16[256,640]{1,0:T(8,128)(2,1)S(1)}, bf16[256,640]{1,0:T(8,128)(2,1)S(1)}, u32[]{:S(2)}, u32[]{:S(2)}) collective-permute-start(bf16[256,640]{1,0:T(8,128)(2,1)S(1)} %get-tuple-element.30.refs_0_), channel_id=1, source_target_pairs={{0,1},{1,0},{2,3},{3,2},{4,5},{5,4},{6,7},{7,6},{8,9},{9,8},{10,11... | collective-permute-start | bytes 983048 | tf_op jit(solution)/shard_map/ppermute | solution.py:332
  18.7 10.6 %collective-permute-start.15 = (bf16[256,384]{1,0:T(8,128)(2,1)S(1)}, bf16[256,384]{1,0:T(8,128)(2,1)S(1)}, u32[]{:S(2)}, u32[]{:S(2)}) collective-permute-start(bf16[256,384]{1,0:T(8,128)(2,1)S(1)} %get-tuple-element.37.refs_6_), channel_id=1, source_target_pairs={{0,4},{4,0},{8,12},{12,8},{1,5},{5,1},{9,13},{13,9},{2,6},{6,2},{1... | collective-permute-start | bytes 589832 | tf_op jit(solution)/shard_map/ppermute | solution.py:330
  23.8 5.5 %collective-permute-start.16 = (bf16[256,384]{1,0:T(8,128)(2,1)S(1)}, bf16[256,384]{1,0:T(8,128)(2,1)S(1)}, u32[]{:S(2)}, u32[]{:S(2)}) collective-permute-start(bf16[256,384]{1,0:T(8,128)(2,1)S(1)} %get-tuple-element.37.refs_6_), channel_id=1, source_target_pairs={{0,1},{1,0},{4,8},{5,9},{8,4},{9,5},{12,13},{13,12},{2,3},{3,2},{6... | collective-permute-start | bytes 589832 | tf_op jit(solution)/shard_map/ppermute | solution.py:331
  24.2 5.7 %collective-permute-start.6 = (bf16[256,640]{1,0:T(8,128)(2,1)S(1)}, bf16[256,640]{1,0:T(8,128)(2,1)S(1)}, u32[]{:S(2)}, u32[]{:S(2)}) collective-permute-start(bf16[256,640]{1,0:T(8,128)(2,1)S(1)} %get-tuple-element.31.refs_2_), channel_id=1, source_target_pairs={{0,1},{1,0},{2,3},{3,2},{4,5},{5,4},{6,7},{7,6},{8,9},{9,8},{10,11... | collective-permute-start | bytes 983048 | tf_op jit(solution)/shard_map/ppermute | solution.py:332
  24.7 5.7 %collective-permute-start.7 = (bf16[256,640]{1,0:T(8,128)(2,1)S(1)}, bf16[256,640]{1,0:T(8,128)(2,1)S(1)}, u32[]{:S(2)}, u32[]{:S(2)}) collective-permute-start(bf16[256,640]{1,0:T(8,128)(2,1)S(1)} %get-tuple-element.32.refs_4_), channel_id=1, source_target_pairs={{0,1},{1,0},{2,3},{3,2},{4,5},{5,4},{6,7},{7,6},{8,9},{9,8},{10,11... | collective-permute-start | bytes 983048 | tf_op jit(solution)/shard_map/ppermute | solution.py:332
  29.3 2.5 %collective-permute-start.17 = (bf16[256,384]{1,0:T(8,128)(2,1)S(1)}, bf16[256,384]{1,0:T(8,128)(2,1)S(1)}, u32[]{:S(2)}, u32[]{:S(2)}) collective-permute-start(bf16[256,384]{1,0:T(8,128)(2,1)S(1)} %collective-permute-done.15.first_ref), channel_id=1, source_target_pairs={{0,1},{1,0},{2,3},{3,2},{4,5},{5,4},{6,7},{7,6},{8,9},{9,8},{10,11... | collective-permute-start | bytes 589832 | tf_op jit(solution)/shard_map/ppermute | solution.py:332
  29.3 2.5 %collective-permute-start.18 = (bf16[256,384]{1,0:T(8,128)(2,1)S(1)}, bf16[256,384]{1,0:T(8,128)(2,1)S(1)}, u32[]{:S(2)}, u32[]{:S(2)}) collective-permute-start(bf16[256,384]{1,0:T(8,128)(2,1)S(1)} %collective-permute-done.16.second_ref), channel_id=1, source_target_pairs={{0,1},{1,0},{2,3},{3,2},{4,5},{5,4},{6,7},{7,6},{8,9},{9,8},{10,11... | collective-permute-start | bytes 589832 | tf_op jit(solution)/shard_map/ppermute | solution.py:332
  29.8 3.7 %collective-permute-start.8 = (bf16[256,256]{1,0:T(8,128)(2,1)S(1)}, bf16[256,256]{1,0:T(8,128)(2,1)S(1)}, u32[]{:S(2)}, u32[]{:S(2)}) collective-permute-start(bf16[256,256]{1,0:T(8,128)(2,1)S(1)} %get-tuple-element.33.refs_6_), channel_id=1, source_target_pairs={{0,1},{1,0},{2,3},{3,2},{4,5},{5,4},{6,7},{7,6},{8,9},{9,8},{10,11... | collective-permute-start | bytes 393224 | tf_op jit(solution)/shard_map/ppermute | solution.py:332
  29.9 4.8 %collective-permute-start.11 = (bf16[256,256]{1,0:T(8,128)(2,1)S(1)}, bf16[256,256]{1,0:T(8,128)(2,1)S(1)}, u32[]{:S(2)}, u32[]{:S(2)}) collective-permute-start(bf16[256,256]{1,0:T(8,128)(2,1)S(1)} %collective-permute-done.9.first_ref), channel_id=1, source_target_pairs={{0,1},{1,0},{2,3},{3,2},{4,5},{5,4},{6,7},{7,6},{8,9},{9,8},{10,11... | collective-permute-start | bytes 393224 | tf_op jit(solution)/shard_map/ppermute | solution.py:332
  30.3 4.3 %collective-permute-start.12 = (bf16[256,256]{1,0:T(8,128)(2,1)S(1)}, bf16[256,256]{1,0:T(8,128)(2,1)S(1)}, u32[]{:S(2)}, u32[]{:S(2)}) collective-permute-start(bf16[256,256]{1,0:T(8,128)(2,1)S(1)} %collective-permute-done.10.second_ref), channel_id=1, source_target_pairs={{0,1},{1,0},{2,3},{3,2},{4,5},{5,4},{6,7},{7,6},{8,9},{9,8},{10,11... | collective-permute-start | bytes 393224 | tf_op jit(solution)/shard_map/ppermute | solution.py:332
  32.2 8.2 %collective-permute-start.19 = (bf16[256,384]{1,0:T(8,128)(2,1)S(1)}, bf16[256,384]{1,0:T(8,128)(2,1)S(1)}, u32[]{:S(2)}, u32[]{:S(2)}) collective-permute-start(bf16[256,384]{1,0:T(8,128)(2,1)S(1)} %gather.3), channel_id=1, source_target_pairs={{0,12},{4,0},{8,4},{12,8},{1,13},{5,1},{9,5},{13,9},{2,14},{6,2},{... | collective-permute-start | bytes 589832 | tf_op jit(solution)/shard_map/ppermute | solution.py:357
  34.9 8.0 %collective-permute-start.13 = (bf16[256,256]{1,0:T(8,128)(2,1)S(1)}, bf16[256,256]{1,0:T(8,128)(2,1)S(1)}, u32[]{:S(2)}, u32[]{:S(2)}) collective-permute-start(bf16[256,256]{1,0:T(8,128)(2,1)S(1)} %gather.2), channel_id=1, source_target_pairs={{0,12},{4,0},{8,4},{12,8},{1,13},{5,1},{9,5},{13,9},{2,14},{6,2},{... | collective-permute-start | bytes 393224 | tf_op jit(solution)/shard_map/ppermute | solution.py:357
